TPU v7x, 512 devices: a whole 4x4x16 slice. The times are simulated.
512 devices in a mesh: req: 64 (over z, y), head: 8 (over x, core).
Axes of the slice: x: 4, y: 4, z: 16, core: 2. Of those that a mesh axis runs over, the one named last changes fastest.
Arguments:
- inner_input: bfloat16 [16384, 16384], P('req', 'head'), may hold values from -6 to 6
- projection_input: bfloat16 [16384, 8, 2, 128], P('req', 'head'), may hold values from -6 to 6
- step_before_bias: bfloat16 [16384, 256], P('req', 'head'), may hold values from -2 to 11
- inner_conv_taps: float32 [4, 16384], P(None, 'head'), may hold values from -3 to 3
- projection_conv_taps: float32 [4, 8, 2, 128], P(None, 'head'), may hold values from -3 to 3
- step_bias: float32 [256], P('head'), may hold values from -4.5 to -3.5
- head_decay_rate: float32 [256], P('head'), may hold values from 0.1 to 3
- head_skip_gain: float32 [256], P('head'), may hold values from 0.5 to 1.5
- group_norm_gain: float32 [16384], P('head'), may hold values from 0.5 to 1.5
- tenant: int32 [64], P('req'), may hold values from 0 to 63
- tenant_adapter_row: int32 [64], replicated, may hold values from 0 to 63, each once
- cache_holder_index: int32 [64], P('req'), may hold values from 0 to 63, as said below
- cache_slot_index: int32 [64], P('req'), may hold values from 0 to 1
- adapter_down_panels: bfloat16 [64, 16384, 64], P('req', 'head'), may hold values from -0.046875 to 0.046875
- adapter_up_panels: bfloat16 [64, 64, 8192], P('req', None, 'head'), may hold values from -0.75 to 0.75
- cached_ssm_states: bfloat16 [128, 256, 64, 128], P('req', 'head'), may hold values from -2.5 to 2.5
- inner_conv_cache: bfloat16 [128, 3, 16384], P('req', None, 'head'), may hold values from -6 to 6
- projection_conv_cache: bfloat16 [128, 3, 8, 2, 128], P('req', None, 'head'), may hold values from -6 to 6
Outputs:
- normed_output: bfloat16 [16384, 16384], P('req', 'head')
- adapter_output_term: bfloat16 [16384, 8192], P('req', 'head')
- updated_state: bfloat16 [64, 256, 64, 128], P('req', 'head')
Inputs may be any that keep to these rules, and one draw needn't show every extreme that they name: `tenant_adapter_row`: every row of the adapter tables belongs to exactly one tenant. `cache_holder_index`: no two requests share a cache slot, and each index of req holds the cached states of exactly 1 request.
All inputs are finite; a program needn't handle non-finite values.
Results may differ from a plain program's by a relative error of at most 0.013.
Values may be sent and summed in bfloat16 or wider, within the bound.
No kernel may reach another device: no remote copies, remote signals or barrier semaphores. Data moves between devices by JAX's collectives and lax.ppermute only.
A program may use at most 64 MiB of HBM per device.

v0:
```python
import jax
import jax.numpy as jnp
from jax import lax
from jax.sharding import PartitionSpec as P

ADAPTER_SCALE = 2.0
NORM_EPSILON = 1e-05


def causal_conv(cached, current, weight):
    joined = jnp.concatenate([cached, current], axis=1)
    length_value = current.shape[1]
    summed = weight[0] * joined[:, 0:length_value]
    for tap in range(1, weight.shape[0]):
        summed = summed + weight[tap] * joined[:, tap : tap + length_value]
    return jax.nn.silu(summed).astype(jnp.bfloat16)


def per_device(
    inner_input,
    projection_input,
    step_before_bias,
    inner_conv_taps,
    projection_conv_taps,
    step_bias,
    head_decay_rate,
    head_skip_gain,
    group_norm_gain,
    tenant,
    tenant_adapter_row,
    cache_holder_index,
    cache_slot_index,
    adapter_down_panels,
    adapter_up_panels,
    cached_ssm_states,
    inner_conv_cache,
    projection_conv_cache,
):
    per_device_share = tenant.shape[0]
    slots_dev = cached_ssm_states.shape[0]
    hidden_features_on_card = inner_input.shape[1]
    heads_dev = step_before_bias.shape[1]
    groups_dev = projection_input.shape[1]
    state_size = projection_input.shape[3]
    head_size = hidden_features_on_card // heads_dev
    per_group = heads_dev // groups_dev
    reduced_width = adapter_down_panels.shape[2]
    model_per_device = adapter_up_panels.shape[2]
    tap_count = inner_conv_taps.shape[0]
    length_value = inner_input.shape[0] // per_device_share
    tenant_all, owner_all, slot_all = (
        lax.all_gather(tenant, "req", axis=0, tiled=True),
        lax.all_gather(cache_holder_index, "req", axis=0, tiled=True),
        lax.all_gather(cache_slot_index, "req", axis=0, tiled=True),
    )
    customer_identifiers = jnp.arange(tenant_adapter_row.shape[0], dtype=jnp.int32)
    picked_customer_matrix_pair = jnp.sum(
        jnp.where(
            tenant_all[:, None] == customer_identifiers[None, :], tenant_adapter_row[None, :], 0
        ),
        axis=1,
    )
    ssm_flat = cached_ssm_states.reshape(slots_dev, -1)
    convx_flat = inner_conv_cache.reshape(slots_dev, -1)
    convbc_flat = projection_conv_cache.reshape(slots_dev, -1)
    cache_pick = owner_all * slots_dev + slot_all
    dispersion_factor = (
        lax.all_to_all(
            adapter_down_panels.reshape(adapter_down_panels.shape[0], -1),
            "req",
            split_axis=1,
            concat_axis=0,
            tiled=True,
        ),
        lax.all_to_all(
            adapter_up_panels.reshape(adapter_up_panels.shape[0], -1),
            "req",
            split_axis=1,
            concat_axis=0,
            tiled=True,
        ),
        lax.all_to_all(ssm_flat, "req", split_axis=1, concat_axis=0, tiled=True),
        lax.all_to_all(convx_flat, "req", split_axis=1, concat_axis=0, tiled=True),
        lax.all_to_all(convbc_flat, "req", split_axis=1, concat_axis=0, tiled=True),
    )
    picked_left_factor = jnp.take(dispersion_factor[0], picked_customer_matrix_pair, axis=0)
    picked_right_factor = jnp.take(dispersion_factor[1], picked_customer_matrix_pair, axis=0)
    chosen_state = jnp.take(dispersion_factor[2], cache_pick, axis=0)
    chosen_convx = jnp.take(dispersion_factor[3], cache_pick, axis=0)
    chosen_convbc = jnp.take(dispersion_factor[4], cache_pick, axis=0)
    fetched = (
        lax.all_to_all(picked_left_factor, "req", split_axis=0, concat_axis=1, tiled=True),
        lax.all_to_all(picked_right_factor, "req", split_axis=0, concat_axis=1, tiled=True),
        lax.all_to_all(chosen_state, "req", split_axis=0, concat_axis=1, tiled=True),
        lax.all_to_all(chosen_convx, "req", split_axis=0, concat_axis=1, tiled=True),
        lax.all_to_all(chosen_convbc, "req", split_axis=0, concat_axis=1, tiled=True),
    )
    down_panel = fetched[0].reshape(per_device_share, hidden_features_on_card, reduced_width)
    up_panel = fetched[1].reshape(per_device_share, reduced_width, model_per_device)
    cached_state = fetched[2].reshape(
        per_device_share, groups_dev, per_group, head_size, state_size
    )
    cached_x = fetched[3].reshape(per_device_share, tap_count - 1, hidden_features_on_card)
    cached_bc = fetched[4].reshape(per_device_share, tap_count - 1, groups_dev, 2, state_size)
    conv_x = causal_conv(
        cached_x,
        inner_input.reshape(per_device_share, length_value, hidden_features_on_card),
        inner_conv_taps,
    )
    conv_bc = causal_conv(
        cached_bc,
        projection_input.reshape(per_device_share, length_value, groups_dev, 2, state_size),
        projection_conv_taps,
    )
    b_proj = conv_bc[:, :, :, 0]
    c_proj = conv_bc[:, :, :, 1]
    step_size = jax.nn.softplus(step_before_bias.astype(jnp.float32) + step_bias).reshape(
        per_device_share, length_value, heads_dev
    )
    log_decay = jnp.cumsum(-head_decay_rate * step_size, axis=1)
    log_decay5 = log_decay.reshape(per_device_share, length_value, groups_dev, per_group)
    step_size5 = step_size.reshape(per_device_share, length_value, groups_dev, per_group)
    score_bc = jnp.einsum("rtgn,rsgn->rgts", c_proj, b_proj, preferred_element_type=jnp.float32)
    decay_rows = jnp.transpose(log_decay5, (0, 2, 3, 1))
    log_gap = decay_rows[..., :, None] - decay_rows[..., None, :]
    token_ids = jnp.arange(length_value, dtype=jnp.int32)
    causal = token_ids[:, None] >= token_ids[None, :]
    decay_factor = jnp.exp(jnp.where(causal, log_gap, -jnp.inf))
    step_rows = jnp.transpose(step_size5, (0, 2, 3, 1))
    mix_weights = (score_bc[:, :, None] * decay_factor * step_rows[..., None, :]).astype(
        jnp.bfloat16
    )
    conv_heads = conv_x.reshape(per_device_share, length_value, groups_dev, per_group, head_size)
    intra = jnp.einsum(
        "rghts,rsghp->rtghp", mix_weights, conv_heads, preferred_element_type=jnp.float32
    )
    inter = (
        jnp.einsum("rtgn,rghpn->rtghp", c_proj, cached_state, preferred_element_type=jnp.float32)
        * jnp.exp(log_decay5)[..., None]
    )
    skip_gain = head_skip_gain.reshape(groups_dev, per_group)[..., None]
    mixed = intra + inter + skip_gain * conv_heads
    mean_square = jnp.mean(mixed * mixed, axis=(3, 4), keepdims=True)
    normed_output = (
        (mixed * lax.rsqrt(mean_square + NORM_EPSILON)).reshape(
            per_device_share, length_value, hidden_features_on_card
        )
        * group_norm_gain
    ).astype(jnp.bfloat16)
    low_partial = jnp.einsum(
        "rtc,rcq->rtq", normed_output, down_panel, preferred_element_type=jnp.float32
    )
    reduced_rank = lax.psum(low_partial, "head").astype(jnp.bfloat16)
    adapter_output_term = (
        jnp.einsum("rtq,rqd->rtd", reduced_rank, up_panel, preferred_element_type=jnp.float32)
        * ADAPTER_SCALE
    ).astype(jnp.bfloat16)
    log_total = log_decay[:, -1:, :]
    carry_weight = (jnp.exp(log_total - log_decay) * step_size).reshape(
        per_device_share, length_value, groups_dev, per_group
    )
    carried = (conv_heads * carry_weight[..., None]).astype(jnp.bfloat16)
    fresh_state = jnp.einsum(
        "rsghp,rsgn->rghpn", carried, b_proj, preferred_element_type=jnp.float32
    )
    keep_factor = jnp.exp(log_total[:, 0]).reshape(per_device_share, groups_dev, per_group)[
        ..., None, None
    ]
    updated_state = fresh_state + keep_factor * cached_state
    return (
        normed_output.reshape(per_device_share * length_value, hidden_features_on_card),
        adapter_output_term.reshape(per_device_share * length_value, model_per_device),
        updated_state.reshape(per_device_share, heads_dev, head_size, state_size).astype(
            jnp.bfloat16
        ),
    )


def solution(mesh):
    return jax.shard_map(
        per_device,
        mesh=mesh,
        in_specs=(
            P("req", "head"),
            P("req", "head", None, None),
            P("req", "head"),
            P(None, "head"),
            P(None, "head", None, None),
            P("head"),
            P("head"),
            P("head"),
            P("head"),
            P("req"),
            P(),
            P("req"),
            P("req"),
            P("req", "head", None),
            P("req", None, "head"),
            P("req", "head", None, None),
            P("req", None, "head"),
            P("req", None, "head", None, None),
        ),
        out_specs=(P("req", "head"), P("req", "head"), P("req", "head", None, None)),
        check_vma=False,
    )
```

profile of v0, /device:TPU:1, one launch (start us, length us, event | category | flops | bytes accessed | tf_op | source)
XLA Modules:
  0.0 329.1 jit_solution(10483867477987839845)
XLA Ops:
  2.1 19.3 %all-to-all-start.2 = ((bf16[2,64,12]{2,0,1:T(2,128)(2,1)}), bf16[2,64,12]{2,0,1:T(2,128)(2,1)S(1)}, u32[]{:S(2)}, u32[]{:S(2)}) async-start(bf16[2,64,12]{2,0,1:T(2,128)(2,1)} %copy.93), calls=%async_computation.2 | async-start | bytes 65536 | tf_op jit(solution)/shard_map/all_to_all | solution.py:84
  23.3 1.3 dynamic-slice
  26.9 22.4 %all-reduce.3 = (s32[64]{0:T(128)S(1)}, s32[64]{0:T(128)S(1)}, s32[64]{0:T(128)S(1)}) all-reduce(s32[64]{0:T(128)S(1)} %dynamic-update-slice.1, s32[64]{0:T(128)S(1)} %dynamic-update-slice, s32[64]{0:T(128)S(1)} %dynamic-update-slice.2), channel_id=1, replica_groups=mesh['req'=64,'head'=8] {'req'}, use_global_device_ids=true, to_apply=%add.1 | all-reduce | flops 192 | bytes 1536
  53.3 1.4 reduce.10
  55.5 10.2 %all-to-all-start = ((bf16[2,64,96]{2,0,1:T(2,128)(2,1)}), bf16[2,64,96]{2,0,1:T(2,128)(2,1)S(1)}, u32[]{:S(2)}, u32[]{:S(2)}) async-start(bf16[2,64,96]{2,0,1:T(2,128)(2,1)} %copy.88), calls=%async_computation | async-start | bytes 65536 | tf_op jit(solution)/shard_map/all_to_all | solution.py:83
  65.7 13.4 %all-to-all-done = bf16[2,64,96]{2,0,1:T(2,128)(2,1)S(1)} async-done(((bf16[2,64,96]{2,0,1:T(2,128)(2,1)}), bf16[2,64,96]{2,0,1:T(2,128)(2,1)S(1)}, u32[]{:S(2)}, u32[]{:S(2)}) %all-to-all-start) | async-done | bytes 24608 | tf_op jit(solution)/shard_map/all_to_all | solution.py:83
  79.1 4.6 %all-to-all-start.8 = ((bf16[64,2,512]{2,1,0:T(2,128)(2,1)}), bf16[64,2,512]{2,1,0:T(2,128)(2,1)S(1)}, u32[]{:S(2)}, u32[]{:S(2)}) async-start(bf16[64,2,512]{2,1,0:T(2,128)(2,1)} %reshape.580), calls=%async_computation.8 | async-start | bytes 262144 | tf_op jit(solution)/shard_map/all_to_all | solution.py:75
  85.7 13.1 %all-to-all-done.8 = bf16[64,2,512]{2,1,0:T(2,128)(2,1)S(1)} async-done(((bf16[64,2,512]{2,1,0:T(2,128)(2,1)}), bf16[64,2,512]{2,1,0:T(2,128)(2,1)S(1)}, u32[]{:S(2)}, u32[]{:S(2)}) %all-to-all-start.8) | async-done | bytes 131104 | tf_op jit(solution)/shard_map/all_to_all | solution.py:75
  98.9 4.6 %all-to-all-start.3 = ((bf16[64,1,12]{2,1,0:T(2,128)(2,1)}), bf16[64,1,12]{2,1,0:T(2,128)(2,1)S(1)}, u32[]{:S(2)}, u32[]{:S(2)}) async-start(bf16[64,1,12]{2,1,0:T(2,128)(2,1)} %copy.94), calls=%async_computation.3 | async-start | bytes 65536 | tf_op jit(solution)/shard_map/all_to_all | solution.py:96
  105.0 11.9 %all-to-all-done.3 = bf16[64,1,12]{2,1,0:T(2,128)(2,1)S(1)} async-done(((bf16[64,1,12]{2,1,0:T(2,128)(2,1)}), bf16[64,1,12]{2,1,0:T(2,128)(2,1)S(1)}, u32[]{:S(2)}, u32[]{:S(2)}) %all-to-all-start.3) | async-done | bytes 1568 | tf_op jit(solution)/shard_map/all_to_all | solution.py:96
  116.9 4.6 %all-to-all-start.1 = ((bf16[64,1,96]{2,1,0:T(2,128)(2,1)}), bf16[64,1,96]{2,1,0:T(2,128)(2,1)S(1)}, u32[]{:S(2)}, u32[]{:S(2)}) async-start(bf16[64,1,96]{2,1,0:T(2,128)(2,1)} %copy.89), calls=%async_computation.1 | async-start | bytes 65536 | tf_op jit(solution)/shard_map/all_to_all | solution.py:95
  123.1 11.9 %all-to-all-done.1 = bf16[64,1,96]{2,1,0:T(2,128)(2,1)S(1)} async-done(((bf16[64,1,96]{2,1,0:T(2,128)(2,1)}), bf16[64,1,96]{2,1,0:T(2,128)(2,1)S(1)}, u32[]{:S(2)}, u32[]{:S(2)}) %all-to-all-start.1) | async-done | bytes 12320 | tf_op jit(solution)/shard_map/all_to_all | solution.py:95
  135.0 4.6 %all-to-all-start.9 = ((bf16[64,2,512]{2,1,0:T(2,128)(2,1)}), bf16[64,2,512]{2,1,0:T(2,128)(2,1)S(1)}, u32[]{:S(2)}, u32[]{:S(2)}) async-start(bf16[64,2,512]{2,1,0:T(2,128)(2,1)} %reshape.582), calls=%async_computation.9 | async-start | bytes 262144 | tf_op jit(solution)/shard_map/all_to_all | solution.py:93
  140.3 2.2 reduce.12
  143.4 11.4 %all-to-all-done.9 = bf16[64,2,512]{2,1,0:T(2,128)(2,1)S(1)} async-done(((bf16[64,2,512]{2,1,0:T(2,128)(2,1)}), bf16[64,2,512]{2,1,0:T(2,128)(2,1)S(1)}, u32[]{:S(2)}, u32[]{:S(2)}) %all-to-all-start.9) | async-done | bytes 131104 | tf_op jit(solution)/shard_map/all_to_all | solution.py:93
  155.5 4.8 %all-to-all-start.6 = ((bf16[64,2,1024]{2,1,0:T(2,128)(2,1)}), bf16[64,2,1024]{2,1,0:T(2,128)(2,1)S(1)}, u32[]{:S(2)}, u32[]{:S(2)}) async-start(bf16[64,2,1024]{2,1,0:T(2,128)(2,1)} %reshape.584), calls=%async_computation.6 | async-start | bytes 524288 | tf_op jit(solution)/shard_map/all_to_all | solution.py:68
  160.8 2.1 copy.100
  162.9 15.0 %all-to-all-done.6 = bf16[64,2,1024]{2,1,0:T(2,128)(2,1)S(1)} async-done(((bf16[64,2,1024]{2,1,0:T(2,128)(2,1)}), bf16[64,2,1024]{2,1,0:T(2,128)(2,1)S(1)}, u32[]{:S(2)}, u32[]{:S(2)}) %all-to-all-start.6) | async-done | bytes 262176 | tf_op jit(solution)/shard_map/all_to_all | solution.py:68
  177.9 4.7 %all-to-all-start.4 = ((bf16[2,64,4096]{2,0,1:T(2,128)(2,1)}), bf16[2,64,4096]{2,0,1:T(2,128)(2,1)S(1)}, u32[]{:S(2)}, u32[]{:S(2)}) async-start(bf16[2,64,4096]{2,0,1:T(2,128)(2,1)} %copy.100), calls=%async_computation.4 | async-start | bytes 2097152 | tf_op jit(solution)/shard_map/all_to_all | solution.py:82
  186.9 35.7 %all-to-all-done.4 = bf16[2,64,4096]{2,0,1:T(2,128)(2,1)S(1)} async-done(((bf16[2,64,4096]{2,0,1:T(2,128)(2,1)}), bf16[2,64,4096]{2,0,1:T(2,128)(2,1)S(1)}, u32[]{:S(2)}, u32[]{:S(2)}) %all-to-all-start.4) | async-done | bytes 1048608 | tf_op jit(solution)/shard_map/all_to_all | solution.py:82
  222.5 13.1 %all-to-all-start.7 = ((bf16[64,2,1024]{2,1,0:T(2,128)(2,1)}), bf16[64,2,1024]{2,1,0:T(2,128)(2,1)S(1)}, u32[]{:S(2)}, u32[]{:S(2)}) async-start(bf16[64,2,1024]{2,1,0:T(2,128)(2,1)} %reshape.586), calls=%async_computation.7 | async-start | bytes 524288 | tf_op jit(solution)/shard_map/all_to_all | solution.py:92
  239.6 13.5 %all-to-all-done.7 = bf16[64,2,1024]{2,1,0:T(2,128)(2,1)S(1)} async-done(((bf16[64,2,1024]{2,1,0:T(2,128)(2,1)}), bf16[64,2,1024]{2,1,0:T(2,128)(2,1)S(1)}, u32[]{:S(2)}, u32[]{:S(2)}) %all-to-all-start.7) | async-done | bytes 262176 | tf_op jit(solution)/shard_map/all_to_all | solution.py:92
  253.1 4.6 %all-to-all-start.5 = ((bf16[64,2,2048]{2,1,0:T(2,128)(2,1)}), bf16[64,2,2048]{2,1,0:T(2,128)(2,1)S(1)}, u32[]{:S(2)}, u32[]{:S(2)}) async-start(bf16[64,2,2048]{2,1,0:T(2,128)(2,1)} %reshape.578), calls=%async_computation.5 | async-start | bytes 1048576 | tf_op jit(solution)/shard_map/all_to_all | solution.py:94
  263.7 3.8 %fusion.9 = (bf16[1,256,2048]{1,2,0:T(8,128)(2,1)}, bf16[1,256,2048]{1,2,0:T(8,128)(2,1)}) fusion(f32[256,32]{0,1:T(8,128)S(1)} %bitcast.165, bf16[256,2048]{0,1:T(8,128)(2,1)S(1)} %copy.90, f32[2048]{0:T(1024)S(1)} %bitcast.169, bf16[1,256,2048]{1,2,0:T(8,128)(2,1)S(1)} %bitcast.147, bf16[1,3,2048]{1,2,0:T(8,128)(2,1)S(1)} %copy.91, f32[2048]{0:T(1024)S(1)} %bitcast.170, ...), kind=kLoop, calls=%fused_computation.17 | loop fusion | flops 14680064 | bytes 4272128 | tf_op jit(solution)/shard_map/convert_element_type | solution.py:162
  267.8 1.5 reduce.5
  269.9 9.7 %all-to-all-done.5 = bf16[64,2,2048]{2,1,0:T(2,128)(2,1)S(1)} async-done(((bf16[64,2,2048]{2,1,0:T(2,128)(2,1)}), bf16[64,2,2048]{2,1,0:T(2,128)(2,1)S(1)}, u32[]{:S(2)}, u32[]{:S(2)}) %all-to-all-start.5) | async-done | bytes 524320 | tf_op jit(solution)/shard_map/all_to_all | solution.py:94
  280.1 3.1 reduce.4
  284.5 2.6 multiply_reduce_fusion
  288.5 33.5 %psum.7 = bf16[1,256,64]{1,2,0:T(8,128)(2,1)S(1)} all-reduce(f32[1,256,64]{1,2,0:T(8,128)} %convolution_bitcast_fusion), channel_id=1, replica_groups=mesh['req'=64,'head'=8] {'head'}, use_global_device_ids=true, to_apply=%region_4.5 | all-reduce | flops 16384 | bytes 98304 | tf_op jit(solution)/shard_map/psum | solution.py:153
  322.0 1.9 copy.102
  323.9 2.8 multiply_convert_fusion.3
  326.7 1.2 fusion.12
  (134 shorter events, 35.3 us)
Async XLA Ops:
  2.1 53.4 %all-to-all-start.2 = ((bf16[2,64,12]{2,0,1:T(2,128)(2,1)}), bf16[2,64,12]{2,0,1:T(2,128)(2,1)S(1)}, u32[]{:S(2)}, u32[]{:S(2)}) async-start(bf16[2,64,12]{2,0,1:T(2,128)(2,1)} %copy.93), calls=%async_computation.2 | async-start | bytes 65536 | tf_op jit(solution)/shard_map/all_to_all | solution.py:84
  54.7 85.0 %copy-start.6 = (bf16[1,2048,64]{1,2,0:T(8,128)(2,1)S(1)}, bf16[1,2048,64]{1,2,0:T(8,128)(2,1)}, u32[]{:S(2)}) copy-start(bf16[1,2048,64]{1,2,0:T(8,128)(2,1)} %param.31) | copy-start | bytes 786436
  55.5 23.6 %all-to-all-start = ((bf16[2,64,96]{2,0,1:T(2,128)(2,1)}), bf16[2,64,96]{2,0,1:T(2,128)(2,1)S(1)}, u32[]{:S(2)}, u32[]{:S(2)}) async-start(bf16[2,64,96]{2,0,1:T(2,128)(2,1)} %copy.88), calls=%async_computation | async-start | bytes 65536 | tf_op jit(solution)/shard_map/all_to_all | solution.py:83
  79.1 19.8 %all-to-all-start.8 = ((bf16[64,2,512]{2,1,0:T(2,128)(2,1)}), bf16[64,2,512]{2,1,0:T(2,128)(2,1)S(1)}, u32[]{:S(2)}, u32[]{:S(2)}) async-start(bf16[64,2,512]{2,1,0:T(2,128)(2,1)} %reshape.580), calls=%async_computation.8 | async-start | bytes 262144 | tf_op jit(solution)/shard_map/all_to_all | solution.py:75
  98.9 18.1 %all-to-all-start.3 = ((bf16[64,1,12]{2,1,0:T(2,128)(2,1)}), bf16[64,1,12]{2,1,0:T(2,128)(2,1)S(1)}, u32[]{:S(2)}, u32[]{:S(2)}) async-start(bf16[64,1,12]{2,1,0:T(2,128)(2,1)} %copy.94), calls=%async_computation.3 | async-start | bytes 65536 | tf_op jit(solution)/shard_map/all_to_all | solution.py:96
  116.9 18.1 %all-to-all-start.1 = ((bf16[64,1,96]{2,1,0:T(2,128)(2,1)}), bf16[64,1,96]{2,1,0:T(2,128)(2,1)S(1)}, u32[]{:S(2)}, u32[]{:S(2)}) async-start(bf16[64,1,96]{2,1,0:T(2,128)(2,1)} %copy.89), calls=%async_computation.1 | async-start | bytes 65536 | tf_op jit(solution)/shard_map/all_to_all | solution.py:95
  122.4 37.9 %copy-start.1 = (bf16[2,32,64,128]{3,2,1,0:T(8,128)(2,1)S(1)}, bf16[2,32,64,128]{3,2,1,0:T(8,128)(2,1)}, u32[]{:S(2)}) copy-start(bf16[2,32,64,128]{3,2,1,0:T(8,128)(2,1)} %param.33) | copy-start | bytes 3145732
  135.0 19.8 %all-to-all-start.9 = ((bf16[64,2,512]{2,1,0:T(2,128)(2,1)}), bf16[64,2,512]{2,1,0:T(2,128)(2,1)S(1)}, u32[]{:S(2)}, u32[]{:S(2)}) async-start(bf16[64,2,512]{2,1,0:T(2,128)(2,1)} %reshape.582), calls=%async_computation.9 | async-start | bytes 262144 | tf_op jit(solution)/shard_map/all_to_all | solution.py:93
  154.8 0.7 copy-start.4
  155.5 22.5 %all-to-all-start.6 = ((bf16[64,2,1024]{2,1,0:T(2,128)(2,1)}), bf16[64,2,1024]{2,1,0:T(2,128)(2,1)S(1)}, u32[]{:S(2)}, u32[]{:S(2)}) async-start(bf16[64,2,1024]{2,1,0:T(2,128)(2,1)} %reshape.584), calls=%async_computation.6 | async-start | bytes 524288 | tf_op jit(solution)/shard_map/all_to_all | solution.py:68
  160.8 21.8 %copy-start.20 = (f32[32]{0:T(128)S(1)}, f32[32]{0:T(128)}, u32[]{:S(2)}) copy-start(f32[32]{0:T(128)} %param.24) | copy-start | bytes 388
  160.8 21.8 %copy-start.16 = (bf16[256,32]{0,1:T(8,128)(2,1)S(1)}, bf16[256,32]{0,1:T(8,128)(2,1)}, u32[]{:S(2)}) copy-start(bf16[256,32]{0,1:T(8,128)(2,1)} %param.20) | copy-start | bytes 49156
  160.8 21.8 %copy-start.18 = (f32[32]{0:T(128)S(1)}, f32[32]{0:T(128)}, u32[]{:S(2)}) copy-start(f32[32]{0:T(128)} %param.23) | copy-start | bytes 388
  177.9 44.6 %all-to-all-start.4 = ((bf16[2,64,4096]{2,0,1:T(2,128)(2,1)}), bf16[2,64,4096]{2,0,1:T(2,128)(2,1)S(1)}, u32[]{:S(2)}, u32[]{:S(2)}) async-start(bf16[2,64,4096]{2,0,1:T(2,128)(2,1)} %copy.100), calls=%async_computation.4 | async-start | bytes 2097152 | tf_op jit(solution)/shard_map/all_to_all | solution.py:82
  222.5 30.6 %all-to-all-start.7 = ((bf16[64,2,1024]{2,1,0:T(2,128)(2,1)}), bf16[64,2,1024]{2,1,0:T(2,128)(2,1)S(1)}, u32[]{:S(2)}, u32[]{:S(2)}) async-start(bf16[64,2,1024]{2,1,0:T(2,128)(2,1)} %reshape.586), calls=%async_computation.7 | async-start | bytes 524288 | tf_op jit(solution)/shard_map/all_to_all | solution.py:92
  237.1 20.7 %copy-start.10 = (f32[2048]{0:T(1024)S(1)}, f32[2048]{0:T(1024)}, u32[]{:S(2)}) copy-start(f32[2048]{0:T(1024)} %param.26) | copy-start | bytes 24580
  237.3 23.3 %copy-start.8 = (bf16[256,1,2,128]{3,2,1,0:T(2,128)(2,1)S(1)}, bf16[256,1,2,128]{3,2,1,0:T(2,128)(2,1)}, u32[]{:S(2)}) copy-start(bf16[256,1,2,128]{3,2,1,0:T(2,128)(2,1)} %param.19) | copy-start | bytes 393220
  237.3 23.3 %copy-start.2 = (bf16[256,2048]{1,0:T(8,128)(2,1)S(1)}, bf16[256,2048]{1,0:T(8,128)(2,1)}, u32[]{:S(2)}) copy-start(bf16[256,2048]{1,0:T(8,128)(2,1)} %param.18) | copy-start | bytes 3145732
  239.6 22.2 %copy-start.17 = (f32[4,1,2,128]{3,2,1,0:T(2,128)S(1)}, f32[4,1,2,128]{3,2,1,0:T(2,128)}, u32[]{:S(2)}) copy-start(f32[4,1,2,128]{3,2,1,0:T(2,128)} %param.22) | copy-start | bytes 12292
  239.6 22.2 %copy-start.13 = (f32[4,2048]{1,0:T(4,128)S(1)}, f32[4,2048]{1,0:T(4,128)}, u32[]{:S(2)}) copy-start(f32[4,2048]{1,0:T(4,128)} %param.21) | copy-start | bytes 98308
  253.1 26.5 %all-to-all-start.5 = ((bf16[64,2,2048]{2,1,0:T(2,128)(2,1)}), bf16[64,2,2048]{2,1,0:T(2,128)(2,1)S(1)}, u32[]{:S(2)}, u32[]{:S(2)}) async-start(bf16[64,2,2048]{2,1,0:T(2,128)(2,1)} %reshape.578), calls=%async_computation.5 | async-start | bytes 1048576 | tf_op jit(solution)/shard_map/all_to_all | solution.py:94
  263.7 3.8 %copy-start.5 = (bf16[64,2,512]{2,1,0:T(2,128)(2,1)S(1)}, bf16[64,2,512]{2,1,0:T(2,128)(2,1)}, u32[]{:S(2)}) copy-start(bf16[64,2,512]{2,1,0:T(2,128)(2,1)} %copy-done.4) | copy-start | bytes 393220
  283.3 1.2 copy-start.3
  283.3 1.3 copy-start.7
  283.3 1.2 copy-start.9
  283.3 1.2 copy-start.12
  283.3 1.2 copy-start.14
  283.3 1.2 copy-start.15
  283.3 1.2 copy-start.21
  322.0 1.9 copy-start.11
  323.9 2.8 copy-start
  323.9 2.8 copy-start.19
where the time goes:
time: 331 us; the launch traced here: 329 us
  waiting for transfers between devices  136 us (41%)
  starting transfers between devices  75.1 us (23%)
  blocking collectives  55.8 us (17%)
  local copies, waits for them, and re-layouts  30.1 us (9%)
  other arithmetic  21.9 us (7%)
  matrix products  7.25 us (2%)
    all_to_all x1, waiting for transfers between devices, per_device(): lax.all_to_all(ssm_flat, 'req', split_axis=1, concat_axis=0, tiled=True)  35.7 us
    psum x1, blocking collectives, per_device(): reduced_rank = lax.psum(low_partial, 'head').astype(jnp.bfloat16)  33.5 us
    unnamed x1, blocking collectives  22.4 us
    all_to_all x1, starting transfers between devices, per_device(): lax.all_to_all(convbc_flat, 'req', split_axis=1, concat_axis=0, tiled=True)  19.3 us
    all_to_all x1, waiting for transfers between devices, per_device(): lax.all_to_all(adapter_down_panels.reshape(adapter_down_panels.shape[0],...  15 us
    unnamed x71, local copies, waits for them, and re-layouts  14.5 us
    all_to_all x1, waiting for transfers between devices, per_device(): lax.all_to_all(picked_left_factor, 'req', split_axis=0, concat_axis=1, ti...  13.5 us
    all_to_all x1, waiting for transfers between devices, per_device(): lax.all_to_all(convx_flat, 'req', split_axis=1, concat_axis=0, tiled=True)  13.4 us
  transfers between devices with their start and end apart: 10, of which 9 were waited for; matrix products, arithmetic and copies ran while one was open for 12% of the time, Pallas kernels for 0%

commit v1 on v0

v1 whole, which is shorter than its diff:
```python
import functools

import jax
import jax.numpy as jnp
from jax import lax
from jax.experimental import pallas as pl
from jax.experimental.pallas import tpu as pltpu
from jax.sharding import PartitionSpec as P

ADAPTER_SCALE = 2.0
NORM_EPSILON = 1e-05
F32, BF16 = jnp.float32, jnp.bfloat16
VMEM_LIMIT = 48 * 1024 * 1024


def params():
    return pltpu.CompilerParams(vmem_limit_bytes=VMEM_LIMIT)


def cost(flops, nbytes):
    return pl.CostEstimate(flops=flops, bytes_accessed=nbytes, transcendentals=0)


def smem():
    return pl.BlockSpec(memory_space=pltpu.SMEM)


def vmem():
    return pl.BlockSpec(memory_space=pltpu.VMEM)


def pack_first(tenant, table, owner, slot, down, up, convx, convbc, out):
    out[:, 0:16, :] = jnp.concatenate([down[0, 0:1024, :], down[0, 1024:2048, :]], axis=1).reshape(64, 16, 128)
    for col in range(8):
        for row in range(8):
            out[col * 8 + row, 16:24, :] = up[0, row * 8 : row * 8 + 8, col * 128 : col * 128 + 128]
    lines = lax.broadcasted_iota(jnp.int32, (8, 128), 0)
    adapter = table[tenant[0]].astype(F32)
    base = jnp.where(lines == 2, adapter, jnp.where(lines == 3, owner[0].astype(F32), slot[0].astype(F32)))
    for chunk in range(64):
        tile = base
        if chunk < 54:
            for which in range(2):
                if chunk < 48:
                    k, col = chunk // 16, chunk % 16
                    line = convx[which, k : k + 1, col * 128 : col * 128 + 128]
                else:
                    k, side = (chunk - 48) // 2, (chunk - 48) % 2
                    line = convbc[which, k, 0, side : side + 1, :]
                tile = jnp.where(lines == which, jnp.broadcast_to(line.astype(F32), (8, 128)), tile)
        out[chunk, 24:32, :] = tile.astype(BF16)


def pack_second(codes, first, states, out):
    out[:, 0:32, :] = states[0]
    lines = lax.broadcasted_iota(jnp.int32, (8, 128), 0)

    def body(j, carry):
        adapter, owner, slot = codes[0, j], codes[1, j], codes[2, j]
        out[j, 32:56, :] = first[adapter, 0:24, :]
        tile = first[owner, 24:32, :].astype(F32)
        picked = jnp.sum(jnp.where(lines == slot, tile, 0.0), axis=0, keepdims=True)
        out[j, 56:64, :] = jnp.broadcast_to(picked, (8, 128)).astype(BF16)
        return carry

    lax.fori_loop(0, 64, body, 0, unroll=8)


def pack_third(codes, second, out):
    def body(j, carry):
        out[j] = second[codes[1, j]]
        return carry

    lax.fori_loop(0, 64, body, 0, unroll=8)


def steps_kernel(raw, bias, rate, decay, decay_t, step, step_t):
    v = raw[...].astype(F32) + bias[...]
    size = jnp.maximum(v, 0.0) + jnp.log(1.0 + jnp.exp(-jnp.abs(v)))
    size = jnp.concatenate([size, jnp.zeros((256, 96), F32)], axis=1)
    drop = -rate[...] * size
    rows = lax.broadcasted_iota(jnp.int32, (256, 256), 0)
    cols = lax.broadcasted_iota(jnp.int32, (256, 256), 1)
    lower = (rows >= cols).astype(F32).astype(BF16)
    high = drop.astype(BF16)
    rest = drop - high.astype(F32)
    middle = rest.astype(BF16)
    low = (rest - middle.astype(F32)).astype(BF16)
    total = jnp.dot(lower, low, preferred_element_type=F32)
    total = total + jnp.dot(lower, middle, preferred_element_type=F32)
    total = total + jnp.dot(lower, high, preferred_element_type=F32)
    decay[...] = total
    step[...] = size
    decay_t[...] = total.T[0:32, :]
    step_t[...] = size.T[0:32, :]


def widen_kernel(decay, step, gate, carry):
    block = pl.program_id(0)
    total = decay[...]
    grow = jnp.exp(total)
    keep = jnp.exp(total[255:256, :] - total) * step[...]
    shift = lax.rem(128 - 4 * block, 128)
    grow, keep = pltpu.roll(grow, shift, 1), pltpu.roll(keep, shift, 1)
    left = lax.broadcasted_iota(jnp.int32, (256, 128), 1) < 64
    for pair in range(2):
        lo, hi = 2 * pair, 2 * pair + 1
        at = slice(pair * 128, pair * 128 + 128)
        gate[:, at] = jnp.where(left, grow[:, lo : lo + 1], grow[:, hi : hi + 1])
        carry[:, at] = jnp.where(left, keep[:, lo : lo + 1], keep[:, hi : hi + 1])


def silu(v):
    return v / (1.0 + jnp.exp(-v))


def history(convs, index):
    lines = lax.broadcasted_iota(jnp.int32, (8, 128), 0)
    old = [convs[i].astype(F32) for i in index]
    return jnp.where(lines == 5, old[0], jnp.where(lines == 6, old[1], old[2]))


def conv(pad, taps):
    out = taps[0:1, :] * pad[5:261, :]
    for k in range(1, 4):
        out = out + taps[k : k + 1, :] * pad[5 + k : 261 + k, :]
    return silu(out).astype(BF16)


def mix_kernel(
    x, bc, taps, bc_taps, convs, skip, decay, decay_t, step_t, carry,
    part, c_out, fresh, pad, pad_bc, score, b_proj,
):
    block = pl.program_id(0)

    @pl.when(block == 0)
    def _():
        for side in range(2):
            at = slice(side * 128, side * 128 + 128)
            pad_bc[0:8, at] = history(convs, [48 + side, 50 + side, 52 + side])
        pad_bc[8:264, :] = bc[...].astype(F32)
        both = conv(pad_bc, bc_taps)
        b_proj[...] = both[:, 0:128]
        c_out[...] = both[:, 128:256]
        score[...] = lax.dot_general(both[:, 128:256], both[:, 0:128], (((1,), (1,)), ((), ())), preferred_element_type=F32)

    for half in range(2):
        at = slice(half * 128, half * 128 + 128)
        col = block * 2 + half
        pad[0:8, at] = history(convs, [col, col + 16, col + 32])
    pad[8:264, :] = x[...].astype(F32)
    inner = conv(pad, taps)
    moved = pltpu.roll(decay[...], lax.rem(128 - 4 * block, 128), 1)
    rows = lax.broadcasted_iota(jnp.int32, (128, 128), 0)
    cols = lax.broadcasted_iota(jnp.int32, (128, 128), 1)
    causal = rows >= cols
    left = cols < 64
    wide = inner.astype(F32)
    for pair in range(2):
        at = slice(pair * 128, pair * 128 + 128)
        values = inner[:, at]
        top, bottom = [], []
        for side in range(2):
            head = 2 * pair + side
            here = moved[:, head : head + 1]
            there = decay_t[pl.ds(4 * block + head, 1), :]
            weight = step_t[pl.ds(4 * block + head, 1), :]
            gap = here[0:128] - there[:, 0:128]
            mix = score[0:128, 0:128] * jnp.exp(jnp.where(causal, gap, -jnp.inf)) * weight[:, 0:128]
            top.append(jnp.dot(mix.astype(BF16), values[0:128], preferred_element_type=F32))
            gap = here[128:256] - there[:, 0:128]
            mix = score[128:256, 0:128] * jnp.exp(gap) * weight[:, 0:128]
            first = mix.astype(BF16)
            gap = here[128:256] - there[:, 128:256]
            mix = score[128:256, 128:256] * jnp.exp(jnp.where(causal, gap, -jnp.inf)) * weight[:, 128:256]
            both = jnp.concatenate([first, mix.astype(BF16)], axis=1)
            bottom.append(jnp.dot(both, values, preferred_element_type=F32))
        gain = skip[:, at]
        part[0:128, at] = jnp.where(left, top[0], top[1]) + gain * wide[0:128, at]
        part[128:256, at] = jnp.where(left, bottom[0], bottom[1]) + gain * wide[128:256, at]
    carried = (wide * carry[...]).astype(BF16)
    fresh[...] = lax.dot_general(carried, b_proj[...], (((0,), (0,)), ((), ())), preferred_element_type=F32)


def state_kernel(state, c_proj, part, gate, fresh, kept, gain, down, normed, low, updated, mixed):
    c_value = c_proj[...]
    square = jnp.zeros((256, 128), F32)
    for block in range(8):
        at = slice(block * 256, block * 256 + 256)
        old = state[block * 8 : block * 8 + 8].reshape(256, 128)
        inter = lax.dot_general(c_value, old, (((1,), (1,)), ((), ())), preferred_element_type=F32)
        total = part[:, at] + inter * gate[:, at]
        mixed[:, at] = total
        square = square + total[:, 0:128] * total[:, 0:128] + total[:, 128:256] * total[:, 128:256]
        updated[0, at, :] = (fresh[at, :] + kept[at, :] * old.astype(F32)).astype(BF16)
    mean = jnp.sum(square, axis=1, keepdims=True) * (1.0 / 2048.0)
    scale = lax.rsqrt(mean + NORM_EPSILON)
    sums = []
    for side in range(2):
        acc = jnp.zeros((256, 128), F32)
        for block in range(4):
            start = side * 1024 + block * 256
            at = slice(start, start + 256)
            value = (mixed[:, at] * scale * gain[:, at]).astype(BF16)
            normed[:, at] = value
            panel = down[block * 16 : block * 16 + 16].reshape(256, 128)
            acc = acc + jnp.dot(value, panel, preferred_element_type=F32)
        sums.append(acc)
    both = sums[0] + pltpu.roll(sums[1], 64, 1)
    left = lax.broadcasted_iota(jnp.int32, (128, 128), 1) < 64
    packed = jnp.where(left, both[0:128], pltpu.roll(both[128:256], 64, 1)).astype(BF16)
    for peer in range(8):
        low[peer] = packed


def up_kernel(parts, up, out):
    total = parts[0].astype(F32)
    for peer in range(1, 8):
        total = total + parts[peer].astype(F32)
    reduced = total.astype(BF16)
    halves = [reduced[:, 0:64], reduced[:, 64:128]]
    for col in range(8):
        panel = up[col * 8 : col * 8 + 8].astype(F32).reshape(64, 128).astype(BF16)
        at = slice(col * 128, col * 128 + 128)
        for half in range(2):
            value = jnp.dot(halves[half], panel, preferred_element_type=F32) * ADAPTER_SCALE
            out[half * 128 : half * 128 + 128, at] = value.astype(BF16)


def exchange(value, axis):
    return lax.all_to_all(value, axis, split_axis=0, concat_axis=0, tiled=True)


def per_device(
    inner_input,
    projection_input,
    step_before_bias,
    inner_conv_taps,
    projection_conv_taps,
    step_bias,
    head_decay_rate,
    head_skip_gain,
    group_norm_gain,
    tenant,
    tenant_adapter_row,
    cache_holder_index,
    cache_slot_index,
    adapter_down_panels,
    adapter_up_panels,
    cached_ssm_states,
    inner_conv_cache,
    projection_conv_cache,
):
    hold = lax.optimization_barrier
    packed = jax.ShapeDtypeStruct
    sent1 = pl.pallas_call(
        pack_first,
        out_shape=packed((64, 32, 128), BF16),
        in_specs=[smem()] * 4 + [vmem()] * 4,
        out_specs=vmem(),
        compiler_params=params(),
        cost_estimate=cost(0, 2 << 20),
        name="pack_first",
    )(
        tenant, tenant_adapter_row, cache_holder_index, cache_slot_index,
        adapter_down_panels, adapter_up_panels, inner_conv_cache, projection_conv_cache,
    )
    sent1, raw = hold((sent1, step_before_bias))
    got1 = exchange(sent1, "req")
    rate = jnp.pad(head_decay_rate, (0, 96)).reshape(1, 128)
    decay, decay_t, step, step_t = pl.pallas_call(
        steps_kernel,
        out_shape=[packed((256, 128), F32), packed((32, 256), F32), packed((256, 128), F32), packed((32, 256), F32)],
        in_specs=[vmem()] * 3,
        out_specs=[vmem()] * 4,
        compiler_params=params(),
        cost_estimate=cost(6 * 256 * 256 * 128, 1 << 20),
        name="steps",
    )(raw, step_bias.reshape(1, 32), rate)
    skip_wide = jnp.repeat(head_skip_gain, 64).reshape(1, 2048)
    got1, decay, skip_wide = hold((got1, decay, skip_wide))

    me = lax.axis_index("req")
    words = got1[:, 26:29, 0].astype(jnp.int32)
    mine = jnp.sum(jnp.where(words[:, 1] == me, words[:, 2], 0))
    codes = jnp.concatenate([words.T, jnp.broadcast_to(mine, (1, 64))], axis=0)
    states = cached_ssm_states.reshape(2, 64, 32, 128)
    sent2 = pl.pallas_call(
        pack_second,
        out_shape=packed((64, 64, 128), BF16),
        grid_spec=pltpu.PrefetchScalarGridSpec(
            num_scalar_prefetch=1,
            grid=(1,),
            in_specs=[
                pl.BlockSpec((64, 32, 128), lambda i, c: (0, 0, 0)),
                pl.BlockSpec((1, 64, 32, 128), lambda i, c: (c[3, 0], 0, 0, 0)),
            ],
            out_specs=pl.BlockSpec((64, 64, 128), lambda i, c: (0, 0, 0)),
        ),
        compiler_params=params(),
        cost_estimate=cost(0, 3 << 20),
        name="pack_second",
    )(codes, got1, states)
    sent2, decay, step = hold((sent2, decay, step))
    got2 = exchange(sent2, "req")
    gate, carry = pl.pallas_call(
        widen_kernel,
        out_shape=[packed((256, 2048), F32)] * 2,
        grid=(8,),
        in_specs=[pl.BlockSpec((256, 128), lambda i: (0, 0))] * 2,
        out_specs=[pl.BlockSpec((256, 256), lambda i: (0, i))] * 2,
        compiler_params=params(),
        cost_estimate=cost(0, 6 << 20),
        name="widen",
    )(decay, step)
    kept = jnp.broadcast_to(gate[255:256, :].reshape(2048, 1), (2048, 128))
    got2, gate, carry, kept = hold((got2, gate, carry, kept))

    sent3 = pl.pallas_call(
        pack_third,
        out_shape=packed((64, 32, 128), BF16),
        grid_spec=pltpu.PrefetchScalarGridSpec(
            num_scalar_prefetch=1,
            grid=(1,),
            in_specs=[pl.BlockSpec((64, 32, 128), lambda i, c: (0, 0, 0))],
            out_specs=pl.BlockSpec((64, 32, 128), lambda i, c: (0, 0, 0)),
        ),
        compiler_params=params(),
        cost_estimate=cost(0, 1 << 20),
        name="pack_third",
    )(codes, got2)
    sent3, got2 = hold((sent3, got2))
    got3 = exchange(sent3, "req")
    part, c_proj, fresh = pl.pallas_call(
        mix_kernel,
        out_shape=[packed((256, 2048), F32), packed((256, 128), BF16), packed((2048, 128), F32)],
        grid=(8,),
        in_specs=[
            pl.BlockSpec((256, 256), lambda i: (0, i)),
            pl.BlockSpec((256, 256), lambda i: (0, 0)),
            pl.BlockSpec((4, 256), lambda i: (0, i)),
            pl.BlockSpec((4, 256), lambda i: (0, 0)),
            pl.BlockSpec((64, 8, 128), lambda i: (0, 7, 0)),
            pl.BlockSpec((1, 256), lambda i: (0, i)),
            pl.BlockSpec((256, 128), lambda i: (0, 0)),
            pl.BlockSpec((32, 256), lambda i: (0, 0)),
            pl.BlockSpec((32, 256), lambda i: (0, 0)),
            pl.BlockSpec((256, 256), lambda i: (0, i)),
        ],
        out_specs=[
            pl.BlockSpec((256, 256), lambda i: (0, i)),
            pl.BlockSpec((256, 128), lambda i: (0, 0)),
            pl.BlockSpec((256, 128), lambda i: (i, 0)),
        ],
        scratch_shapes=[
            pltpu.VMEM((264, 256), F32),
            pltpu.VMEM((264, 256), F32),
            pltpu.VMEM((256, 256), F32),
            pltpu.VMEM((256, 128), BF16),
        ],
        compiler_params=params(),
        cost_estimate=cost(2 << 30, 10 << 20),
        name="mix",
    )(
        inner_input, projection_input.reshape(256, 256), inner_conv_taps, projection_conv_taps.reshape(4, 256),
        got2, skip_wide, decay, decay_t, step_t, carry,
    )
    got3, part, c_proj, fresh = hold((got3, part, c_proj, fresh))

    normed, low, updated = pl.pallas_call(
        state_kernel,
        out_shape=[packed((256, 2048), BF16), packed((8, 128, 128), BF16), packed((1, 2048, 128), BF16)],
        grid=(1,),
        in_specs=[
            pl.BlockSpec((64, 32, 128), lambda i: (0, 0, 0)),
            pl.BlockSpec((256, 128), lambda i: (0, 0)),
            pl.BlockSpec((256, 2048), lambda i: (0, 0)),
            pl.BlockSpec((256, 2048), lambda i: (0, 0)),
            pl.BlockSpec((2048, 128), lambda i: (0, 0)),
            pl.BlockSpec((2048, 128), lambda i: (0, 0)),
            pl.BlockSpec((1, 2048), lambda i: (0, 0)),
            pl.BlockSpec((64, 16, 128), lambda i: (0, 2, 0)),
        ],
        out_specs=[
            pl.BlockSpec((256, 2048), lambda i: (0, 0)),
            pl.BlockSpec((8, 128, 128), lambda i: (0, 0, 0)),
            pl.BlockSpec((1, 2048, 128), lambda i: (0, 0, 0)),
        ],
        scratch_shapes=[pltpu.VMEM((256, 2048), F32)],
        compiler_params=params(),
        cost_estimate=cost(1 << 28, 8 << 20),
        name="state",
    )(got3, c_proj, part, gate, fresh, kept, group_norm_gain.reshape(1, 2048), got2)
    parts = exchange(low, "head")
    term = pl.pallas_call(
        up_kernel,
        out_shape=packed((256, 1024), BF16),
        grid=(1,),
        in_specs=[
            pl.BlockSpec((8, 128, 128), lambda i: (0, 0, 0)),
            pl.BlockSpec((64, 8, 128), lambda i: (0, 6, 0)),
        ],
        out_specs=pl.BlockSpec((256, 1024), lambda i: (0, 0)),
        compiler_params=params(),
        cost_estimate=cost(1 << 26, 1 << 20),
        name="up",
    )(parts, got2)
    return normed, term, updated.reshape(1, 32, 64, 128)


def solution(mesh):
    return jax.shard_map(
        per_device,
        mesh=mesh,
        in_specs=(
            P("req", "head"),
            P("req", "head", None, None),
            P("req", "head"),
            P(None, "head"),
            P(None, "head", None, None),
            P("head"),
            P("head"),
            P("head"),
            P("head"),
            P("req"),
            P(),
            P("req"),
            P("req"),
            P("req", "head", None),
            P("req", None, "head"),
            P("req", "head", None, None),
            P("req", None, "head"),
            P("req", None, "head", None, None),
        ),
        out_specs=(P("req", "head"), P("req", "head"), P("req", "head", None, None)),
        check_vma=False,
    )
```

time: 331 us -> 185 us (0.56)
  waiting for transfers between devices: 136 us -> 90.6 us
  blocking collectives: 55.8 us -> 16.3 us
  starting transfers between devices: 75.1 us -> 35.8 us
  Pallas kernels: 0 us -> 21.7 us
  other arithmetic: 21.9 us -> 0.65 us
  local copies, waits for them, and re-layouts: 30.1 us -> 16.1 us
  matrix products: 7.25 us -> 0 us
    all_to_all x10 -> x3, waiting for transfers between devices: 136 us -> 90.6 us  [exchange(): return lax.all_to_all(value, axis, split_axis=0, concat_axis=0, tiled=True)]
    all_to_all x10 -> x3, starting transfers between devices: 75.1 us -> 35.8 us  [exchange(): return lax.all_to_all(value, axis, split_axis=0, concat_axis=0, tiled=True)]
    psum x1 -> x0, blocking collectives: 33.5 us -> none  [per_device(): reduced_rank = lax.psum(low_partial, 'head').astype(jnp.bfloat16)]
    unnamed x1 -> x0, blocking collectives: 22.4 us -> none
    pallas_call x0 -> x8, Pallas kernels: none -> 21.7 us  [the longest x1 7.95 us: per_device(): pl.pallas_call(mix_kernel, out_shape=[packed((256, 2048), F32), packed((2...]
    all_to_all x0 -> x1, blocking collectives: none -> 16.3 us  [exchange(): return lax.all_to_all(value, axis, split_axis=0, concat_axis=0, tiled=True)]
    dot_general x6 -> x0, matrix products: 7.25 us -> none  [the longest x1 2.63 us: per_device(): jnp.einsum('rghts,rsghp->rtghp', mix_weights, conv_heads, preferred_eleme...]
    convert_element_type x4 -> x1, other arithmetic: 7.24 us -> 0.01 us  [per_device(): words = got1[:, 26:29, 0].astype(jnp.int32)]
  transfers between devices with their start and end apart: 10 -> 3, of which waited for: 9 -> 3; matrix products, arithmetic and copies ran while one was open for 12% -> 0% of each run, Pallas kernels for 0% -> 7%
where the time goes in v1:
time: 185 us; the launch traced here: 184 us
  waiting for transfers between devices  90.6 us (49%)
  starting transfers between devices  35.8 us (19%)
  Pallas kernels  21.7 us (12%)
  blocking collectives  16.3 us (9%)
  local copies, waits for them, and re-layouts  16.1 us (9%)
  between operations  2.87 us (2%)
    all_to_all x3, waiting for transfers between devices, exchange(): return lax.all_to_all(value, axis, split_axis=0, concat_axis=0, tiled=True)  90.6 us
    all_to_all x3, starting transfers between devices, exchange(): return lax.all_to_all(value, axis, split_axis=0, concat_axis=0, tiled=True)  35.8 us
    all_to_all x1, blocking collectives, exchange(): return lax.all_to_all(value, axis, split_axis=0, concat_axis=0, tiled=True)  16.3 us
    unnamed x42, local copies, waits for them, and re-layouts  13.2 us
    pallas_call x1, Pallas kernels, per_device(): pl.pallas_call(mix_kernel, out_shape=[packed((256, 2048), F32), packed((2...  7.95 us
  transfers between devices with their start and end apart: 3, of which 3 were waited for; matrix products, arithmetic and copies ran while one was open for 0% of the time, Pallas kernels for 7%

profile of v1, /device:TPU:1, one launch (start us, length us, event | category | flops | bytes accessed | tf_op | source)
XLA Modules:
  0.0 184.1 jit_solution(13538182316608469467)
XLA Ops:
  2.6 0.8 copy.27.convx
  3.4 1.2 copy.26.down
  4.6 0.9 copy-done.6
  5.5 0.7 copy-done.8
  6.2 0.7 copy-done.9
  6.9 1.5 pack_first.1
  8.4 19.3 %all-to-all-start = ((bf16[64,32,128]{2,1,0:T(8,128)(2,1)}), bf16[64,32,128]{2,1,0:T(8,128)(2,1)S(1)}, u32[]{:S(2)}, u32[]{:S(2)}) async-start(bf16[64,32,128]{2,1,0:T(8,128)(2,1)} %pack_first.1), calls=%async_computation | async-start | bytes 1048576 | tf_op jit(solution)/shard_map/all_to_all | solution.py:231
  27.8 0.1 copy.28.raw
  28.0 0.4 steps.1
  28.4 29.3 %all-to-all-done.first = bf16[64,32,128]{2,1,0:T(8,128)(2,1)S(1)} async-done(((bf16[64,32,128]{2,1,0:T(8,128)(2,1)}), bf16[64,32,128]{2,1,0:T(8,128)(2,1)S(1)}, u32[]{:S(2)}, u32[]{:S(2)}) %all-to-all-start) | async-done | bytes 524320 | tf_op jit(solution)/shard_map/all_to_all | solution.py:231
  57.7 1.7 copy.29
  59.4 0.6 fusion.1
  60.0 0.6 concatenate.3.codes
  60.7 1.9 %pack_second.1 = bf16[64,64,128]{2,1,0:T(8,128)(2,1)} custom-call(s32[4,64]{1,0:T(4,128)S(1)} %concatenate.3.codes, bf16[64,32,128]{2,1,0:T(8,128)(2,1)S(1)} %all-to-all-done.first, bf16[2,64,32,128]{3,2,1,0:T(8,128)(2,1)S(1)} %bitcast.26), custom_call_target="tpu_custom_call" | custom-call | bytes 3145728 | tf_op jit(solution)/shard_map/pack_second/pallas_call | solution.py:288
  62.6 7.9 %all-to-all-start.1 = ((bf16[64,64,128]{2,1,0:T(8,128)(2,1)}), bf16[64,64,128]{2,1,0:T(8,128)(2,1)S(1)}, u32[]{:S(2)}, u32[]{:S(2)}) async-start(bf16[64,64,128]{2,1,0:T(8,128)(2,1)} %pack_second.1), calls=%async_computation.1 | async-start | bytes 2097152 | tf_op jit(solution)/shard_map/all_to_all | solution.py:231
  70.5 3.6 %widen.1 = (f32[256,2048]{1,0:T(8,128)S(1)}, f32[256,2048]{1,0:T(8,128)S(1)}) custom-call(f32[256,128]{1,0:T(8,128)S(1)} %get-tuple-element.40.decay, f32[256,128]{1,0:T(8,128)S(1)} %get-tuple-element.41.step), custom_call_target="tpu_custom_call" | custom-call | bytes 6291456 | tf_op jit(solution)/shard_map/widen/pallas_call | solution.py:306
  74.2 1.3 copy-done.10
  75.5 1.3 copy-done
  76.8 44.5 %all-to-all-done.1.second.convs.down.up = bf16[64,64,128]{2,1,0:T(8,128)(2,1)S(1)} async-done(((bf16[64,64,128]{2,1,0:T(8,128)(2,1)}), bf16[64,64,128]{2,1,0:T(8,128)(2,1)S(1)}, u32[]{:S(2)}, u32[]{:S(2)}) %all-to-all-start.1) | async-done | bytes 1048608 | tf_op jit(solution)/shard_map/all_to_all | solution.py:231
  121.3 0.3 broadcast_in_dim.18.kept
  121.6 1.6 pack_third.1
  123.2 8.7 %all-to-all-start.2 = ((bf16[64,32,128]{2,1,0:T(8,128)(2,1)}), bf16[64,32,128]{2,1,0:T(8,128)(2,1)S(1)}, u32[]{:S(2)}, u32[]{:S(2)}) async-start(bf16[64,32,128]{2,1,0:T(8,128)(2,1)} %pack_third.1), calls=%async_computation.2 | async-start | bytes 1048576 | tf_op jit(solution)/shard_map/all_to_all | solution.py:231
  132.0 1.2 copy-done.11
  133.2 7.9 %mix.1 = (f32[256,2048]{1,0:T(8,128)S(1)}, bf16[256,128]{1,0:T(8,128)(2,1)S(1)}, f32[2048,128]{1,0:T(8,128)S(1)}) custom-call(bf16[256,2048]{1,0:T(8,128)(2,1)S(1)} %copy-done.11, bf16[256,256]{1,0:T(8,128)(2,1)S(1)} %bitcast.27, f32[4,2048]{1,0:T(4,128)S(1)} %copy-done.12, f32[4,256]{1,0:T(4,128)S(1)} %bitcast.29, ...), custom_call_target="tpu_custom_call" | custom-call | flops 2147483648 | bytes 10485760 | tf_op jit(solution)/shard_map/mix/pallas_call | solution.py:334
  141.1 1.3 copy-done.1
  142.4 1.0 copy-done.3
  143.4 16.8 %all-to-all-done.2.state = bf16[64,32,128]{2,1,0:T(8,128)(2,1)S(1)} async-done(((bf16[64,32,128]{2,1,0:T(8,128)(2,1)}), bf16[64,32,128]{2,1,0:T(8,128)(2,1)S(1)}, u32[]{:S(2)}, u32[]{:S(2)}) %all-to-all-start.2) | async-done | bytes 524320 | tf_op jit(solution)/shard_map/all_to_all | solution.py:231
  160.2 1.6 copy-done.2
  161.8 1.2 copy-done.4
  163.0 3.6 %state.1 = (bf16[256,2048]{1,0:T(8,128)(2,1)}, bf16[8,128,128]{2,1,0:T(8,128)(2,1)S(1)}, bf16[1,2048,128]{2,1,0:T(8,128)(2,1)}) custom-call(bf16[64,32,128]{2,1,0:T(8,128)(2,1)S(1)} %all-to-all-done.2.state, bf16[256,128]{1,0:T(8,128)(2,1)S(1)} %get-tuple-element.55.c_proj, f32[256,2048]{1,0:T(8,128)S(1)} %copy-done.2, f32[256,2048]{1,0:T(8,128)} %copy-done, ...), custom_call_target="tpu_custom_call" | custom-call | flops 268435456 | bytes 8388608 | tf_op jit(solution)/shard_map/state/pallas_call | solution.py:370
  166.6 16.3 %all_to_all.20.parts = bf16[8,128,128]{2,1,0:T(8,128)(2,1)S(1)} all-to-all(bf16[8,128,128]{2,1,0:T(8,128)(2,1)S(1)} %get-tuple-element.61), channel_id=1, replica_groups=mesh['req'=64,'head'=8] {'head'}, dimensions={0} | all-to-all | bytes 524288 | tf_op jit(solution)/shard_map/all_to_all | solution.py:231
  182.9 1.2 up.3
  (35 shorter events, 0.3 us)
Async XLA Ops:
  0.6 27.2 %copy-start.15 = (bf16[256,32]{0,1:T(8,128)(2,1)S(1)}, bf16[256,32]{0,1:T(8,128)(2,1)}, u32[]{:S(2)}) copy-start(bf16[256,32]{0,1:T(8,128)(2,1)} %param.20) | copy-start | bytes 49156
  0.6 27.0 %copy-start.17 = (f32[32]{0:T(128)S(1)}, f32[32]{0:T(128)}, u32[]{:S(2)}) copy-start(f32[32]{0:T(128)} %param.25) | copy-start | bytes 388
  0.7 27.3 %copy-start.18 = (f32[32]{0:T(128)S(1)}, f32[32]{0:T(128)}, u32[]{:S(2)}) copy-start(f32[32]{0:T(128)} %param.24) | copy-start | bytes 388
  0.7 27.3 %copy-start.13 = (f32[32]{0:T(128)S(1)}, f32[32]{0:T(128)}, u32[]{:S(2)}) copy-start(f32[32]{0:T(128)} %param.23) | copy-start | bytes 388
  4.6 0.9 copy-start.6
  5.5 0.7 copy-start.8
  6.2 0.7 copy-start.9
  6.9 53.8 %copy-start.5 = (bf16[2,32,64,128]{3,2,1,0:T(8,128)(2,1)S(1)}, bf16[2,32,64,128]{3,2,1,0:T(8,128)(2,1)}, u32[]{:S(2)}) copy-start(bf16[2,32,64,128]{3,2,1,0:T(8,128)(2,1)} %param.33) | copy-start | bytes 3145732
  8.4 49.3 %all-to-all-start = ((bf16[64,32,128]{2,1,0:T(8,128)(2,1)}), bf16[64,32,128]{2,1,0:T(8,128)(2,1)S(1)}, u32[]{:S(2)}, u32[]{:S(2)}) async-start(bf16[64,32,128]{2,1,0:T(8,128)(2,1)} %pack_first.1), calls=%async_computation | async-start | bytes 1048576 | tf_op jit(solution)/shard_map/all_to_all | solution.py:231
  62.6 58.7 %all-to-all-start.1 = ((bf16[64,64,128]{2,1,0:T(8,128)(2,1)}), bf16[64,64,128]{2,1,0:T(8,128)(2,1)S(1)}, u32[]{:S(2)}, u32[]{:S(2)}) async-start(bf16[64,64,128]{2,1,0:T(8,128)(2,1)} %pack_second.1), calls=%async_computation.1 | async-start | bytes 2097152 | tf_op jit(solution)/shard_map/all_to_all | solution.py:231
  70.5 61.4 %copy-start.16 = (f32[4,1,2,128]{3,2,1,0:T(2,128)S(1)}, f32[4,1,2,128]{3,2,1,0:T(2,128)}, u32[]{:S(2)}) copy-start(f32[4,1,2,128]{3,2,1,0:T(2,128)} %param.22) | copy-start | bytes 12292
  70.5 61.4 %copy-start.14 = (bf16[256,1,2,128]{3,2,1,0:T(2,128)(2,1)S(1)}, bf16[256,1,2,128]{3,2,1,0:T(2,128)(2,1)}, u32[]{:S(2)}) copy-start(bf16[256,1,2,128]{3,2,1,0:T(2,128)(2,1)} %param.19) | copy-start | bytes 393220
  70.5 61.4 %copy-start.12 = (f32[4,2048]{1,0:T(4,128)S(1)}, f32[4,2048]{1,0:T(4,128)}, u32[]{:S(2)}) copy-start(f32[4,2048]{1,0:T(4,128)} %taps.1) | copy-start | bytes 98308
  74.2 1.3 copy-start.10
  75.5 1.3 copy-start
  123.2 37.0 %all-to-all-start.2 = ((bf16[64,32,128]{2,1,0:T(8,128)(2,1)}), bf16[64,32,128]{2,1,0:T(8,128)(2,1)S(1)}, u32[]{:S(2)}, u32[]{:S(2)}) async-start(bf16[64,32,128]{2,1,0:T(8,128)(2,1)} %pack_third.1), calls=%async_computation.2 | async-start | bytes 1048576 | tf_op jit(solution)/shard_map/all_to_all | solution.py:231
  132.0 1.2 copy-start.11
  133.2 27.0 %copy-start.7 = (f32[2048]{0:T(1024)S(1)}, f32[2048]{0:T(1024)}, u32[]{:S(2)}) copy-start(f32[2048]{0:T(1024)} %param.26) | copy-start | bytes 24580
  141.1 1.3 copy-start.1
  142.4 1.0 copy-start.3
  160.2 1.6 copy-start.2
  161.8 1.2 copy-start.4

commit v2 on v1

--- a/solution.py
+++ b/solution.py
@@ -10,11 +10,11 @@
 ADAPTER_SCALE = 2.0
 NORM_EPSILON = 1e-05
 F32, BF16 = jnp.float32, jnp.bfloat16
-VMEM_LIMIT = 48 * 1024 * 1024
-
-
-def params():
-    return pltpu.CompilerParams(vmem_limit_bytes=VMEM_LIMIT)
+MIB = 1024 * 1024
+
+
+def params(mib=20):
+    return pltpu.CompilerParams(vmem_limit_bytes=mib * MIB)
 
 
 def cost(flops, nbytes):
@@ -29,46 +29,70 @@
     return pl.BlockSpec(memory_space=pltpu.VMEM)
 
 
-def pack_first(tenant, table, owner, slot, down, up, convx, convbc, out):
-    out[:, 0:16, :] = jnp.concatenate([down[0, 0:1024, :], down[0, 1024:2048, :]], axis=1).reshape(64, 16, 128)
-    for col in range(8):
-        for row in range(8):
-            out[col * 8 + row, 16:24, :] = up[0, row * 8 : row * 8 + 8, col * 128 : col * 128 + 128]
+def pack_first(tenant, table, owner, slot, down, up, convx, convbc, states, out):
+    for chunk in range(64):
+        col, row = chunk // 4, chunk % 4
+        out[chunk, 0:16, :] = down[row * 16 : row * 16 + 16, col * 128 : col * 128 + 128]
+        col, row = chunk // 8, chunk % 8
+        out[chunk, 16:24, :] = up[0, row * 8 : row * 8 + 8, col * 128 : col * 128 + 128]
     lines = lax.broadcasted_iota(jnp.int32, (8, 128), 0)
+    lanes = lax.broadcasted_iota(jnp.int32, (8, 128), 1)
     adapter = table[tenant[0]].astype(F32)
-    base = jnp.where(lines == 2, adapter, jnp.where(lines == 3, owner[0].astype(F32), slot[0].astype(F32)))
+    base = jnp.where(lanes == 0, adapter, jnp.where(lanes == 1, owner[0].astype(F32), slot[0].astype(F32)))
     for chunk in range(64):
         tile = base
         if chunk < 54:
             for which in range(2):
                 if chunk < 48:
                     k, col = chunk // 16, chunk % 16
-                    line = convx[which, k : k + 1, col * 128 : col * 128 + 128]
+                    line = convx[k, which : which + 1, col * 128 : col * 128 + 128]
                 else:
                     k, side = (chunk - 48) // 2, (chunk - 48) % 2
                     line = convbc[which, k, 0, side : side + 1, :]
                 tile = jnp.where(lines == which, jnp.broadcast_to(line.astype(F32), (8, 128)), tile)
+        tile = jnp.where(lines >= 4, pltpu.roll(states[0, chunk].astype(F32), 6, 0), tile)
+        tile = jnp.where(lines >= 6, states[1, chunk].astype(F32), tile)
         out[chunk, 24:32, :] = tile.astype(BF16)
 
 
-def pack_second(codes, first, states, out):
-    out[:, 0:32, :] = states[0]
+def pack_second(me, first, states, out, codes, words, sems):
     lines = lax.broadcasted_iota(jnp.int32, (8, 128), 0)
+    tall = lax.broadcasted_iota(jnp.int32, (64, 8, 128), 1)
+    picked = jnp.sum(jnp.where(tall == 2, first[:, 24:32, :].astype(F32), 0.0), axis=1)
+    turned = jnp.concatenate([picked, jnp.zeros((64, 128), F32)], axis=0).T
+    words[...] = turned[0:8, :].astype(jnp.int32)
+    to_scalars = pltpu.make_async_copy(words, codes, sems.at[0])
+    to_scalars.start()
+    to_scalars.wait()
+    mine = lax.fori_loop(0, 64, lambda j, m: jnp.where(codes[1, j] == me[0], codes[2, j], m), 0, unroll=8)
+    own = pltpu.make_async_copy(states.at[mine], out.at[:, 0:32, :], sems.at[1])
+    own.start()
+
+    def panels(j, carry):
+        out[j, 32:56, :] = first[codes[0, j], 0:24, :]
+        return carry
+
+    lax.fori_loop(0, 64, panels, 0, unroll=8)
+    own.wait()
+
+    def lines_of(j, carry):
+        tile = first[codes[1, j], 24:32, :].astype(F32)
+        line = jnp.where(codes[2, j] == 0, tile[0:1], tile[1:2])
+        out[j, 24:32, :] = jnp.where(lines == 6, line, out[j, 24:32, :].astype(F32)).astype(BF16)
+        return carry
+
+    lax.fori_loop(0, 64, lines_of, 0, unroll=8)
+
+
+def pack_third(codes, first, second, out):
+    lines = lax.broadcasted_iota(jnp.int32, (8, 128), 0)
 
     def body(j, carry):
-        adapter, owner, slot = codes[0, j], codes[1, j], codes[2, j]
-        out[j, 32:56, :] = first[adapter, 0:24, :]
-        tile = first[owner, 24:32, :].astype(F32)
-        picked = jnp.sum(jnp.where(lines == slot, tile, 0.0), axis=0, keepdims=True)
-        out[j, 56:64, :] = jnp.broadcast_to(picked, (8, 128)).astype(BF16)
-        return carry
-
-    lax.fori_loop(0, 64, body, 0, unroll=8)
-
-
-def pack_third(codes, second, out):
-    def body(j, carry):
-        out[j] = second[codes[1, j]]
+        owner = codes[1, j]
+        out[j, 0:24, :] = second[owner, 0:24, :]
+        rest = first[owner, 24:32, :].astype(F32)
+        rest = jnp.where(codes[2, j] == 0, pltpu.roll(rest, 2, 0), rest)
+        out[j, 24:32, :] = jnp.where(lines >= 6, rest, second[owner, 24:32, :].astype(F32)).astype(BF16)
         return carry
 
     lax.fori_loop(0, 64, body, 0, unroll=8)
@@ -95,7 +119,7 @@
     step_t[...] = size.T[0:32, :]
 
 
-def widen_kernel(decay, step, gate, carry):
+def widen_kernel(decay, step, gate, carry, kept):
     block = pl.program_id(0)
     total = decay[...]
     grow = jnp.exp(total)
@@ -108,6 +132,8 @@
         at = slice(pair * 128, pair * 128 + 128)
         gate[:, at] = jnp.where(left, grow[:, lo : lo + 1], grow[:, hi : hi + 1])
         carry[:, at] = jnp.where(left, keep[:, lo : lo + 1], keep[:, hi : hi + 1])
+    for head in range(4):
+        kept[head * 64 : head * 64 + 64, :] = jnp.broadcast_to(grow[255:256, head : head + 1], (64, 128))
 
 
 def silu(v):
@@ -116,7 +142,7 @@
 
 def history(convs, index):
     lines = lax.broadcasted_iota(jnp.int32, (8, 128), 0)
-    old = [convs[i].astype(F32) for i in index]
+    old = [convs[i].astype(F32)[6:7, :] for i in index]
     return jnp.where(lines == 5, old[0], jnp.where(lines == 6, old[1], old[2]))
 
 
@@ -182,35 +208,47 @@
     fresh[...] = lax.dot_general(carried, b_proj[...], (((0,), (0,)), ((), ())), preferred_element_type=F32)
 
 
-def state_kernel(state, c_proj, part, gate, fresh, kept, gain, down, normed, low, updated, mixed):
+def state_kernel(state, c_far, part_far, gate_far, gain, panels, normed, low, mixed, part, gate, tile, c_proj, sems):
+    fetch = pltpu.make_async_copy(c_far, c_proj, sems.at[0, 8])
+    fetch.start()
+    copies = []
+    for block in range(8):
+        at = pl.ds(block * 256, 256)
+        copies.append(pltpu.make_async_copy(part_far.at[:, at], part.at[:, at], sems.at[0, block]))
+        copies.append(pltpu.make_async_copy(gate_far.at[:, at], gate.at[:, at], sems.at[1, block]))
+    for copy in copies:
+        copy.start()
+    fetch.wait()
     c_value = c_proj[...]
     square = jnp.zeros((256, 128), F32)
     for block in range(8):
         at = slice(block * 256, block * 256 + 256)
         old = state[block * 8 : block * 8 + 8].reshape(256, 128)
         inter = lax.dot_general(c_value, old, (((1,), (1,)), ((), ())), preferred_element_type=F32)
+        copies[2 * block].wait()
+        copies[2 * block + 1].wait()
         total = part[:, at] + inter * gate[:, at]
         mixed[:, at] = total
         square = square + total[:, 0:128] * total[:, 0:128] + total[:, 128:256] * total[:, 128:256]
-        updated[0, at, :] = (fresh[at, :] + kept[at, :] * old.astype(F32)).astype(BF16)
     mean = jnp.sum(square, axis=1, keepdims=True) * (1.0 / 2048.0)
     scale = lax.rsqrt(mean + NORM_EPSILON)
-    sums = []
-    for side in range(2):
-        acc = jnp.zeros((256, 128), F32)
-        for block in range(4):
-            start = side * 1024 + block * 256
-            at = slice(start, start + 256)
-            value = (mixed[:, at] * scale * gain[:, at]).astype(BF16)
-            normed[:, at] = value
-            panel = down[block * 16 : block * 16 + 16].reshape(256, 128)
-            acc = acc + jnp.dot(value, panel, preferred_element_type=F32)
-        sums.append(acc)
-    both = sums[0] + pltpu.roll(sums[1], 64, 1)
-    left = lax.broadcasted_iota(jnp.int32, (128, 128), 1) < 64
-    packed = jnp.where(left, both[0:128], pltpu.roll(both[128:256], 64, 1)).astype(BF16)
-    for peer in range(8):
-        low[peer] = packed
+    acc = jnp.zeros((256, 64), F32)
+    for col in range(16):
+        at = slice(col * 128, col * 128 + 128)
+        value = (mixed[:, at] * scale * gain[:, at]).astype(BF16)
+        normed[:, at] = value
+        panel = panels[col * 4 : col * 4 + 4, 32:48, :].reshape(64, 128)
+        acc = acc + lax.dot_general(value, panel, (((1,), (1,)), ((), ())), preferred_element_type=F32)
+    tile[...] = jnp.concatenate([acc[0:128], acc[128:256]], axis=1).astype(BF16)
+    copies = [pltpu.make_async_copy(tile, low.at[peer], sems.at[0, peer]) for peer in range(8)]
+    for copy in copies:
+        copy.start()
+    for copy in copies:
+        copy.wait()
+
+
+def update_kernel(state, fresh, kept, updated):
+    updated[0] = (fresh[...] + kept[...] * state[...].reshape(2048, 128).astype(F32)).astype(BF16)
 
 
 def up_kernel(parts, up, out):
@@ -220,7 +258,7 @@
     reduced = total.astype(BF16)
     halves = [reduced[:, 0:64], reduced[:, 64:128]]
     for col in range(8):
-        panel = up[col * 8 : col * 8 + 8].astype(F32).reshape(64, 128).astype(BF16)
+        panel = up[col * 8 : col * 8 + 8, 48:56, :].astype(F32).reshape(64, 128).astype(BF16)
         at = slice(col * 128, col * 128 + 128)
         for half in range(2):
             value = jnp.dot(halves[half], panel, preferred_element_type=F32) * ADAPTER_SCALE
@@ -253,17 +291,29 @@
 ):
     hold = lax.optimization_barrier
     packed = jax.ShapeDtypeStruct
+    whole = lambda *shape: pl.BlockSpec(shape, lambda i: (0,) * len(shape))
+    far = pl.BlockSpec(memory_space=pltpu.HBM)
+    states = cached_ssm_states.reshape(2, 64, 32, 128)
     sent1 = pl.pallas_call(
         pack_first,
         out_shape=packed((64, 32, 128), BF16),
-        in_specs=[smem()] * 4 + [vmem()] * 4,
-        out_specs=vmem(),
-        compiler_params=params(),
+        grid=(1,),
+        in_specs=[smem()] * 4
+        + [
+            whole(64, 2048),
+            whole(1, 64, 1024),
+            whole(3, 2, 2048),
+            whole(2, 3, 1, 2, 128),
+            pl.BlockSpec((2, 64, 8, 128), lambda i: (0, 0, 3, 0)),
+        ],
+        out_specs=whole(64, 32, 128),
+        compiler_params=params(60),
         cost_estimate=cost(0, 2 << 20),
         name="pack_first",
     )(
         tenant, tenant_adapter_row, cache_holder_index, cache_slot_index,
-        adapter_down_panels, adapter_up_panels, inner_conv_cache, projection_conv_cache,
+        jnp.swapaxes(adapter_down_panels, 1, 2).reshape(64, 2048), adapter_up_panels,
+        jnp.swapaxes(inner_conv_cache, 0, 1), projection_conv_cache, states,
     )
     sent1, raw = hold((sent1, step_before_bias))
     got1 = exchange(sent1, "req")
@@ -278,57 +328,42 @@
         name="steps",
     )(raw, step_bias.reshape(1, 32), rate)
     skip_wide = jnp.repeat(head_skip_gain, 64).reshape(1, 2048)
-    got1, decay, skip_wide = hold((got1, decay, skip_wide))
-
-    me = lax.axis_index("req")
-    words = got1[:, 26:29, 0].astype(jnp.int32)
-    mine = jnp.sum(jnp.where(words[:, 1] == me, words[:, 2], 0))
-    codes = jnp.concatenate([words.T, jnp.broadcast_to(mine, (1, 64))], axis=0)
-    states = cached_ssm_states.reshape(2, 64, 32, 128)
-    sent2 = pl.pallas_call(
+    me = lax.axis_index("req").astype(jnp.int32).reshape(1)
+    got1, decay, skip_wide, me = hold((got1, decay, skip_wide, me))
+
+    sent2, codes = pl.pallas_call(
         pack_second,
-        out_shape=packed((64, 64, 128), BF16),
-        grid_spec=pltpu.PrefetchScalarGridSpec(
-            num_scalar_prefetch=1,
-            grid=(1,),
-            in_specs=[
-                pl.BlockSpec((64, 32, 128), lambda i, c: (0, 0, 0)),
-                pl.BlockSpec((1, 64, 32, 128), lambda i, c: (c[3, 0], 0, 0, 0)),
-            ],
-            out_specs=pl.BlockSpec((64, 64, 128), lambda i, c: (0, 0, 0)),
-        ),
-        compiler_params=params(),
+        out_shape=[packed((64, 56, 128), BF16), packed((8, 128), jnp.int32)],
+        in_specs=[smem(), vmem(), pl.BlockSpec(memory_space=pl.ANY)],
+        out_specs=[vmem(), smem()],
+        scratch_shapes=[pltpu.VMEM((8, 128), jnp.int32), pltpu.SemaphoreType.DMA((2,))],
+        compiler_params=params(52),
         cost_estimate=cost(0, 3 << 20),
         name="pack_second",
-    )(codes, got1, states)
+    )(me, got1, states)
     sent2, decay, step = hold((sent2, decay, step))
     got2 = exchange(sent2, "req")
-    gate, carry = pl.pallas_call(
+    gate, carry, kept = pl.pallas_call(
         widen_kernel,
-        out_shape=[packed((256, 2048), F32)] * 2,
+        out_shape=[packed((256, 2048), F32)] * 2 + [packed((2048, 128), F32)],
         grid=(8,),
         in_specs=[pl.BlockSpec((256, 128), lambda i: (0, 0))] * 2,
-        out_specs=[pl.BlockSpec((256, 256), lambda i: (0, i))] * 2,
+        out_specs=[pl.BlockSpec((256, 256), lambda i: (0, i))] * 2 + [pl.BlockSpec((256, 128), lambda i: (i, 0))],
         compiler_params=params(),
         cost_estimate=cost(0, 6 << 20),
         name="widen",
     )(decay, step)
-    kept = jnp.broadcast_to(gate[255:256, :].reshape(2048, 1), (2048, 128))
     got2, gate, carry, kept = hold((got2, gate, carry, kept))
 
     sent3 = pl.pallas_call(
         pack_third,
         out_shape=packed((64, 32, 128), BF16),
-        grid_spec=pltpu.PrefetchScalarGridSpec(
-            num_scalar_prefetch=1,
-            grid=(1,),
-            in_specs=[pl.BlockSpec((64, 32, 128), lambda i, c: (0, 0, 0))],
-            out_specs=pl.BlockSpec((64, 32, 128), lambda i, c: (0, 0, 0)),
-        ),
-        compiler_params=params(),
+        in_specs=[smem(), vmem(), vmem()],
+        out_specs=vmem(),
+        compiler_params=params(52),
         cost_estimate=cost(0, 1 << 20),
         name="pack_third",
-    )(codes, got2)
+    )(codes, got1, got2)
     sent3, got2 = hold((sent3, got2))
     got3 = exchange(sent3, "req")
     part, c_proj, fresh = pl.pallas_call(
@@ -340,7 +375,7 @@
             pl.BlockSpec((256, 256), lambda i: (0, 0)),
             pl.BlockSpec((4, 256), lambda i: (0, i)),
             pl.BlockSpec((4, 256), lambda i: (0, 0)),
-            pl.BlockSpec((64, 8, 128), lambda i: (0, 7, 0)),
+            pl.BlockSpec((64, 8, 128), lambda i: (0, 3, 0)),
             pl.BlockSpec((1, 256), lambda i: (0, i)),
             pl.BlockSpec((256, 128), lambda i: (0, 0)),
             pl.BlockSpec((32, 256), lambda i: (0, 0)),
@@ -367,40 +402,35 @@
     )
     got3, part, c_proj, fresh = hold((got3, part, c_proj, fresh))
 
-    normed, low, updated = pl.pallas_call(
+    normed, low = pl.pallas_call(
         state_kernel,
-        out_shape=[packed((256, 2048), BF16), packed((8, 128, 128), BF16), packed((1, 2048, 128), BF16)],
+        out_shape=[packed((256, 2048), BF16), packed((8, 128, 128), BF16)],
         grid=(1,),
-        in_specs=[
-            pl.BlockSpec((64, 32, 128), lambda i: (0, 0, 0)),
-            pl.BlockSpec((256, 128), lambda i: (0, 0)),
-            pl.BlockSpec((256, 2048), lambda i: (0, 0)),
-            pl.BlockSpec((256, 2048), lambda i: (0, 0)),
-            pl.BlockSpec((2048, 128), lambda i: (0, 0)),
-            pl.BlockSpec((2048, 128), lambda i: (0, 0)),
-            pl.BlockSpec((1, 2048), lambda i: (0, 0)),
-            pl.BlockSpec((64, 16, 128), lambda i: (0, 2, 0)),
-        ],
-        out_specs=[
-            pl.BlockSpec((256, 2048), lambda i: (0, 0)),
-            pl.BlockSpec((8, 128, 128), lambda i: (0, 0, 0)),
-            pl.BlockSpec((1, 2048, 128), lambda i: (0, 0, 0)),
-        ],
-        scratch_shapes=[pltpu.VMEM((256, 2048), F32)],
-        compiler_params=params(),
+        in_specs=[whole(64, 32, 128), far, far, far, whole(1, 2048), whole(64, 56, 128)],
+        out_specs=[whole(256, 2048), far],
+        scratch_shapes=[pltpu.VMEM((256, 2048), F32)] * 3
+        + [pltpu.VMEM((128, 128), BF16), pltpu.VMEM((256, 128), BF16), pltpu.SemaphoreType.DMA((2, 9))],
+        compiler_params=params(50),
         cost_estimate=cost(1 << 28, 8 << 20),
         name="state",
-    )(got3, c_proj, part, gate, fresh, kept, group_norm_gain.reshape(1, 2048), got2)
+    )(got3, c_proj, part, gate, group_norm_gain.reshape(1, 2048), got2)
+    low, fresh = hold((low, fresh))
     parts = exchange(low, "head")
+    updated = pl.pallas_call(
+        update_kernel,
+        out_shape=packed((1, 2048, 128), BF16),
+        in_specs=[vmem()] * 3,
+        out_specs=vmem(),
+        compiler_params=params(),
+        cost_estimate=cost(1 << 20, 3 << 20),
+        name="update",
+    )(got3, fresh, kept)
+    parts, updated = hold((parts, updated))
     term = pl.pallas_call(
         up_kernel,
         out_shape=packed((256, 1024), BF16),
-        grid=(1,),
-        in_specs=[
-            pl.BlockSpec((8, 128, 128), lambda i: (0, 0, 0)),
-            pl.BlockSpec((64, 8, 128), lambda i: (0, 6, 0)),
-        ],
-        out_specs=pl.BlockSpec((256, 1024), lambda i: (0, 0)),
+        in_specs=[vmem()] * 2,
+        out_specs=vmem(),
         compiler_params=params(),
         cost_estimate=cost(1 << 26, 1 << 20),
         name="up",

time: 185 us -> 175 us (0.946)
  blocking collectives: 16.3 us -> 0 us
  starting transfers between devices: 35.8 us -> 45.2 us
  waiting for transfers between devices: 90.6 us -> 84.4 us
  Pallas kernels: 21.7 us -> 25.2 us
    all_to_all x1 -> x0, blocking collectives: 16.3 us -> none  [exchange(): return lax.all_to_all(value, axis, split_axis=0, concat_axis=0, tiled=True)]
    all_to_all x3 -> x4, starting transfers between devices: 35.8 us -> 45.2 us  [exchange(): return lax.all_to_all(value, axis, split_axis=0, concat_axis=0, tiled=True)]
    all_to_all x3 -> x4, waiting for transfers between devices: 90.6 us -> 84.4 us  [exchange(): return lax.all_to_all(value, axis, split_axis=0, concat_axis=0, tiled=True)]
    pallas_call x5 -> x6, Pallas kernels: 9.81 us -> 13 us  [the longest x1 3.84 us: per_device(): pl.pallas_call(widen_kernel, out_shape=[packed((256, 2048), F32)] * 2 + [...]
    unnamed x42 -> x52, local copies, waits for them, and re-layouts: 13.2 us -> 16 us
  transfers between devices with their start and end apart: 3 -> 4, of which waited for: 3 -> 4; matrix products, arithmetic and copies ran while one was open for 0% -> 0% of each run, Pallas kernels for 7% -> 7%
where the time goes in v2:
time: 175 us; the launch traced here: 174 us
  waiting for transfers between devices  84.4 us (48%)
  starting transfers between devices  45.2 us (26%)
  Pallas kernels  25.2 us (14%)
  local copies, waits for them, and re-layouts  16.3 us (9%)
  between operations  2.84 us (2%)
    all_to_all x4, waiting for transfers between devices, exchange(): return lax.all_to_all(value, axis, split_axis=0, concat_axis=0, tiled=True)  84.4 us
    all_to_all x4, starting transfers between devices, exchange(): return lax.all_to_all(value, axis, split_axis=0, concat_axis=0, tiled=True)  45.2 us
    unnamed x52, local copies, waits for them, and re-layouts  16 us
    pallas_call x1, Pallas kernels, per_device(): pl.pallas_call(mix_kernel, out_shape=[packed((256, 2048), F32), packed((2...  6.51 us
    pallas_call x1, Pallas kernels, per_device(): pl.pallas_call(state_kernel, out_shape=[packed((256, 2048), BF16), packed...  5.24 us
    pallas_call x1, Pallas kernels, per_device(): pl.pallas_call(widen_kernel, out_shape=[packed((256, 2048), F32)] * 2 + [...  3.84 us
  transfers between devices with their start and end apart: 4, of which 4 were waited for; matrix products, arithmetic and copies ran while one was open for 0% of the time, Pallas kernels for 7%

profile of v2, /device:TPU:1, one launch (start us, length us, event | category | flops | bytes accessed | tf_op | source)
XLA Modules:
  0.0 173.8 jit_solution(558654192695397165)
XLA Ops:
  2.6 2.1 %pack_first.1 = bf16[64,32,128]{2,1,0:T(8,128)(2,1)} custom-call(s32[1]{0:T(128)S(6)} %copy.28.tenant, s32[64]{0:T(128)} %table.1, s32[1]{0:T(128)S(6)} %copy.29.owner, s32[1]{0:T(128)S(6)} %copy.30.slot, bf16[64,2048]{1,0:T(8,128)(2,1)} %bitcast.28, bf16[1,64,1024]{2,1,0:T(8,128)(2,1)} %up.2, bf16[3,2,2048]{2,1,0:T(2,128)(2,1)} %bitcast.30, ...), custom_call_target="tpu_custom_call" | custom-call | bytes 2097152 | tf_op jit(solution)/shard_map/pack_first/pallas_call | solution.py:297
  4.7 19.3 %all-to-all-start = ((bf16[64,32,128]{2,1,0:T(8,128)(2,1)}), bf16[64,32,128]{2,1,0:T(8,128)(2,1)S(1)}, u32[]{:S(2)}, u32[]{:S(2)}) async-start(bf16[64,32,128]{2,1,0:T(8,128)(2,1)} %pack_first.1), calls=%async_computation | async-start | bytes 1048576 | tf_op jit(solution)/shard_map/all_to_all | solution.py:269
  24.7 0.6 copy-done.16
  25.3 28.7 %all-to-all-done.first = bf16[64,32,128]{2,1,0:T(8,128)(2,1)S(1)} async-done(((bf16[64,32,128]{2,1,0:T(8,128)(2,1)}), bf16[64,32,128]{2,1,0:T(8,128)(2,1)S(1)}, u32[]{:S(2)}, u32[]{:S(2)}) %all-to-all-start) | async-done | bytes 524320 | tf_op jit(solution)/shard_map/all_to_all | solution.py:269
  54.0 3.3 %pack_second.1 = (bf16[64,56,128]{2,1,0:T(8,128)(2,1)}, s32[8,128]{1,0:T(8,128)S(1)}) custom-call(s32[1]{0:T(128)} %bitcast.6.me, bf16[64,32,128]{2,1,0:T(8,128)(2,1)S(1)} %all-to-all-done.first, bf16[2,64,32,128]{3,2,1,0:T(8,128)(2,1)} %bitcast.26), custom_call_target="tpu_custom_call" | custom-call | bytes 3145728 | tf_op jit(solution)/shard_map/pack_second/pallas_call | solution.py:334
  57.3 7.9 %all-to-all-start.1 = ((bf16[64,56,128]{2,1,0:T(8,128)(2,1)}), bf16[64,56,128]{2,1,0:T(8,128)(2,1)S(1)}, u32[]{:S(2)}, u32[]{:S(2)}) async-start(bf16[64,56,128]{2,1,0:T(8,128)(2,1)} %get-tuple-element.49), calls=%async_computation.1 | async-start | bytes 1835008 | tf_op jit(solution)/shard_map/all_to_all | solution.py:269
  65.2 3.8 %widen.1 = (f32[256,2048]{1,0:T(8,128)S(1)}, f32[256,2048]{1,0:T(8,128)S(1)}, f32[2048,128]{1,0:T(8,128)S(1)}) custom-call(f32[256,128]{1,0:T(8,128)S(1)} %get-tuple-element.50.decay, f32[256,128]{1,0:T(8,128)S(1)} %get-tuple-element.51.step), custom_call_target="tpu_custom_call" | custom-call | bytes 6291456 | tf_op jit(solution)/shard_map/widen/pallas_call | solution.py:346
  69.1 1.3 copy-done
  70.4 1.0 copy-done.1
  71.5 1.3 copy-done.11
  72.8 37.6 %all-to-all-done.1.second.convs.panels.up = bf16[64,56,128]{2,1,0:T(8,128)(2,1)S(1)} async-done(((bf16[64,56,128]{2,1,0:T(8,128)(2,1)}), bf16[64,56,128]{2,1,0:T(8,128)(2,1)S(1)}, u32[]{:S(2)}, u32[]{:S(2)}) %all-to-all-start.1) | async-done | bytes 917536 | tf_op jit(solution)/shard_map/all_to_all | solution.py:269
  110.4 1.7 %pack_third.1 = bf16[64,32,128]{2,1,0:T(8,128)(2,1)} custom-call(s32[8,128]{1,0:T(8,128)S(1)} %get-tuple-element.45.codes, bf16[64,32,128]{2,1,0:T(8,128)(2,1)S(1)} %all-to-all-done.first, bf16[64,56,128]{2,1,0:T(8,128)(2,1)S(1)} %all-to-all-done.1.second.convs.panels.up), custom_call_target="tpu_custom_call" | custom-call | bytes 1048576 | tf_op jit(solution)/shard_map/pack_third/pallas_call | solution.py:358
  112.2 9.0 %all-to-all-start.2 = ((bf16[64,32,128]{2,1,0:T(8,128)(2,1)}), bf16[64,32,128]{2,1,0:T(8,128)(2,1)S(1)}, u32[]{:S(2)}, u32[]{:S(2)}) async-start(bf16[64,32,128]{2,1,0:T(8,128)(2,1)} %pack_third.1), calls=%async_computation.2 | async-start | bytes 1048576 | tf_op jit(solution)/shard_map/all_to_all | solution.py:269
  121.2 0.9 copy-done.7
  122.1 1.6 copy-done.12
  123.7 1.2 copy-done.13
  124.9 0.8 copy-done.14
  125.7 0.8 copy-done.17
  126.5 0.8 copy-done.19
  127.2 6.5 %mix.1 = (f32[256,2048]{1,0:T(8,128)S(1)}, bf16[256,128]{1,0:T(8,128)(2,1)S(1)}, f32[2048,128]{1,0:T(8,128)S(1)}) custom-call(bf16[256,2048]{1,0:T(8,128)(2,1)S(1)} %copy-done.13, bf16[256,256]{1,0:T(8,128)(2,1)S(1)} %bitcast.21, f32[4,2048]{1,0:T(4,128)S(1)} %copy-done.14, f32[4,256]{1,0:T(4,128)S(1)} %bitcast.23, ...), custom_call_target="tpu_custom_call" | custom-call | flops 2147483648 | bytes 10485760 | tf_op jit(solution)/shard_map/mix/pallas_call | solution.py:369
  133.7 1.0 copy-done.3
  134.7 0.6 copy-done.8
  135.4 14.9 %all-to-all-done.2.state = bf16[64,32,128]{2,1,0:T(8,128)(2,1)S(1)} async-done(((bf16[64,32,128]{2,1,0:T(8,128)(2,1)}), bf16[64,32,128]{2,1,0:T(8,128)(2,1)S(1)}, u32[]{:S(2)}, u32[]{:S(2)}) %all-to-all-start.2) | async-done | bytes 524320 | tf_op jit(solution)/shard_map/all_to_all | solution.py:269
  150.3 0.8 copy-done.9
  151.1 5.2 %state.1 = (bf16[256,2048]{1,0:T(8,128)(2,1)}, bf16[8,128,128]{2,1,0:T(8,128)(2,1)S(1)}) custom-call(bf16[64,32,128]{2,1,0:T(8,128)(2,1)S(1)} %all-to-all-done.2.state, bf16[256,128]{1,0:T(8,128)(2,1)S(1)} %copy-done.9, f32[256,2048]{1,0:T(8,128)S(1)} %get-tuple-element.67.part_far, f32[256,2048]{1,0:T(8,128)} %copy-done, f32[1,2048]{1,0:T(1,128)S(1)} %bitcast.22, ...), custom_call_target="tpu_custom_call" | custom-call | flops 268435456 | bytes 8388608 | tf_op jit(solution)/shard_map/state/pallas_call | solution.py:405
  156.4 0.7 copy-done.5
  157.1 9.1 %all-to-all-start.3 = ((bf16[8,128,128]{2,1,0:T(8,128)(2,1)}), bf16[8,128,128]{2,1,0:T(8,128)(2,1)S(1)}, u32[]{:S(2)}, u32[]{:S(2)}) async-start(bf16[8,128,128]{2,1,0:T(8,128)(2,1)} %copy-done.5), calls=%async_computation.3 | async-start | bytes 524288 | tf_op jit(solution)/shard_map/all_to_all | solution.py:269
  166.2 1.2 copy-done.2
  167.4 1.2 copy-done.4
  168.6 0.9 update.1
  169.6 3.1 %all-to-all-done.3.parts = bf16[8,128,128]{2,1,0:T(8,128)(2,1)S(1)} async-done(((bf16[8,128,128]{2,1,0:T(8,128)(2,1)}), bf16[8,128,128]{2,1,0:T(8,128)(2,1)S(1)}, u32[]{:S(2)}, u32[]{:S(2)}) %all-to-all-start.3) | async-done | bytes 262176 | tf_op jit(solution)/shard_map/all_to_all | solution.py:269
  172.7 1.1 up.3
  (41 shorter events, 0.7 us)
Async XLA Ops:
  0.6 23.6 %copy-start.21 = (bf16[256,32]{0,1:T(8,128)(2,1)S(1)}, bf16[256,32]{0,1:T(8,128)(2,1)}, u32[]{:S(2)}) copy-start(bf16[256,32]{0,1:T(8,128)(2,1)} %param.20) | copy-start | bytes 49156
  0.6 23.4 %copy-start.23 = (f32[32]{0:T(128)S(1)}, f32[32]{0:T(128)}, u32[]{:S(2)}) copy-start(f32[32]{0:T(128)} %param.25) | copy-start | bytes 388
  0.7 23.7 %copy-start.24 = (f32[32]{0:T(128)S(1)}, f32[32]{0:T(128)}, u32[]{:S(2)}) copy-start(f32[32]{0:T(128)} %param.24) | copy-start | bytes 388
  0.7 23.7 %copy-start.15 = (f32[32]{0:T(128)S(1)}, f32[32]{0:T(128)}, u32[]{:S(2)}) copy-start(f32[32]{0:T(128)} %param.23) | copy-start | bytes 388
  4.7 49.3 %all-to-all-start = ((bf16[64,32,128]{2,1,0:T(8,128)(2,1)}), bf16[64,32,128]{2,1,0:T(8,128)(2,1)S(1)}, u32[]{:S(2)}, u32[]{:S(2)}) async-start(bf16[64,32,128]{2,1,0:T(8,128)(2,1)} %pack_first.1), calls=%async_computation | async-start | bytes 1048576 | tf_op jit(solution)/shard_map/all_to_all | solution.py:269
  24.7 0.6 copy-start.16
  25.3 32.0 %copy-start.18 = (f32[32,256]{1,0:T(8,128)}, f32[32,256]{1,0:T(8,128)S(1)}, u32[]{:S(2)}) copy-start(f32[32,256]{1,0:T(8,128)S(1)} %get-tuple-element.60.step_t) | copy-start | bytes 98308
  25.3 86.8 %copy-start.6 = (f32[256,128]{1,0:T(8,128)}, f32[256,128]{1,0:T(8,128)S(1)}, u32[]{:S(2)}) copy-start(f32[256,128]{1,0:T(8,128)S(1)} %get-tuple-element.50.decay) | copy-start | bytes 393220
  57.3 53.1 %all-to-all-start.1 = ((bf16[64,56,128]{2,1,0:T(8,128)(2,1)}), bf16[64,56,128]{2,1,0:T(8,128)(2,1)S(1)}, u32[]{:S(2)}, u32[]{:S(2)}) async-start(bf16[64,56,128]{2,1,0:T(8,128)(2,1)} %get-tuple-element.49), calls=%async_computation.1 | async-start | bytes 1835008 | tf_op jit(solution)/shard_map/all_to_all | solution.py:269
  65.2 55.9 %copy-start.22 = (f32[4,1,2,128]{3,2,1,0:T(2,128)S(1)}, f32[4,1,2,128]{3,2,1,0:T(2,128)}, u32[]{:S(2)}) copy-start(f32[4,1,2,128]{3,2,1,0:T(2,128)} %param.22) | copy-start | bytes 12292
  65.2 55.9 %copy-start.20 = (bf16[256,1,2,128]{3,2,1,0:T(2,128)(2,1)S(1)}, bf16[256,1,2,128]{3,2,1,0:T(2,128)(2,1)}, u32[]{:S(2)}) copy-start(bf16[256,1,2,128]{3,2,1,0:T(2,128)(2,1)} %param.19) | copy-start | bytes 393220
  69.1 1.4 copy-start
  70.4 1.0 copy-start.1
  71.5 1.3 copy-start.11
  112.2 38.1 %all-to-all-start.2 = ((bf16[64,32,128]{2,1,0:T(8,128)(2,1)}), bf16[64,32,128]{2,1,0:T(8,128)(2,1)S(1)}, u32[]{:S(2)}, u32[]{:S(2)}) async-start(bf16[64,32,128]{2,1,0:T(8,128)(2,1)} %pack_third.1), calls=%async_computation.2 | async-start | bytes 1048576 | tf_op jit(solution)/shard_map/all_to_all | solution.py:269
  121.2 0.9 copy-start.7
  122.1 1.6 copy-start.12
  123.7 1.2 copy-start.13
  124.9 0.8 copy-start.14
  125.7 0.8 copy-start.17
  126.5 0.8 copy-start.19
  127.2 23.1 %copy-start.10 = (f32[2048]{0:T(1024)S(1)}, f32[2048]{0:T(1024)}, u32[]{:S(2)}) copy-start(f32[2048]{0:T(1024)} %param.26) | copy-start | bytes 24580
  133.7 1.0 copy-start.3
  134.7 0.6 copy-start.8
  150.3 0.8 copy-start.9
  156.4 0.7 copy-start.5
  157.1 15.6 %all-to-all-start.3 = ((bf16[8,128,128]{2,1,0:T(8,128)(2,1)}), bf16[8,128,128]{2,1,0:T(8,128)(2,1)S(1)}, u32[]{:S(2)}, u32[]{:S(2)}) async-start(bf16[8,128,128]{2,1,0:T(8,128)(2,1)} %copy-done.5), calls=%async_computation.3 | async-start | bytes 524288 | tf_op jit(solution)/shard_map/all_to_all | solution.py:269
  166.2 1.2 copy-start.2
  167.4 1.2 copy-start.4

commit v3 on v2

--- a/solution.py
+++ b/solution.py
@@ -98,44 +98,6 @@
     lax.fori_loop(0, 64, body, 0, unroll=8)
 
 
-def steps_kernel(raw, bias, rate, decay, decay_t, step, step_t):
-    v = raw[...].astype(F32) + bias[...]
-    size = jnp.maximum(v, 0.0) + jnp.log(1.0 + jnp.exp(-jnp.abs(v)))
-    size = jnp.concatenate([size, jnp.zeros((256, 96), F32)], axis=1)
-    drop = -rate[...] * size
-    rows = lax.broadcasted_iota(jnp.int32, (256, 256), 0)
-    cols = lax.broadcasted_iota(jnp.int32, (256, 256), 1)
-    lower = (rows >= cols).astype(F32).astype(BF16)
-    high = drop.astype(BF16)
-    rest = drop - high.astype(F32)
-    middle = rest.astype(BF16)
-    low = (rest - middle.astype(F32)).astype(BF16)
-    total = jnp.dot(lower, low, preferred_element_type=F32)
-    total = total + jnp.dot(lower, middle, preferred_element_type=F32)
-    total = total + jnp.dot(lower, high, preferred_element_type=F32)
-    decay[...] = total
-    step[...] = size
-    decay_t[...] = total.T[0:32, :]
-    step_t[...] = size.T[0:32, :]
-
-
-def widen_kernel(decay, step, gate, carry, kept):
-    block = pl.program_id(0)
-    total = decay[...]
-    grow = jnp.exp(total)
-    keep = jnp.exp(total[255:256, :] - total) * step[...]
-    shift = lax.rem(128 - 4 * block, 128)
-    grow, keep = pltpu.roll(grow, shift, 1), pltpu.roll(keep, shift, 1)
-    left = lax.broadcasted_iota(jnp.int32, (256, 128), 1) < 64
-    for pair in range(2):
-        lo, hi = 2 * pair, 2 * pair + 1
-        at = slice(pair * 128, pair * 128 + 128)
-        gate[:, at] = jnp.where(left, grow[:, lo : lo + 1], grow[:, hi : hi + 1])
-        carry[:, at] = jnp.where(left, keep[:, lo : lo + 1], keep[:, hi : hi + 1])
-    for head in range(4):
-        kept[head * 64 : head * 64 + 64, :] = jnp.broadcast_to(grow[255:256, head : head + 1], (64, 128))
-
-
 def silu(v):
     return v / (1.0 + jnp.exp(-v))
 
@@ -146,66 +108,163 @@
     return jnp.where(lines == 5, old[0], jnp.where(lines == 6, old[1], old[2]))
 
 
-def conv(pad, taps):
-    out = taps[0:1, :] * pad[5:261, :]
+def conv(pad, taps, count):
+    out = taps[0:1, :] * pad[5 : 5 + count, :]
     for k in range(1, 4):
-        out = out + taps[k : k + 1, :] * pad[5 + k : 261 + k, :]
-    return silu(out).astype(BF16)
-
-
-def mix_kernel(
-    x, bc, taps, bc_taps, convs, skip, decay, decay_t, step_t, carry,
-    part, c_out, fresh, pad, pad_bc, score, b_proj,
+        out = out + taps[k : k + 1, :] * pad[5 + k : 5 + count + k, :]
+    return silu(out)
+
+
+def widened(value, lo, hi):
+    left = lax.broadcasted_iota(jnp.int32, (value.shape[0], 128), 1) < 64
+    return jnp.where(left, value[:, lo : lo + 1], value[:, hi : hi + 1])
+
+
+def wide_row(row):
+    return jnp.concatenate([row, jnp.zeros((1, 96), F32)], axis=1)
+
+
+def dots(a, b, left, right):
+    return lax.dot_general(a, b, (((left,), (right,)), ((), ())), preferred_element_type=F32)
+
+
+def scan_kernel(flag, x, bc, taps, bc_taps, raw, bias, rate, skip, *rest):
+    outs, (pad, pad_bc, score) = rest[-13:-3], rest[-3:]
+    old = rest[:-13]
+    part, gate, fresh, kept, c_out, b_out, decay, decay_t, step, step_t = outs
+    block = pl.program_id(0)
+    active = flag[0] == 1
+
+    if old:
+
+        @pl.when(jnp.logical_and(jnp.logical_not(active), block == 0))
+        def _():
+            for source, target in zip(old, outs):
+                target[...] = source[...]
+
+    @pl.when(jnp.logical_and(active, block == 0))
+    def _():
+        v = jnp.concatenate([raw[...].astype(F32), jnp.zeros((96, 256), F32)], axis=0).T + wide_row(bias[...])
+        size = jnp.maximum(v, 0.0) + jnp.log(1.0 + jnp.exp(-jnp.abs(v)))
+        drop = -wide_row(rate[...]) * size
+        rows = lax.broadcasted_iota(jnp.int32, (256, 256), 0)
+        cols = lax.broadcasted_iota(jnp.int32, (256, 256), 1)
+        lower = (rows >= cols).astype(F32).astype(BF16)
+        high = drop.astype(BF16)
+        spare = drop - high.astype(F32)
+        middle = spare.astype(BF16)
+        low = (spare - middle.astype(F32)).astype(BF16)
+        total = jnp.dot(lower, low, preferred_element_type=F32)
+        total = total + jnp.dot(lower, middle, preferred_element_type=F32)
+        total = total + jnp.dot(lower, high, preferred_element_type=F32)
+        decay[...] = total
+        step[...] = size
+        decay_t[...] = total.T[0:32, :]
+        step_t[...] = size.T[0:32, :]
+        pad_bc[0:8, :] = jnp.zeros((8, 256), F32)
+        pad_bc[8:264, :] = bc[...].astype(F32)
+        both = jnp.where(rows >= 3, conv(pad_bc, bc_taps, 256), 0.0).astype(BF16)
+        b_out[...] = both[:, 0:128]
+        c_out[...] = both[:, 128:256]
+        score[...] = dots(both[:, 128:256], both[:, 0:128], 1, 1)
+
+    @pl.when(active)
+    def _():
+        pad[0:8, :] = jnp.zeros((8, 256), F32)
+        pad[8:264, :] = x[...].astype(F32)
+        tall = lax.broadcasted_iota(jnp.int32, (256, 256), 0)
+        inner = jnp.where(tall >= 3, conv(pad, taps, 256), 0.0).astype(BF16)
+        total = decay[...]
+        shift = lax.rem(128 - 4 * block, 128)
+        moved = pltpu.roll(total, shift, 1)
+        grow = jnp.exp(moved)
+        keep = pltpu.roll(jnp.exp(total[255:256, :] - total) * step[...], shift, 1)
+        gains = pltpu.roll(jnp.broadcast_to(wide_row(skip[...]), (8, 128)), shift, 1)
+        rows = lax.broadcasted_iota(jnp.int32, (128, 128), 0)
+        cols = lax.broadcasted_iota(jnp.int32, (128, 128), 1)
+        causal = rows >= cols
+        left = cols < 64
+        wide = inner.astype(F32)
+        for pair in range(2):
+            lo, hi = 2 * pair, 2 * pair + 1
+            at = slice(pair * 128, pair * 128 + 128)
+            values = inner[:, at]
+            top, bottom = [], []
+            for head in (lo, hi):
+                here = moved[:, head : head + 1]
+                there = decay_t[pl.ds(4 * block + head, 1), :]
+                weight = step_t[pl.ds(4 * block + head, 1), :]
+                gap = here[0:128] - there[:, 0:128]
+                mix = score[0:128, 0:128] * jnp.exp(jnp.where(causal, gap, -jnp.inf)) * weight[:, 0:128]
+                top.append(jnp.dot(mix.astype(BF16), values[0:128], preferred_element_type=F32))
+                gap = here[128:256] - there[:, 0:128]
+                mix = score[128:256, 0:128] * jnp.exp(gap) * weight[:, 0:128]
+                early = mix.astype(BF16)
+                gap = here[128:256] - there[:, 128:256]
+                mix = score[128:256, 128:256] * jnp.exp(jnp.where(causal, gap, -jnp.inf)) * weight[:, 128:256]
+                both = jnp.concatenate([early, mix.astype(BF16)], axis=1)
+                bottom.append(jnp.dot(both, values, preferred_element_type=F32))
+            gain = widened(gains[0:1, :], lo, hi)
+            part[0:128, at] = jnp.where(left, top[0], top[1]) + gain * wide[0:128, at]
+            part[128:256, at] = jnp.where(left, bottom[0], bottom[1]) + gain * wide[128:256, at]
+            gate[:, at] = widened(grow, lo, hi)
+            carried = (wide[:, at] * widened(keep, lo, hi)).astype(BF16)
+            fresh[at, :] = dots(carried, b_out[...], 0, 0)
+        for head in range(4):
+            kept[head * 64 : head * 64 + 64, :] = jnp.broadcast_to(grow[255:256, head : head + 1], (64, 128))
+
+
+def early_rows(
+    x, bc, taps, bc_taps, convs, skip, c_main, decay, decay_t, step, step_t, part_in, fresh_in,
+    part, fresh, c_out, pad, pad_bc, score, b_proj,
 ):
     block = pl.program_id(0)
+    short = lax.broadcasted_iota(jnp.int32, (8, 256), 0) < 3
+    rest = jnp.zeros((120, 128), F32)
 
     @pl.when(block == 0)
     def _():
         for side in range(2):
             at = slice(side * 128, side * 128 + 128)
             pad_bc[0:8, at] = history(convs, [48 + side, 50 + side, 52 + side])
-        pad_bc[8:264, :] = bc[...].astype(F32)
-        both = conv(pad_bc, bc_taps)
-        b_proj[...] = both[:, 0:128]
-        c_out[...] = both[:, 128:256]
-        score[...] = lax.dot_general(both[:, 128:256], both[:, 0:128], (((1,), (1,)), ((), ())), preferred_element_type=F32)
+        pad_bc[8:16, :] = bc[0:8, :].astype(F32)
+        both = jnp.where(short, conv(pad_bc, bc_taps, 8), 0.0)
+        b_proj[...] = jnp.concatenate([both[:, 0:128], rest], axis=0).astype(BF16)
+        c_all = c_main[...].astype(F32)
+        c_all = jnp.concatenate([c_all[0:8] + both[:, 128:256], c_all[8:256]], axis=0).astype(BF16)
+        c_out[...] = c_all
+        score[...] = dots(c_all, b_proj[...], 1, 1)
 
     for half in range(2):
         at = slice(half * 128, half * 128 + 128)
         col = block * 2 + half
         pad[0:8, at] = history(convs, [col, col + 16, col + 32])
-    pad[8:264, :] = x[...].astype(F32)
-    inner = conv(pad, taps)
-    moved = pltpu.roll(decay[...], lax.rem(128 - 4 * block, 128), 1)
-    rows = lax.broadcasted_iota(jnp.int32, (128, 128), 0)
-    cols = lax.broadcasted_iota(jnp.int32, (128, 128), 1)
+    pad[8:16, :] = x[0:8, :].astype(F32)
+    inner = jnp.where(short, conv(pad, taps, 8), 0.0).astype(BF16).astype(F32)
+    total = decay[...]
+    shift = lax.rem(128 - 4 * block, 128)
+    moved = pltpu.roll(total, shift, 1)
+    keep = pltpu.roll(jnp.exp(total[255:256, :] - total[0:8, :]) * step[0:8, :], shift, 1)
+    gains = pltpu.roll(jnp.broadcast_to(wide_row(skip[...]), (8, 128)), shift, 1)
+    rows = lax.broadcasted_iota(jnp.int32, (256, 128), 0)
+    cols = lax.broadcasted_iota(jnp.int32, (256, 128), 1)
     causal = rows >= cols
     left = cols < 64
-    wide = inner.astype(F32)
     for pair in range(2):
+        lo, hi = 2 * pair, 2 * pair + 1
         at = slice(pair * 128, pair * 128 + 128)
-        values = inner[:, at]
-        top, bottom = [], []
-        for side in range(2):
-            head = 2 * pair + side
-            here = moved[:, head : head + 1]
-            there = decay_t[pl.ds(4 * block + head, 1), :]
-            weight = step_t[pl.ds(4 * block + head, 1), :]
-            gap = here[0:128] - there[:, 0:128]
-            mix = score[0:128, 0:128] * jnp.exp(jnp.where(causal, gap, -jnp.inf)) * weight[:, 0:128]
-            top.append(jnp.dot(mix.astype(BF16), values[0:128], preferred_element_type=F32))
-            gap = here[128:256] - there[:, 0:128]
-            mix = score[128:256, 0:128] * jnp.exp(gap) * weight[:, 0:128]
-            first = mix.astype(BF16)
-            gap = here[128:256] - there[:, 128:256]
-            mix = score[128:256, 128:256] * jnp.exp(jnp.where(causal, gap, -jnp.inf)) * weight[:, 128:256]
-            both = jnp.concatenate([first, mix.astype(BF16)], axis=1)
-            bottom.append(jnp.dot(both, values, preferred_element_type=F32))
-        gain = skip[:, at]
-        part[0:128, at] = jnp.where(left, top[0], top[1]) + gain * wide[0:128, at]
-        part[128:256, at] = jnp.where(left, bottom[0], bottom[1]) + gain * wide[128:256, at]
-    carried = (wide * carry[...]).astype(BF16)
-    fresh[...] = lax.dot_general(carried, b_proj[...], (((0,), (0,)), ((), ())), preferred_element_type=F32)
+        values = jnp.concatenate([inner[:, at], rest], axis=0).astype(BF16)
+        added = []
+        for head in (lo, hi):
+            gap = moved[:, head : head + 1] - decay_t[pl.ds(4 * block + head, 1), :][:, 0:128]
+            weight = step_t[pl.ds(4 * block + head, 1), :][:, 0:128]
+            mix = score[...] * jnp.exp(jnp.where(causal, gap, -jnp.inf)) * weight
+            added.append(jnp.dot(mix.astype(BF16), values, preferred_element_type=F32))
+        part[:, at] = part_in[:, at] + jnp.where(left, added[0], added[1])
+        part[0:8, at] = part[0:8, at] + widened(gains[0:1, :], lo, hi) * inner[:, at]
+        carried = (inner[:, at] * widened(keep, lo, hi)).astype(BF16).astype(F32)
+        carried = jnp.concatenate([carried, rest], axis=0).astype(BF16)
+        fresh[at, :] = fresh_in[at, :] + dots(carried, b_proj[...], 0, 0)
 
 
 def state_kernel(state, c_far, part_far, gate_far, gain, panels, normed, low, mixed, part, gate, tile, c_proj, sems):
@@ -315,21 +374,53 @@
         jnp.swapaxes(adapter_down_panels, 1, 2).reshape(64, 2048), adapter_up_panels,
         jnp.swapaxes(inner_conv_cache, 0, 1), projection_conv_cache, states,
     )
-    sent1, raw = hold((sent1, step_before_bias))
+    even = 1 - (lax.axis_index("head").astype(jnp.int32) & 1)
+    cols = lambda *shape: pl.BlockSpec(shape, lambda i: (0,) * (len(shape) - 1) + (i,))
+    scan_shapes = [
+        packed((256, 2048), F32), packed((256, 2048), F32), packed((2048, 128), F32), packed((2048, 128), F32),
+        packed((256, 128), BF16), packed((256, 128), BF16), packed((256, 128), F32), packed((32, 256), F32),
+        packed((256, 128), F32), packed((32, 256), F32),
+    ]
+    wide_at = lambda *shape: pl.BlockSpec(shape, lambda i, on: (0, i * on[0]))
+    tall_at = lambda *shape: pl.BlockSpec(shape, lambda i, on: (i * on[0], 0))
+    fixed = lambda *shape: pl.BlockSpec(shape, lambda i, on: (0, 0))
+    scan_specs = [
+        wide_at(256, 256), wide_at(256, 256), tall_at(256, 128), tall_at(256, 128),
+        fixed(256, 128), fixed(256, 128), fixed(256, 128), fixed(32, 256), fixed(256, 128), fixed(32, 256),
+    ]
+    scan_args = [
+        inner_input, projection_input.reshape(256, 256), inner_conv_taps, projection_conv_taps.reshape(4, 256),
+        step_before_bias.T, step_bias.reshape(1, 32), head_decay_rate.reshape(1, 32), head_skip_gain.reshape(1, 32),
+    ]
+
+    def scan(on, old, limit):
+        inputs = [
+            wide_at(256, 256), fixed(256, 256), wide_at(4, 256), fixed(4, 256), fixed(32, 256),
+            fixed(1, 32), fixed(1, 32), fixed(1, 32),
+        ]
+        return pl.pallas_call(
+            scan_kernel,
+            out_shape=scan_shapes,
+            grid_spec=pltpu.PrefetchScalarGridSpec(
+                num_scalar_prefetch=1,
+                grid=(8,),
+                in_specs=inputs + scan_specs[: len(old)],
+                out_specs=scan_specs,
+                scratch_shapes=[pltpu.VMEM((264, 256), F32), pltpu.VMEM((264, 256), F32), pltpu.VMEM((256, 256), F32)],
+            ),
+            input_output_aliases={9 + i: i for i in range(len(old))},
+            compiler_params=params(limit),
+            cost_estimate=cost(2 << 30, 10 << 20),
+            name="scan_late" if old else "scan_early",
+        )(on.reshape(1), *scan_args, *old)
+
+    early = scan(even, [], 60)
+    sent1, *early = hold((sent1, *early))
     got1 = exchange(sent1, "req")
-    rate = jnp.pad(head_decay_rate, (0, 96)).reshape(1, 128)
-    decay, decay_t, step, step_t = pl.pallas_call(
-        steps_kernel,
-        out_shape=[packed((256, 128), F32), packed((32, 256), F32), packed((256, 128), F32), packed((32, 256), F32)],
-        in_specs=[vmem()] * 3,
-        out_specs=[vmem()] * 4,
-        compiler_params=params(),
-        cost_estimate=cost(6 * 256 * 256 * 128, 1 << 20),
-        name="steps",
-    )(raw, step_bias.reshape(1, 32), rate)
-    skip_wide = jnp.repeat(head_skip_gain, 64).reshape(1, 2048)
+    late = scan(1 - even, early, 60)
     me = lax.axis_index("req").astype(jnp.int32).reshape(1)
-    got1, decay, skip_wide, me = hold((got1, decay, skip_wide, me))
+    got1, me, *late = hold((got1, me, *late))
+    part, gate, fresh, kept, c_main, b_main, decay, decay_t, step, step_t = late
 
     sent2, codes = pl.pallas_call(
         pack_second,
@@ -341,20 +432,7 @@
         cost_estimate=cost(0, 3 << 20),
         name="pack_second",
     )(me, got1, states)
-    sent2, decay, step = hold((sent2, decay, step))
     got2 = exchange(sent2, "req")
-    gate, carry, kept = pl.pallas_call(
-        widen_kernel,
-        out_shape=[packed((256, 2048), F32)] * 2 + [packed((2048, 128), F32)],
-        grid=(8,),
-        in_specs=[pl.BlockSpec((256, 128), lambda i: (0, 0))] * 2,
-        out_specs=[pl.BlockSpec((256, 256), lambda i: (0, i))] * 2 + [pl.BlockSpec((256, 128), lambda i: (i, 0))],
-        compiler_params=params(),
-        cost_estimate=cost(0, 6 << 20),
-        name="widen",
-    )(decay, step)
-    got2, gate, carry, kept = hold((got2, gate, carry, kept))
-
     sent3 = pl.pallas_call(
         pack_third,
         out_shape=packed((64, 32, 128), BF16),
@@ -366,39 +444,27 @@
     )(codes, got1, got2)
     sent3, got2 = hold((sent3, got2))
     got3 = exchange(sent3, "req")
-    part, c_proj, fresh = pl.pallas_call(
-        mix_kernel,
-        out_shape=[packed((256, 2048), F32), packed((256, 128), BF16), packed((2048, 128), F32)],
+    part, fresh, c_proj = pl.pallas_call(
+        early_rows,
+        out_shape=[packed((256, 2048), F32), packed((2048, 128), F32), packed((256, 128), BF16)],
         grid=(8,),
         in_specs=[
-            pl.BlockSpec((256, 256), lambda i: (0, i)),
-            pl.BlockSpec((256, 256), lambda i: (0, 0)),
-            pl.BlockSpec((4, 256), lambda i: (0, i)),
-            pl.BlockSpec((4, 256), lambda i: (0, 0)),
+            pl.BlockSpec((16, 256), lambda i: (0, i)), whole(16, 256), cols(4, 256), whole(4, 256),
             pl.BlockSpec((64, 8, 128), lambda i: (0, 3, 0)),
-            pl.BlockSpec((1, 256), lambda i: (0, i)),
-            pl.BlockSpec((256, 128), lambda i: (0, 0)),
-            pl.BlockSpec((32, 256), lambda i: (0, 0)),
-            pl.BlockSpec((32, 256), lambda i: (0, 0)),
-            pl.BlockSpec((256, 256), lambda i: (0, i)),
+            whole(1, 32), whole(256, 128), whole(256, 128), whole(32, 256), whole(256, 128), whole(32, 256),
+            cols(256, 256), pl.BlockSpec((256, 128), lambda i: (i, 0)),
         ],
-        out_specs=[
-            pl.BlockSpec((256, 256), lambda i: (0, i)),
-            pl.BlockSpec((256, 128), lambda i: (0, 0)),
-            pl.BlockSpec((256, 128), lambda i: (i, 0)),
+        out_specs=[cols(256, 256), pl.BlockSpec((256, 128), lambda i: (i, 0)), whole(256, 128)],
+        scratch_shapes=[
+            pltpu.VMEM((16, 256), F32), pltpu.VMEM((16, 256), F32),
+            pltpu.VMEM((256, 128), F32), pltpu.VMEM((128, 128), BF16),
         ],
-        scratch_shapes=[
-            pltpu.VMEM((264, 256), F32),
-            pltpu.VMEM((264, 256), F32),
-            pltpu.VMEM((256, 256), F32),
-            pltpu.VMEM((256, 128), BF16),
-        ],
-        compiler_params=params(),
-        cost_estimate=cost(2 << 30, 10 << 20),
-        name="mix",
+        compiler_params=params(52),
+        cost_estimate=cost(1 << 29, 8 << 20),
+        name="early_rows",
     )(
-        inner_input, projection_input.reshape(256, 256), inner_conv_taps, projection_conv_taps.reshape(4, 256),
-        got2, skip_wide, decay, decay_t, step_t, carry,
+        inner_input, scan_args[1], inner_conv_taps, scan_args[3], got2, scan_args[7], c_main,
+        decay, decay_t, step, step_t, part, fresh,
     )
     got3, part, c_proj, fresh = hold((got3, part, c_proj, fresh))
 
@@ -410,7 +476,7 @@
         out_specs=[whole(256, 2048), far],
         scratch_shapes=[pltpu.VMEM((256, 2048), F32)] * 3
         + [pltpu.VMEM((128, 128), BF16), pltpu.VMEM((256, 128), BF16), pltpu.SemaphoreType.DMA((2, 9))],
-        compiler_params=params(50),
+        compiler_params=params(52),
         cost_estimate=cost(1 << 28, 8 << 20),
         name="state",
     )(got3, c_proj, part, gate, group_norm_gain.reshape(1, 2048), got2)

time: 175 us -> 170 us (0.971)
  waiting for transfers between devices: 84.4 us -> 34.6 us
  blocking collectives: 0 us -> 48.2 us
  Pallas kernels: 25.2 us -> 37.8 us
  local copies, waits for them, and re-layouts: 16.3 us -> 5.08 us
  starting transfers between devices: 45.2 us -> 40.5 us
    all_to_all x4 -> x3, waiting for transfers between devices: 84.4 us -> 34.6 us  [exchange(): return lax.all_to_all(value, axis, split_axis=0, concat_axis=0, tiled=True)]
    all_to_all x0 -> x1, blocking collectives: none -> 48.2 us  [exchange(): return lax.all_to_all(value, axis, split_axis=0, concat_axis=0, tiled=True)]
    pallas_call x3, Pallas kernels: 10.7 us -> 22.6 us  [the longest x2 14.5 us: scan(): pl.pallas_call(scan_kernel, out_shape=scan_shapes, grid_spec=pltpu.Prefet...]
    unnamed x52 -> x32, local copies, waits for them, and re-layouts: 16 us -> 5.08 us
    all_to_all x4 -> x3, starting transfers between devices: 45.2 us -> 40.5 us  [exchange(): return lax.all_to_all(value, axis, split_axis=0, concat_axis=0, tiled=True)]
  transfers between devices with their start and end apart: 4 -> 3, of which waited for: 4 -> 3; matrix products, arithmetic and copies ran while one was open for 0% -> 0% of each run, Pallas kernels for 7% -> 13%
where the time goes in v3:
time: 170 us; the launch traced here: 169 us
  blocking collectives  48.2 us (28%)
  starting transfers between devices  40.5 us (24%)
  Pallas kernels  37.8 us (22%)
  waiting for transfers between devices  34.6 us (20%)
  local copies, waits for them, and re-layouts  5.08 us (3%)
  between operations  2.79 us (2%)
    all_to_all x1, blocking collectives, exchange(): return lax.all_to_all(value, axis, split_axis=0, concat_axis=0, tiled=True)  48.2 us
    all_to_all x3, starting transfers between devices, exchange(): return lax.all_to_all(value, axis, split_axis=0, concat_axis=0, tiled=True)  40.5 us
    all_to_all x3, waiting for transfers between devices, exchange(): return lax.all_to_all(value, axis, split_axis=0, concat_axis=0, tiled=True)  34.6 us
    pallas_call x2, Pallas kernels, scan(): pl.pallas_call(scan_kernel, out_shape=scan_shapes, grid_spec=pltpu.Prefet...  14.5 us
    pallas_call x1, Pallas kernels, per_device(): pl.pallas_call(early_rows, out_shape=[packed((256, 2048), F32), packed((2...  8.09 us
    pallas_call x1, Pallas kernels, per_device(): pl.pallas_call(state_kernel, out_shape=[packed((256, 2048), BF16), packed...  5.44 us
    unnamed x32, local copies, waits for them, and re-layouts  5.08 us
  transfers between devices with their start and end apart: 3, of which 3 were waited for; matrix products, arithmetic and copies ran while one was open for 0% of the time, Pallas kernels for 13%

profile of v3, /device:TPU:1, one launch (start us, length us, event | category | flops | bytes accessed | tf_op | source)
XLA Modules:
  0.0 169.0 jit_solution(16815262466175994212)
XLA Ops:
  2.6 1.3 copy.36
  3.8 1.6 copy.35
  5.4 2.1 %pack_first.1 = bf16[64,32,128]{2,1,0:T(8,128)(2,1)} custom-call(s32[1]{0:T(128)S(6)} %copy.47.tenant, s32[64]{0:T(128)} %table.1, s32[1]{0:T(128)S(6)} %copy.48.owner, s32[1]{0:T(128)S(6)} %copy.49.slot, bf16[64,2048]{1,0:T(8,128)(2,1)} %bitcast.37, bf16[1,64,1024]{2,1,0:T(8,128)(2,1)} %up.2, bf16[3,2,2048]{2,1,0:T(2,128)(2,1)} %bitcast.39, ...), custom_call_target="tpu_custom_call" | custom-call | bytes 2097152 | tf_op jit(solution)/shard_map/pack_first/pallas_call | solution.py:356
  7.5 2.1 %scan_early.1 = (f32[256,2048]{1,0:T(8,128)}, f32[256,2048]{1,0:T(8,128)}, f32[2048,128]{1,0:T(8,128)}, f32[2048,128]{1,0:T(8,128)}, bf16[256,128]{1,0:T(8,128)(...) custom-call(s32[1]{0:T(128)} %bitcast.4.flag, ...), custom_call_target="tpu_custom_call" | custom-call | flops 2147483648 | bytes 10485760 | tf_op jit(solution)/shard_map/scan_early/pallas_call | solution.py:401
  9.6 19.3 %all-to-all-start = ((bf16[64,32,128]{2,1,0:T(8,128)(2,1)}), bf16[64,32,128]{2,1,0:T(8,128)(2,1)S(1)}, u32[]{:S(2)}, u32[]{:S(2)}) async-start(bf16[64,32,128]{2,1,0:T(8,128)(2,1)} %pack_first.1), calls=%async_computation | async-start | bytes 1048576 | tf_op jit(solution)/shard_map/all_to_all | solution.py:328
  28.9 12.4 %scan_late.1 = (f32[256,2048]{1,0:T(8,128)}, f32[256,2048]{1,0:T(8,128)}, f32[2048,128]{1,0:T(8,128)}, f32[2048,128]{1,0:T(8,128)}, bf16[256,128]{1,0:T(8,128)(2...) custom-call(s32[1]{0:T(128)} %bitcast.10.flag, ...), custom_call_target="tpu_custom_call", output_to_operand_aliasing={{0}: (9, {}), {1}: (10, {}), {2}: (11, {}), {3}: (12, {}), ... | custom-call | flops 2147483648 | bytes 10485760 | tf_op jit(solution)/shard_map/scan_late/pallas_call | solution.py:401
  41.3 10.0 %all-to-all-done.first = bf16[64,32,128]{2,1,0:T(8,128)(2,1)S(1)} async-done(((bf16[64,32,128]{2,1,0:T(8,128)(2,1)}), bf16[64,32,128]{2,1,0:T(8,128)(2,1)S(1)}, u32[]{:S(2)}, u32[]{:S(2)}) %all-to-all-start) | async-done | bytes 524320 | tf_op jit(solution)/shard_map/all_to_all | solution.py:328
  51.3 3.0 %pack_second.1 = (bf16[64,56,128]{2,1,0:T(8,128)(2,1)S(1)}, s32[8,128]{1,0:T(8,128)S(1)}) custom-call(s32[1]{0:T(128)} %bitcast.9.me, bf16[64,32,128]{2,1,0:T(8,128)(2,1)S(1)} %all-to-all-done.first, bf16[2,64,32,128]{3,2,1,0:T(8,128)(2,1)} %bitcast.35), custom_call_target="tpu_custom_call" | custom-call | bytes 3145728 | tf_op jit(solution)/shard_map/pack_second/pallas_call | solution.py:425
  54.3 0.0 copy-start.1
  54.3 0.0 copy-start.3
  54.3 0.0 copy-start.4
  54.3 0.0 copy-start.5
  54.4 0.0 copy-start.7
  54.4 0.0 copy-start.8
  54.4 0.0 copy-start.9
  54.4 0.0 copy-start.14
  54.4 48.2 %all_to_all.20.second.convs.panels.up = bf16[64,56,128]{2,1,0:T(8,128)(2,1)S(1)} all-to-all(bf16[64,56,128]{2,1,0:T(8,128)(2,1)S(1)} %get-tuple-element.94), channel_id=1, replica_groups=mesh['req'=64,'head'=8] {'req'}, dimensions={0} | all-to-all | bytes 1835008 | tf_op jit(solution)/shard_map/all_to_all | solution.py:328
  102.6 1.7 %pack_third.1 = bf16[64,32,128]{2,1,0:T(8,128)(2,1)} custom-call(s32[8,128]{1,0:T(8,128)S(1)} %get-tuple-element.93.codes, bf16[64,32,128]{2,1,0:T(8,128)(2,1)S(1)} %all-to-all-done.first, bf16[64,56,128]{2,1,0:T(8,128)(2,1)S(1)} %all_to_all.20.second.convs.panels.up), custom_call_target="tpu_custom_call" | custom-call | bytes 1048576 | tf_op jit(solution)/shard_map/pack_third/pallas_call | solution.py:436
  104.4 10.9 %all-to-all-start.2 = ((bf16[64,32,128]{2,1,0:T(8,128)(2,1)}), bf16[64,32,128]{2,1,0:T(8,128)(2,1)S(1)}, u32[]{:S(2)}, u32[]{:S(2)}) async-start(bf16[64,32,128]{2,1,0:T(8,128)(2,1)} %pack_third.1), calls=%async_computation.2 | async-start | bytes 1048576 | tf_op jit(solution)/shard_map/all_to_all | solution.py:328
  115.4 0.0 copy-start.13
  115.4 8.1 %early_rows.1 = (f32[256,2048]{1,0:T(8,128)}, f32[2048,128]{1,0:T(8,128)}, bf16[256,128]{1,0:T(8,128)(2,1)S(1)}) custom-call(bf16[256,2048]{1,0:T(8,128)(2,1)} %x.5, bf16[256,256]{1,0:T(8,128)(2,1)S(1)} %bitcast.26, f32[4,2048]{1,0:T(4,128)S(1)} %copy-done.7, f32[4,256]{1,0:T(4,128)S(1)} %bitcast.29, ...), custom_call_target="tpu_custom_call" | custom-call | flops 536870912 | bytes 8388608 | tf_op jit(solution)/shard_map/early_rows/pallas_call | solution.py:447
  123.5 0.6 copy-done.10
  124.1 19.0 %all-to-all-done.2.state = bf16[64,32,128]{2,1,0:T(8,128)(2,1)S(1)} async-done(((bf16[64,32,128]{2,1,0:T(8,128)(2,1)}), bf16[64,32,128]{2,1,0:T(8,128)(2,1)S(1)}, u32[]{:S(2)}, u32[]{:S(2)}) %all-to-all-start.2) | async-done | bytes 524320 | tf_op jit(solution)/shard_map/all_to_all | solution.py:328
  143.1 0.8 copy-done.11
  143.9 5.4 %state.1 = (bf16[256,2048]{1,0:T(8,128)(2,1)}, bf16[8,128,128]{2,1,0:T(8,128)(2,1)S(1)}) custom-call(bf16[64,32,128]{2,1,0:T(8,128)(2,1)S(1)} %all-to-all-done.2.state, bf16[256,128]{1,0:T(8,128)(2,1)S(1)} %copy-done.11, f32[256,2048]{1,0:T(8,128)} %get-tuple-element.109.part_far, f32[256,2048]{1,0:T(8,128)} %get-tuple-element.110.gate_far, ...), custom_call_target="tpu_custom_call" | custom-call | flops 268435456 | bytes 8388608 | tf_op jit(solution)/shard_map/state/pallas_call | solution.py:471
  149.4 0.0 copy-start.6
  149.4 0.7 copy-done.6
  150.1 10.3 %all-to-all-start.3 = ((bf16[8,128,128]{2,1,0:T(8,128)(2,1)}), bf16[8,128,128]{2,1,0:T(8,128)(2,1)}, u32[]{:S(2)}, u32[]{:S(2)}) async-start(bf16[8,128,128]{2,1,0:T(8,128)(2,1)} %copy-done.6), calls=%async_computation.3 | async-start | bytes 524288 | tf_op jit(solution)/shard_map/all_to_all | solution.py:328
  160.3 0.0 copy-done
  160.3 0.9 update.1
  161.3 5.7 %all-to-all-done.3.parts = bf16[8,128,128]{2,1,0:T(8,128)(2,1)} async-done(((bf16[8,128,128]{2,1,0:T(8,128)(2,1)}), bf16[8,128,128]{2,1,0:T(8,128)(2,1)}, u32[]{:S(2)}, u32[]{:S(2)}) %all-to-all-start.3) | async-done | bytes 262176 | tf_op jit(solution)/shard_map/all_to_all | solution.py:328
  166.9 2.1 %up.3 = bf16[256,1024]{1,0:T(8,128)(2,1)} custom-call(bf16[8,128,128]{2,1,0:T(8,128)(2,1)} %all-to-all-done.3.parts, bf16[64,56,128]{2,1,0:T(8,128)(2,1)S(1)} %all_to_all.20.second.convs.panels.up), custom_call_target="tpu_custom_call" | custom-call | flops 67108864 | bytes 1048576 | tf_op jit(solution)/shard_map/up/pallas_call | solution.py:495
  (16 shorter events, 0.0 us)
Async XLA Ops:
  9.6 41.7 %all-to-all-start = ((bf16[64,32,128]{2,1,0:T(8,128)(2,1)}), bf16[64,32,128]{2,1,0:T(8,128)(2,1)S(1)}, u32[]{:S(2)}, u32[]{:S(2)}) async-start(bf16[64,32,128]{2,1,0:T(8,128)(2,1)} %pack_first.1), calls=%async_computation | async-start | bytes 1048576 | tf_op jit(solution)/shard_map/all_to_all | solution.py:328
  54.3 60.9 %copy-start.1 = (bf16[32,8,2,128]{3,1,2,0:T(8,128)(2,1)S(1)}, bf16[32,8,2,128]{3,1,2,0:T(8,128)(2,1)}, u32[]{:S(2)}) copy-start(bf16[32,8,2,128]{3,1,2,0:T(8,128)(2,1)} %copy.35) | copy-start | bytes 393220
  54.3 60.9 %copy-start.3 = (f32[256,128]{1,0:T(8,128)S(1)}, f32[256,128]{1,0:T(8,128)}, u32[]{:S(2)}) copy-start(f32[256,128]{1,0:T(8,128)} %get-tuple-element.98.decay) | copy-start | bytes 393220
  54.3 60.9 %copy-start.4 = (f32[256,128]{1,0:T(8,128)S(1)}, f32[256,128]{1,0:T(8,128)}, u32[]{:S(2)}) copy-start(f32[256,128]{1,0:T(8,128)} %get-tuple-element.100.step) | copy-start | bytes 393220
  54.3 60.9 %copy-start.5 = (bf16[256,128]{1,0:T(8,128)(2,1)S(1)}, bf16[256,128]{1,0:T(8,128)(2,1)}, u32[]{:S(2)}) copy-start(bf16[256,128]{1,0:T(8,128)(2,1)} %get-tuple-element.97.c_main) | copy-start | bytes 196612
  54.4 60.9 %copy-start.7 = (f32[4,2048]{1,0:T(4,128)S(1)}, f32[4,2048]{1,0:T(4,128)}, u32[]{:S(2)}) copy-start(f32[4,2048]{1,0:T(4,128)} %taps.5) | copy-start | bytes 98308
  54.4 60.9 %copy-start.8 = (f32[32,256]{1,0:T(8,128)S(1)}, f32[32,256]{1,0:T(8,128)}, u32[]{:S(2)}) copy-start(f32[32,256]{1,0:T(8,128)} %get-tuple-element.99.decay_t) | copy-start | bytes 98308
  54.4 60.9 %copy-start.9 = (f32[32,256]{1,0:T(8,128)S(1)}, f32[32,256]{1,0:T(8,128)}, u32[]{:S(2)}) copy-start(f32[32,256]{1,0:T(8,128)} %get-tuple-element.101.step_t) | copy-start | bytes 98308
  54.4 60.9 %copy-start.12 = (f32[1,4,2,128]{3,1,2,0:T(4,128)S(1)}, f32[1,4,2,128]{3,1,2,0:T(4,128)}, u32[]{:S(2)}) copy-start(f32[1,4,2,128]{3,1,2,0:T(4,128)} %copy.36) | copy-start | bytes 12292
  54.4 60.9 %copy-start.14 = (f32[32]{0:T(128)S(1)}, f32[32]{0:T(128)}, u32[]{:S(2)}) copy-start(f32[32]{0:T(128)} %param.25) | copy-start | bytes 388
  104.4 38.7 %all-to-all-start.2 = ((bf16[64,32,128]{2,1,0:T(8,128)(2,1)}), bf16[64,32,128]{2,1,0:T(8,128)(2,1)S(1)}, u32[]{:S(2)}, u32[]{:S(2)}) async-start(bf16[64,32,128]{2,1,0:T(8,128)(2,1)} %pack_third.1), calls=%async_computation.2 | async-start | bytes 1048576 | tf_op jit(solution)/shard_map/all_to_all | solution.py:328
  115.4 27.7 %copy-start.13 = (f32[2048]{0:T(1024)S(1)}, f32[2048]{0:T(1024)}, u32[]{:S(2)}) copy-start(f32[2048]{0:T(1024)} %param.26) | copy-start | bytes 24580
  123.5 0.6 copy-start.10
  143.1 0.8 copy-start.11
  143.9 16.4 %copy-start = (f32[2048,128]{1,0:T(8,128)S(1)}, f32[2048,128]{1,0:T(8,128)}, u32[]{:S(2)}) copy-start(f32[2048,128]{1,0:T(8,128)} %get-tuple-element.116.kept) | copy-start | bytes 3145732
  143.9 16.4 %copy-start.2 = (f32[2048,128]{1,0:T(8,128)S(1)}, f32[2048,128]{1,0:T(8,128)}, u32[]{:S(2)}) copy-start(f32[2048,128]{1,0:T(8,128)} %get-tuple-element.115.fresh) | copy-start | bytes 3145732
  149.4 0.7 copy-start.6
  150.1 16.9 %all-to-all-start.3 = ((bf16[8,128,128]{2,1,0:T(8,128)(2,1)}), bf16[8,128,128]{2,1,0:T(8,128)(2,1)}, u32[]{:S(2)}, u32[]{:S(2)}) async-start(bf16[8,128,128]{2,1,0:T(8,128)(2,1)} %copy-done.6), calls=%async_computation.3 | async-start | bytes 524288 | tf_op jit(solution)/shard_map/all_to_all | solution.py:328

commit v4 on v3

--- a/solution.py
+++ b/solution.py
@@ -115,6 +115,18 @@
     return silu(out)
 
 
+def conv_pair(pad, bc, taps, count):
+    sides = []
+    for side in range(2):
+        at = slice(side * 128, side * 128 + 128)
+        pad[8 : 8 + count, at] = bc[0:count, side, :].astype(F32)
+        out = taps[0, side : side + 1, :] * pad[5 : 5 + count, at]
+        for k in range(1, 4):
+            out = out + taps[k, side : side + 1, :] * pad[5 + k : 5 + count + k, at]
+        sides.append(silu(out))
+    return jnp.concatenate(sides, axis=1)
+
+
 def widened(value, lo, hi):
     left = lax.broadcasted_iota(jnp.int32, (value.shape[0], 128), 1) < 64
     return jnp.where(left, value[:, lo : lo + 1], value[:, hi : hi + 1])
@@ -162,8 +174,7 @@
         decay_t[...] = total.T[0:32, :]
         step_t[...] = size.T[0:32, :]
         pad_bc[0:8, :] = jnp.zeros((8, 256), F32)
-        pad_bc[8:264, :] = bc[...].astype(F32)
-        both = jnp.where(rows >= 3, conv(pad_bc, bc_taps, 256), 0.0).astype(BF16)
+        both = jnp.where(rows >= 3, conv_pair(pad_bc, bc, bc_taps, 256), 0.0).astype(BF16)
         b_out[...] = both[:, 0:128]
         c_out[...] = both[:, 128:256]
         score[...] = dots(both[:, 128:256], both[:, 0:128], 1, 1)
@@ -214,6 +225,16 @@
             kept[head * 64 : head * 64 + 64, :] = jnp.broadcast_to(grow[255:256, head : head + 1], (64, 128))
 
 
+def scan_first_kernel(flag, *refs):
+    pack_refs, scan_refs, sent, scratch = refs[:9], refs[9:27], refs[27], refs[28:]
+
+    @pl.when(pl.program_id(0) == 0)
+    def _():
+        pack_first(*pack_refs, sent)
+
+    scan_kernel(flag, *scan_refs, *scratch)
+
+
 def early_rows(
     x, bc, taps, bc_taps, convs, skip, c_main, decay, decay_t, step, step_t, part_in, fresh_in,
     part, fresh, c_out, pad, pad_bc, score, b_proj,
@@ -227,8 +248,7 @@
         for side in range(2):
             at = slice(side * 128, side * 128 + 128)
             pad_bc[0:8, at] = history(convs, [48 + side, 50 + side, 52 + side])
-        pad_bc[8:16, :] = bc[0:8, :].astype(F32)
-        both = jnp.where(short, conv(pad_bc, bc_taps, 8), 0.0)
+        both = jnp.where(short, conv_pair(pad_bc, bc, bc_taps, 8), 0.0)
         b_proj[...] = jnp.concatenate([both[:, 0:128], rest], axis=0).astype(BF16)
         c_all = c_main[...].astype(F32)
         c_all = jnp.concatenate([c_all[0:8] + both[:, 128:256], c_all[8:256]], axis=0).astype(BF16)
@@ -353,27 +373,11 @@
     whole = lambda *shape: pl.BlockSpec(shape, lambda i: (0,) * len(shape))
     far = pl.BlockSpec(memory_space=pltpu.HBM)
     states = cached_ssm_states.reshape(2, 64, 32, 128)
-    sent1 = pl.pallas_call(
-        pack_first,
-        out_shape=packed((64, 32, 128), BF16),
-        grid=(1,),
-        in_specs=[smem()] * 4
-        + [
-            whole(64, 2048),
-            whole(1, 64, 1024),
-            whole(3, 2, 2048),
-            whole(2, 3, 1, 2, 128),
-            pl.BlockSpec((2, 64, 8, 128), lambda i: (0, 0, 3, 0)),
-        ],
-        out_specs=whole(64, 32, 128),
-        compiler_params=params(60),
-        cost_estimate=cost(0, 2 << 20),
-        name="pack_first",
-    )(
+    pack_args = [
         tenant, tenant_adapter_row, cache_holder_index, cache_slot_index,
         jnp.swapaxes(adapter_down_panels, 1, 2).reshape(64, 2048), adapter_up_panels,
         jnp.swapaxes(inner_conv_cache, 0, 1), projection_conv_cache, states,
-    )
+    ]
     even = 1 - (lax.axis_index("head").astype(jnp.int32) & 1)
     cols = lambda *shape: pl.BlockSpec(shape, lambda i: (0,) * (len(shape) - 1) + (i,))
     scan_shapes = [
@@ -383,38 +387,44 @@
     ]
     wide_at = lambda *shape: pl.BlockSpec(shape, lambda i, on: (0, i * on[0]))
     tall_at = lambda *shape: pl.BlockSpec(shape, lambda i, on: (i * on[0], 0))
-    fixed = lambda *shape: pl.BlockSpec(shape, lambda i, on: (0, 0))
+    fixed = lambda *shape: pl.BlockSpec(shape, lambda i, on: (0,) * len(shape))
     scan_specs = [
         wide_at(256, 256), wide_at(256, 256), tall_at(256, 128), tall_at(256, 128),
         fixed(256, 128), fixed(256, 128), fixed(256, 128), fixed(32, 256), fixed(256, 128), fixed(32, 256),
     ]
     scan_args = [
-        inner_input, projection_input.reshape(256, 256), inner_conv_taps, projection_conv_taps.reshape(4, 256),
+        inner_input, projection_input.reshape(256, 2, 128), inner_conv_taps, projection_conv_taps.reshape(4, 2, 128),
         step_before_bias.T, step_bias.reshape(1, 32), head_decay_rate.reshape(1, 32), head_skip_gain.reshape(1, 32),
     ]
 
+    pack_specs = [smem()] * 4 + [
+        fixed(64, 2048), fixed(1, 64, 1024), fixed(3, 2, 2048), fixed(2, 3, 1, 2, 128),
+        pl.BlockSpec((2, 64, 8, 128), lambda i, on: (0, 0, 3, 0)),
+    ]
+
     def scan(on, old, limit):
         inputs = [
-            wide_at(256, 256), fixed(256, 256), wide_at(4, 256), fixed(4, 256), fixed(32, 256),
+            wide_at(256, 256), fixed(256, 2, 128), wide_at(4, 256), fixed(4, 2, 128), fixed(32, 256),
             fixed(1, 32), fixed(1, 32), fixed(1, 32),
         ]
+        first = not old
         return pl.pallas_call(
-            scan_kernel,
-            out_shape=scan_shapes,
+            scan_first_kernel if first else scan_kernel,
+            out_shape=scan_shapes + [packed((64, 32, 128), BF16)] * first,
             grid_spec=pltpu.PrefetchScalarGridSpec(
                 num_scalar_prefetch=1,
                 grid=(8,),
-                in_specs=inputs + scan_specs[: len(old)],
-                out_specs=scan_specs,
+                in_specs=pack_specs * first + inputs + scan_specs[: len(old)],
+                out_specs=scan_specs + [fixed(64, 32, 128)] * first,
                 scratch_shapes=[pltpu.VMEM((264, 256), F32), pltpu.VMEM((264, 256), F32), pltpu.VMEM((256, 256), F32)],
             ),
             input_output_aliases={9 + i: i for i in range(len(old))},
             compiler_params=params(limit),
             cost_estimate=cost(2 << 30, 10 << 20),
-            name="scan_late" if old else "scan_early",
-        )(on.reshape(1), *scan_args, *old)
-
-    early = scan(even, [], 60)
+            name="scan_early" if first else "scan_late",
+        )(on.reshape(1), *(pack_args * first), *scan_args, *old)
+
+    *early, sent1 = scan(even, [], 60)
     sent1, *early = hold((sent1, *early))
     got1 = exchange(sent1, "req")
     late = scan(1 - even, early, 60)
@@ -449,7 +459,7 @@
         out_shape=[packed((256, 2048), F32), packed((2048, 128), F32), packed((256, 128), BF16)],
         grid=(8,),
         in_specs=[
-            pl.BlockSpec((16, 256), lambda i: (0, i)), whole(16, 256), cols(4, 256), whole(4, 256),
+            pl.BlockSpec((16, 256), lambda i: (0, i)), whole(16, 2, 128), cols(4, 256), whole(4, 2, 128),
             pl.BlockSpec((64, 8, 128), lambda i: (0, 3, 0)),
             whole(1, 32), whole(256, 128), whole(256, 128), whole(32, 256), whole(256, 128), whole(32, 256),
             cols(256, 256), pl.BlockSpec((256, 128), lambda i: (i, 0)),

time: 170 us -> 169 us (level)
  blocking collectives: 48.2 us -> 52.1 us
  local copies, waits for them, and re-layouts: 5.08 us -> 2.23 us
    all_to_all x1, blocking collectives: 48.2 us -> 52.1 us  [exchange(): return lax.all_to_all(value, axis, split_axis=0, concat_axis=0, tiled=True)]
    unnamed x32 -> x30, local copies, waits for them, and re-layouts: 5.08 us -> 2.23 us
    pallas_call x3 -> x2, Pallas kernels: 16.6 us -> 16.8 us  [scan(): pl.pallas_call(scan_first_kernel if first else scan_kernel, out_shape=sca...]
where the time goes in v4:
time: 169 us
  blocking collectives  52.1 us (31%)
  starting transfers between devices  39.2 us (23%)
  Pallas kernels  38 us (22%)
  waiting for transfers between devices  34.2 us (20%)
  between operations  2.79 us (2%)
  local copies, waits for them, and re-layouts  2.23 us (1%)
    all_to_all x1, blocking collectives, exchange(): return lax.all_to_all(value, axis, split_axis=0, concat_axis=0, tiled=True)  52.1 us
    all_to_all x3, starting transfers between devices, exchange(): return lax.all_to_all(value, axis, split_axis=0, concat_axis=0, tiled=True)  39.2 us
    all_to_all x3, waiting for transfers between devices, exchange(): return lax.all_to_all(value, axis, split_axis=0, concat_axis=0, tiled=True)  34.2 us
    pallas_call x2, Pallas kernels, scan(): pl.pallas_call(scan_first_kernel if first else scan_kernel, out_shape=sca...  16.8 us
    pallas_call x1, Pallas kernels, per_device(): pl.pallas_call(early_rows, out_shape=[packed((256, 2048), F32), packed((2...  8.09 us
    pallas_call x1, Pallas kernels, per_device(): pl.pallas_call(state_kernel, out_shape=[packed((256, 2048), BF16), packed...  5.44 us
  transfers between devices with their start and end apart: 3, of which 3 were waited for; matrix products, arithmetic and copies ran while one was open for 0% of the time, Pallas kernels for 13%

profile of v4, /device:TPU:1, one launch (start us, length us, event | category | flops | bytes accessed | tf_op | source)
XLA Modules:
  0.0 168.6 jit_solution(5388019215703821297)
XLA Ops:
  2.6 4.0 %scan_early.1 = (f32[256,2048]{1,0:T(8,128)}, f32[256,2048]{1,0:T(8,128)}, f32[2048,128]{1,0:T(8,128)}, f32[2048,128]{1,0:T(8,128)}, bf16[256,128]{1,0:T(8,128)(...) custom-call(s32[1]{0:T(128)} %bitcast.flag, ...), custom_call_target="tpu_custom_call" | custom-call | flops 2147483648 | bytes 10485760 | tf_op jit(solution)/shard_map/scan_early/pallas_call | solution.py:411
  6.6 19.3 %all-to-all-start = ((bf16[64,32,128]{2,1,0:T(8,128)(2,1)}), bf16[64,32,128]{2,1,0:T(8,128)(2,1)S(1)}, u32[]{:S(2)}, u32[]{:S(2)}) async-start(bf16[64,32,128]{2,1,0:T(8,128)(2,1)} %get-tuple-element.73), calls=%async_computation | async-start | bytes 1048576 | tf_op jit(solution)/shard_map/all_to_all | solution.py:348
  25.9 12.8 %scan_late.1 = (f32[256,2048]{1,0:T(8,128)}, f32[256,2048]{1,0:T(8,128)}, f32[2048,128]{1,0:T(8,128)}, f32[2048,128]{1,0:T(8,128)}, bf16[256,128]{1,0:T(8,128)(2...) custom-call(s32[1]{0:T(128)} %bitcast.12.flag, ...), custom_call_target="tpu_custom_call", output_to_operand_aliasing={{0}: (9, {}), {1}: (10, {}), {2}: (11, {}), {3}: (12, {}), ... | custom-call | flops 2147483648 | bytes 10485760 | tf_op jit(solution)/shard_map/scan_late/pallas_call | solution.py:411
  38.7 9.6 %all-to-all-done.first = bf16[64,32,128]{2,1,0:T(8,128)(2,1)S(1)} async-done(((bf16[64,32,128]{2,1,0:T(8,128)(2,1)}), bf16[64,32,128]{2,1,0:T(8,128)(2,1)S(1)}, u32[]{:S(2)}, u32[]{:S(2)}) %all-to-all-start) | async-done | bytes 524320 | tf_op jit(solution)/shard_map/all_to_all | solution.py:348
  48.2 3.0 %pack_second.1 = (bf16[64,56,128]{2,1,0:T(8,128)(2,1)S(1)}, s32[8,128]{1,0:T(8,128)S(1)}) custom-call(s32[1]{0:T(128)} %bitcast.11.me, bf16[64,32,128]{2,1,0:T(8,128)(2,1)S(1)} %all-to-all-done.first, bf16[2,64,32,128]{3,2,1,0:T(8,128)(2,1)} %bitcast.27), custom_call_target="tpu_custom_call" | custom-call | bytes 3145728 | tf_op jit(solution)/shard_map/pack_second/pallas_call | solution.py:435
  51.2 0.0 copy-start.2
  51.2 0.0 copy-start.3
  51.2 0.0 copy-start.4
  51.3 0.0 copy-start.5
  51.3 0.0 copy-start.7
  51.3 0.0 copy-start.12
  51.3 0.0 copy-start.14
  51.3 52.1 %all_to_all.20.second.convs.panels.up = bf16[64,56,128]{2,1,0:T(8,128)(2,1)S(1)} all-to-all(bf16[64,56,128]{2,1,0:T(8,128)(2,1)S(1)} %get-tuple-element.96), channel_id=1, replica_groups=mesh['req'=64,'head'=8] {'req'}, dimensions={0} | all-to-all | bytes 1835008 | tf_op jit(solution)/shard_map/all_to_all | solution.py:348
  103.5 1.7 %pack_third.1 = bf16[64,32,128]{2,1,0:T(8,128)(2,1)} custom-call(s32[8,128]{1,0:T(8,128)S(1)} %get-tuple-element.95.codes, bf16[64,32,128]{2,1,0:T(8,128)(2,1)S(1)} %all-to-all-done.first, bf16[64,56,128]{2,1,0:T(8,128)(2,1)S(1)} %all_to_all.20.second.convs.panels.up), custom_call_target="tpu_custom_call" | custom-call | bytes 1048576 | tf_op jit(solution)/shard_map/pack_third/pallas_call | solution.py:446
  105.2 9.6 %all-to-all-start.2 = ((bf16[64,32,128]{2,1,0:T(8,128)(2,1)}), bf16[64,32,128]{2,1,0:T(8,128)(2,1)S(1)}, u32[]{:S(2)}, u32[]{:S(2)}) async-start(bf16[64,32,128]{2,1,0:T(8,128)(2,1)} %pack_third.1), calls=%async_computation.2 | async-start | bytes 1048576 | tf_op jit(solution)/shard_map/all_to_all | solution.py:348
  114.8 0.0 copy-done.2
  114.8 0.0 copy-done.3
  114.8 0.0 copy-done.4
  114.8 0.0 copy-done.5
  114.8 0.0 copy-done.7
  114.9 0.0 copy-start.13
  114.9 8.1 %early_rows.1 = (f32[256,2048]{1,0:T(8,128)}, f32[2048,128]{1,0:T(8,128)}, bf16[256,128]{1,0:T(8,128)(2,1)S(1)}) custom-call(bf16[256,2048]{1,0:T(8,128)(2,1)} %x.3, bf16[256,2,128]{2,1,0:T(2,128)(2,1)S(1)} %bitcast.18, f32[4,2048]{1,0:T(4,128)S(1)} %copy-done.7, f32[4,2,128]{2,1,0:T(2,128)S(1)} %bitcast.21, ...), custom_call_target="tpu_custom_call" | custom-call | flops 536870912 | bytes 8388608 | tf_op jit(solution)/shard_map/early_rows/pallas_call | solution.py:457
  123.0 0.6 copy-done.10
  123.6 19.0 %all-to-all-done.2.state = bf16[64,32,128]{2,1,0:T(8,128)(2,1)S(1)} async-done(((bf16[64,32,128]{2,1,0:T(8,128)(2,1)}), bf16[64,32,128]{2,1,0:T(8,128)(2,1)S(1)}, u32[]{:S(2)}, u32[]{:S(2)}) %all-to-all-start.2) | async-done | bytes 524320 | tf_op jit(solution)/shard_map/all_to_all | solution.py:348
  142.6 0.8 copy-done.11
  143.4 5.4 %state.1 = (bf16[256,2048]{1,0:T(8,128)(2,1)}, bf16[8,128,128]{2,1,0:T(8,128)(2,1)S(1)}) custom-call(bf16[64,32,128]{2,1,0:T(8,128)(2,1)S(1)} %all-to-all-done.2.state, bf16[256,128]{1,0:T(8,128)(2,1)S(1)} %copy-done.11, f32[256,2048]{1,0:T(8,128)} %get-tuple-element.111.part_far, f32[256,2048]{1,0:T(8,128)} %get-tuple-element.112.gate_far, ...), custom_call_target="tpu_custom_call" | custom-call | flops 268435456 | bytes 8388608 | tf_op jit(solution)/shard_map/state/pallas_call | solution.py:481
  148.9 0.0 copy-start.6
  148.9 0.7 copy-done.6
  149.6 10.3 %all-to-all-start.3 = ((bf16[8,128,128]{2,1,0:T(8,128)(2,1)}), bf16[8,128,128]{2,1,0:T(8,128)(2,1)}, u32[]{:S(2)}, u32[]{:S(2)}) async-start(bf16[8,128,128]{2,1,0:T(8,128)(2,1)} %copy-done.6), calls=%async_computation.3 | async-start | bytes 524288 | tf_op jit(solution)/shard_map/all_to_all | solution.py:348
  159.9 0.9 update.1
  160.8 5.7 %all-to-all-done.3.parts = bf16[8,128,128]{2,1,0:T(8,128)(2,1)} async-done(((bf16[8,128,128]{2,1,0:T(8,128)(2,1)}), bf16[8,128,128]{2,1,0:T(8,128)(2,1)}, u32[]{:S(2)}, u32[]{:S(2)}) %all-to-all-start.3) | async-done | bytes 262176 | tf_op jit(solution)/shard_map/all_to_all | solution.py:348
  166.5 2.1 %up.1 = bf16[256,1024]{1,0:T(8,128)(2,1)} custom-call(bf16[8,128,128]{2,1,0:T(8,128)(2,1)} %all-to-all-done.3.parts, bf16[64,56,128]{2,1,0:T(8,128)(2,1)S(1)} %all_to_all.20.second.convs.panels.up), custom_call_target="tpu_custom_call" | custom-call | flops 67108864 | bytes 1048576 | tf_op jit(solution)/shard_map/up/pallas_call | solution.py:505
  (13 shorter events, 0.0 us)
Async XLA Ops:
  6.6 41.7 %all-to-all-start = ((bf16[64,32,128]{2,1,0:T(8,128)(2,1)}), bf16[64,32,128]{2,1,0:T(8,128)(2,1)S(1)}, u32[]{:S(2)}, u32[]{:S(2)}) async-start(bf16[64,32,128]{2,1,0:T(8,128)(2,1)} %get-tuple-element.73), calls=%async_computation | async-start | bytes 1048576 | tf_op jit(solution)/shard_map/all_to_all | solution.py:348
  51.2 63.6 %copy-start.2 = (bf16[256,1,2,128]{3,2,1,0:T(2,128)(2,1)S(1)}, bf16[256,1,2,128]{3,2,1,0:T(2,128)(2,1)}, u32[]{:S(2)}) copy-start(bf16[256,1,2,128]{3,2,1,0:T(2,128)(2,1)} %param.19) | copy-start | bytes 393220
  51.2 63.6 %copy-start.3 = (f32[256,128]{1,0:T(8,128)S(1)}, f32[256,128]{1,0:T(8,128)}, u32[]{:S(2)}) copy-start(f32[256,128]{1,0:T(8,128)} %get-tuple-element.100.decay) | copy-start | bytes 393220
  51.2 63.6 %copy-start.4 = (f32[256,128]{1,0:T(8,128)S(1)}, f32[256,128]{1,0:T(8,128)}, u32[]{:S(2)}) copy-start(f32[256,128]{1,0:T(8,128)} %get-tuple-element.102.step) | copy-start | bytes 393220
  51.3 63.6 %copy-start.5 = (bf16[256,128]{1,0:T(8,128)(2,1)S(1)}, bf16[256,128]{1,0:T(8,128)(2,1)}, u32[]{:S(2)}) copy-start(bf16[256,128]{1,0:T(8,128)(2,1)} %get-tuple-element.99.c_main) | copy-start | bytes 196612
  51.3 63.6 %copy-start.7 = (f32[4,2048]{1,0:T(4,128)S(1)}, f32[4,2048]{1,0:T(4,128)}, u32[]{:S(2)}) copy-start(f32[4,2048]{1,0:T(4,128)} %taps.3) | copy-start | bytes 98308
  51.3 63.6 %copy-start.8 = (f32[32,256]{1,0:T(8,128)S(1)}, f32[32,256]{1,0:T(8,128)}, u32[]{:S(2)}) copy-start(f32[32,256]{1,0:T(8,128)} %get-tuple-element.101.decay_t) | copy-start | bytes 98308
  51.3 63.6 %copy-start.9 = (f32[32,256]{1,0:T(8,128)S(1)}, f32[32,256]{1,0:T(8,128)}, u32[]{:S(2)}) copy-start(f32[32,256]{1,0:T(8,128)} %get-tuple-element.103.step_t) | copy-start | bytes 98308
  51.3 63.6 %copy-start.12 = (f32[4,1,2,128]{3,2,1,0:T(2,128)S(1)}, f32[4,1,2,128]{3,2,1,0:T(2,128)}, u32[]{:S(2)}) copy-start(f32[4,1,2,128]{3,2,1,0:T(2,128)} %param.22) | copy-start | bytes 12292
  51.3 63.6 %copy-start.14 = (f32[32]{0:T(128)S(1)}, f32[32]{0:T(128)}, u32[]{:S(2)}) copy-start(f32[32]{0:T(128)} %param.25) | copy-start | bytes 388
  105.2 37.4 %all-to-all-start.2 = ((bf16[64,32,128]{2,1,0:T(8,128)(2,1)}), bf16[64,32,128]{2,1,0:T(8,128)(2,1)S(1)}, u32[]{:S(2)}, u32[]{:S(2)}) async-start(bf16[64,32,128]{2,1,0:T(8,128)(2,1)} %pack_third.1), calls=%async_computation.2 | async-start | bytes 1048576 | tf_op jit(solution)/shard_map/all_to_all | solution.py:348
  114.9 27.7 %copy-start.13 = (f32[2048]{0:T(1024)S(1)}, f32[2048]{0:T(1024)}, u32[]{:S(2)}) copy-start(f32[2048]{0:T(1024)} %param.26) | copy-start | bytes 24580
  123.0 0.6 copy-start.10
  142.6 0.8 copy-start.11
  143.4 16.4 %copy-start = (f32[2048,128]{1,0:T(8,128)S(1)}, f32[2048,128]{1,0:T(8,128)}, u32[]{:S(2)}) copy-start(f32[2048,128]{1,0:T(8,128)} %get-tuple-element.118.kept) | copy-start | bytes 3145732
  143.4 16.4 %copy-start.1 = (f32[2048,128]{1,0:T(8,128)S(1)}, f32[2048,128]{1,0:T(8,128)}, u32[]{:S(2)}) copy-start(f32[2048,128]{1,0:T(8,128)} %get-tuple-element.117.fresh) | copy-start | bytes 3145732
  148.9 0.7 copy-start.6
  149.6 16.9 %all-to-all-start.3 = ((bf16[8,128,128]{2,1,0:T(8,128)(2,1)}), bf16[8,128,128]{2,1,0:T(8,128)(2,1)}, u32[]{:S(2)}, u32[]{:S(2)}) async-start(bf16[8,128,128]{2,1,0:T(8,128)(2,1)} %copy-done.6), calls=%async_computation.3 | async-start | bytes 524288 | tf_op jit(solution)/shard_map/all_to_all | solution.py:348

commit v5 on v4

--- a/solution.py
+++ b/solution.py
@@ -237,9 +237,26 @@
 
 def early_rows(
     x, bc, taps, bc_taps, convs, skip, c_main, decay, decay_t, step, step_t, part_in, fresh_in,
-    part, fresh, c_out, pad, pad_bc, score, b_proj,
+    part, fresh, pad, pad_bc, score, b_proj, c_all,
 ):
     block = pl.program_id(0)
+
+    @pl.when(block == 8)
+    def _():
+        part[:, 0:128] = c_all[...].astype(F32)
+
+    @pl.when(block < 8)
+    def _():
+        early_block(
+            block, x, bc, taps, bc_taps, convs, skip, c_main, decay, decay_t, step, step_t, part_in, fresh_in,
+            part, fresh, pad, pad_bc, score, b_proj, c_all,
+        )
+
+
+def early_block(
+    block, x, bc, taps, bc_taps, convs, skip, c_main, decay, decay_t, step, step_t, part_in, fresh_in,
+    part, fresh, pad, pad_bc, score, b_proj, c_proj,
+):
     short = lax.broadcasted_iota(jnp.int32, (8, 256), 0) < 3
     rest = jnp.zeros((120, 128), F32)
 
@@ -252,7 +269,7 @@
         b_proj[...] = jnp.concatenate([both[:, 0:128], rest], axis=0).astype(BF16)
         c_all = c_main[...].astype(F32)
         c_all = jnp.concatenate([c_all[0:8] + both[:, 128:256], c_all[8:256]], axis=0).astype(BF16)
-        c_out[...] = c_all
+        c_proj[...] = c_all
         score[...] = dots(c_all, b_proj[...], 1, 1)
 
     for half in range(2):
@@ -287,8 +304,8 @@
         fresh[at, :] = fresh_in[at, :] + dots(carried, b_proj[...], 0, 0)
 
 
-def state_kernel(state, c_far, part_far, gate_far, gain, panels, normed, low, mixed, part, gate, tile, c_proj, sems):
-    fetch = pltpu.make_async_copy(c_far, c_proj, sems.at[0, 8])
+def state_kernel(state, part_far, gate_far, gain, panels, normed_far, low, mixed, part, gate, tile, c_proj, normed, sems):
+    fetch = pltpu.make_async_copy(part_far.at[:, pl.ds(2048, 128)], c_proj, sems.at[0, 8])
     fetch.start()
     copies = []
     for block in range(8):
@@ -298,7 +315,7 @@
     for copy in copies:
         copy.start()
     fetch.wait()
-    c_value = c_proj[...]
+    c_value = c_proj[...].astype(BF16)
     square = jnp.zeros((256, 128), F32)
     for block in range(8):
         at = slice(block * 256, block * 256 + 256)
@@ -312,17 +329,22 @@
     mean = jnp.sum(square, axis=1, keepdims=True) * (1.0 / 2048.0)
     scale = lax.rsqrt(mean + NORM_EPSILON)
     acc = jnp.zeros((256, 64), F32)
+    leaving = []
     for col in range(16):
         at = slice(col * 128, col * 128 + 128)
         value = (mixed[:, at] * scale * gain[:, at]).astype(BF16)
         normed[:, at] = value
         panel = panels[col * 4 : col * 4 + 4, 32:48, :].reshape(64, 128)
         acc = acc + lax.dot_general(value, panel, (((1,), (1,)), ((), ())), preferred_element_type=F32)
+        if col % 4 == 3:
+            at = pl.ds(col * 128 - 384, 512)
+            leaving.append(pltpu.make_async_copy(normed.at[:, at], normed_far.at[:, at], sems.at[1, col // 4]))
+            leaving[-1].start()
     tile[...] = jnp.concatenate([acc[0:128], acc[128:256]], axis=1).astype(BF16)
     copies = [pltpu.make_async_copy(tile, low.at[peer], sems.at[0, peer]) for peer in range(8)]
     for copy in copies:
         copy.start()
-    for copy in copies:
+    for copy in copies + leaving:
         copy.wait()
 
 
@@ -397,17 +419,27 @@
         step_before_bias.T, step_bias.reshape(1, 32), head_decay_rate.reshape(1, 32), head_skip_gain.reshape(1, 32),
     ]
 
-    pack_specs = [smem()] * 4 + [
-        fixed(64, 2048), fixed(1, 64, 1024), fixed(3, 2, 2048), fixed(2, 3, 1, 2, 128),
-        pl.BlockSpec((2, 64, 8, 128), lambda i, on: (0, 0, 3, 0)),
-    ]
+    sent1 = pl.pallas_call(
+        pack_first,
+        out_shape=packed((64, 32, 128), BF16),
+        grid=(1,),
+        in_specs=[smem()] * 4
+        + [
+            whole(64, 2048), whole(1, 64, 1024), whole(3, 2, 2048), whole(2, 3, 1, 2, 128),
+            pl.BlockSpec((2, 64, 8, 128), lambda i: (0, 0, 3, 0)),
+        ],
+        out_specs=whole(64, 32, 128),
+        compiler_params=params(60),
+        cost_estimate=cost(0, 2 << 20),
+        name="pack_first",
+    )(*pack_args)
 
     def scan(on, old, limit):
         inputs = [
             wide_at(256, 256), fixed(256, 2, 128), wide_at(4, 256), fixed(4, 2, 128), fixed(32, 256),
             fixed(1, 32), fixed(1, 32), fixed(1, 32),
         ]
-        first = not old
+        first, pack_specs = False, []
         return pl.pallas_call(
             scan_first_kernel if first else scan_kernel,
             out_shape=scan_shapes + [packed((64, 32, 128), BF16)] * first,
@@ -421,10 +453,13 @@
             input_output_aliases={9 + i: i for i in range(len(old))},
             compiler_params=params(limit),
             cost_estimate=cost(2 << 30, 10 << 20),
-            name="scan_early" if first else "scan_late",
+            name="scan_late" if old else "scan_early",
         )(on.reshape(1), *(pack_args * first), *scan_args, *old)
 
-    *early, sent1 = scan(even, [], 60)
+    skipped = pl.pallas_call(
+        lambda *refs: None, out_shape=scan_shapes, out_specs=[far] * 10, compiler_params=params(60), name="skip"
+    )
+    early = lax.cond(even == 1, lambda: scan(jnp.int32(1), [], 60), lambda: skipped())
     sent1, *early = hold((sent1, *early))
     got1 = exchange(sent1, "req")
     late = scan(1 - even, early, 60)
@@ -454,20 +489,22 @@
     )(codes, got1, got2)
     sent3, got2 = hold((sent3, got2))
     got3 = exchange(sent3, "req")
-    part, fresh, c_proj = pl.pallas_call(
+    held = lambda i: jnp.minimum(i, 7)
+    part, fresh = pl.pallas_call(
         early_rows,
-        out_shape=[packed((256, 2048), F32), packed((2048, 128), F32), packed((256, 128), BF16)],
-        grid=(8,),
+        out_shape=[packed((256, 2304), F32), packed((2048, 128), F32)],
+        grid=(9,),
         in_specs=[
-            pl.BlockSpec((16, 256), lambda i: (0, i)), whole(16, 2, 128), cols(4, 256), whole(4, 2, 128),
+            pl.BlockSpec((16, 256), lambda i: (0, held(i))), whole(16, 2, 128),
+            pl.BlockSpec((4, 256), lambda i: (0, held(i))), whole(4, 2, 128),
             pl.BlockSpec((64, 8, 128), lambda i: (0, 3, 0)),
             whole(1, 32), whole(256, 128), whole(256, 128), whole(32, 256), whole(256, 128), whole(32, 256),
-            cols(256, 256), pl.BlockSpec((256, 128), lambda i: (i, 0)),
+            pl.BlockSpec((256, 256), lambda i: (0, held(i))), pl.BlockSpec((256, 128), lambda i: (held(i), 0)),
         ],
-        out_specs=[cols(256, 256), pl.BlockSpec((256, 128), lambda i: (i, 0)), whole(256, 128)],
+        out_specs=[cols(256, 256), pl.BlockSpec((256, 128), lambda i: (held(i), 0))],
         scratch_shapes=[
             pltpu.VMEM((16, 256), F32), pltpu.VMEM((16, 256), F32),
-            pltpu.VMEM((256, 128), F32), pltpu.VMEM((128, 128), BF16),
+            pltpu.VMEM((256, 128), F32), pltpu.VMEM((128, 128), BF16), pltpu.VMEM((256, 128), BF16),
         ],
         compiler_params=params(52),
         cost_estimate=cost(1 << 29, 8 << 20),
@@ -476,20 +513,20 @@
         inner_input, scan_args[1], inner_conv_taps, scan_args[3], got2, scan_args[7], c_main,
         decay, decay_t, step, step_t, part, fresh,
     )
-    got3, part, c_proj, fresh = hold((got3, part, c_proj, fresh))
+    got3, part, fresh = hold((got3, part, fresh))
 
     normed, low = pl.pallas_call(
         state_kernel,
         out_shape=[packed((256, 2048), BF16), packed((8, 128, 128), BF16)],
         grid=(1,),
-        in_specs=[whole(64, 32, 128), far, far, far, whole(1, 2048), whole(64, 56, 128)],
-        out_specs=[whole(256, 2048), far],
+        in_specs=[whole(64, 32, 128), far, far, whole(1, 2048), whole(64, 56, 128)],
+        out_specs=[far, far],
         scratch_shapes=[pltpu.VMEM((256, 2048), F32)] * 3
-        + [pltpu.VMEM((128, 128), BF16), pltpu.VMEM((256, 128), BF16), pltpu.SemaphoreType.DMA((2, 9))],
+        + [pltpu.VMEM((128, 128), BF16), pltpu.VMEM((256, 128), F32), pltpu.VMEM((256, 2048), BF16), pltpu.SemaphoreType.DMA((2, 9))],
         compiler_params=params(52),
         cost_estimate=cost(1 << 28, 8 << 20),
         name="state",
-    )(got3, c_proj, part, gate, group_norm_gain.reshape(1, 2048), got2)
+    )(got3, part, gate, group_norm_gain.reshape(1, 2048), got2)
     low, fresh = hold((low, fresh))
     parts = exchange(low, "head")
     updated = pl.pallas_call(
@@ -497,7 +534,7 @@
         out_shape=packed((1, 2048, 128), BF16),
         in_specs=[vmem()] * 3,
         out_specs=vmem(),
-        compiler_params=params(),
+        compiler_params=params(60),
         cost_estimate=cost(1 << 20, 3 << 20),
         name="update",
     )(got3, fresh, kept)

time: 169 us -> 156 us (0.923)
  blocking collectives: 52.1 us -> 40.2 us
  starting transfers between devices: 39.2 us -> 48.9 us
  waiting for transfers between devices: 34.2 us -> 27.5 us
  Pallas kernels: 38 us -> 35 us
    all_to_all x1, blocking collectives: 52.1 us -> 40.2 us  [exchange(): return lax.all_to_all(value, axis, split_axis=0, concat_axis=0, tiled=True)]
    all_to_all x3, starting transfers between devices: 39.2 us -> 48.9 us  [exchange(): return lax.all_to_all(value, axis, split_axis=0, concat_axis=0, tiled=True)]
    all_to_all x3, waiting for transfers between devices: 34.2 us -> 27.5 us  [exchange(): return lax.all_to_all(value, axis, split_axis=0, concat_axis=0, tiled=True)]
    pallas_call x2 -> x1, Pallas kernels: 16.8 us -> 11.5 us  [scan(): pl.pallas_call(scan_first_kernel if first else scan_kernel, out_shape=sca...]
    pallas_call x1 -> x3, Pallas kernels: 8.09 us -> 10.3 us  [the longest x1 8.11 us: per_device(): pl.pallas_call(early_rows, out_shape=[packed((256, 2304), F32), packed((2...]
  transfers between devices with their start and end apart: 3 -> 3, of which waited for: 3 -> 3; matrix products, arithmetic and copies ran while one was open for 0% -> 0% of each run, Pallas kernels for 13% -> 14%
where the time goes in v5:
time: 156 us
  starting transfers between devices  48.9 us (31%)
  blocking collectives  40.2 us (26%)
  Pallas kernels  35 us (22%)
  waiting for transfers between devices  27.5 us (18%)
  between operations  2.83 us (2%)
    all_to_all x3, starting transfers between devices, exchange(): return lax.all_to_all(value, axis, split_axis=0, concat_axis=0, tiled=True)  48.9 us
    all_to_all x1, blocking collectives, exchange(): return lax.all_to_all(value, axis, split_axis=0, concat_axis=0, tiled=True)  40.2 us
    all_to_all x3, waiting for transfers between devices, exchange(): return lax.all_to_all(value, axis, split_axis=0, concat_axis=0, tiled=True)  27.5 us
    pallas_call x1, Pallas kernels, scan(): pl.pallas_call(scan_first_kernel if first else scan_kernel, out_shape=sca...  11.5 us
    pallas_call x1, Pallas kernels, per_device(): pl.pallas_call(early_rows, out_shape=[packed((256, 2304), F32), packed((2...  8.11 us
    pallas_call x1, Pallas kernels, per_device(): pl.pallas_call(state_kernel, out_shape=[packed((256, 2048), BF16), packed...  5.07 us
  transfers between devices with their start and end apart: 3, of which 3 were waited for; matrix products, arithmetic and copies ran while one was open for 0% of the time, Pallas kernels for 14%

profile of v5, /device:TPU:1, one launch (start us, length us, event | category | flops | bytes accessed | tf_op | source)
XLA Modules:
  0.0 155.6 jit_solution(16133863807391000023)
XLA Ops:
  2.6 0.0 copy-start.4
  2.6 0.0 copy-start.8
  2.6 0.0 copy-start.11
  2.6 0.0 copy-start.12
  2.7 0.0 copy-start.13
  2.7 0.0 copy-start.14
  2.7 0.0 copy-start.15
  2.7 2.2 %pack_first.1 = bf16[64,32,128]{2,1,0:T(8,128)(2,1)} custom-call(s32[1]{0:T(128)S(6)} %copy.61.tenant, s32[64]{0:T(128)} %table.1, s32[1]{0:T(128)S(6)} %copy.62.owner, s32[1]{0:T(128)S(6)} %copy.63.slot, bf16[64,2048]{1,0:T(8,128)(2,1)} %bitcast.22, bf16[1,64,1024]{2,1,0:T(8,128)(2,1)} %up.2, bf16[3,2,2048]{2,1,0:T(2,128)(2,1)} %bitcast.23, ...), custom_call_target="tpu_custom_call" | custom-call | bytes 2097152 | tf_op jit(solution)/shard_map/pack_first/pallas_call | solution.py:422
  4.8 19.3 %all-to-all-start = ((bf16[64,32,128]{2,1,0:T(8,128)(2,1)}), bf16[64,32,128]{2,1,0:T(8,128)(2,1)S(1)}, u32[]{:S(2)}, u32[]{:S(2)}) async-start(bf16[64,32,128]{2,1,0:T(8,128)(2,1)} %pack_first.1), calls=%async_computation | async-start | bytes 1048576 | tf_op jit(solution)/shard_map/all_to_all | solution.py:370
  24.1 0.0 copy-done.4
  24.1 0.0 copy-done.8
  24.2 0.0 copy-done.11
  24.2 11.5 %scan_late.1 = (f32[256,2048]{1,0:T(8,128)S(1)}, f32[256,2048]{1,0:T(8,128)}, f32[2048,128]{1,0:T(8,128)}, f32[2048,128]{1,0:T(8,128)}, bf16[256,128]{1,0:T(8,12...) custom-call(s32[1]{0:T(128)} %bitcast.11.flag, ...), custom_call_target="tpu_custom_call", output_to_operand_aliasing={{0}: (9, {}), {1}: (10, {}), {2}: (11, {}), {3}: (12, {}), ... | custom-call | flops 2147483648 | bytes 10485760 | tf_op jit(solution)/shard_map/scan_late/pallas_call | solution.py:443
  35.8 10.2 %all-to-all-done.first = bf16[64,32,128]{2,1,0:T(8,128)(2,1)S(1)} async-done(((bf16[64,32,128]{2,1,0:T(8,128)(2,1)}), bf16[64,32,128]{2,1,0:T(8,128)(2,1)S(1)}, u32[]{:S(2)}, u32[]{:S(2)}) %all-to-all-start) | async-done | bytes 524320 | tf_op jit(solution)/shard_map/all_to_all | solution.py:370
  46.0 3.0 %pack_second.1 = (bf16[64,56,128]{2,1,0:T(8,128)(2,1)S(1)}, s32[8,128]{1,0:T(8,128)S(1)}) custom-call(s32[1]{0:T(128)} %bitcast.10.me, bf16[64,32,128]{2,1,0:T(8,128)(2,1)S(1)} %all-to-all-done.first, bf16[2,64,32,128]{3,2,1,0:T(8,128)(2,1)} %bitcast.17), custom_call_target="tpu_custom_call" | custom-call | bytes 3145728 | tf_op jit(solution)/shard_map/pack_second/pallas_call | solution.py:470
  49.0 0.0 copy-done.5
  49.0 0.0 copy-done.6
  49.0 0.0 copy-done.7
  49.0 0.0 copy-done.9
  49.0 0.0 copy-done.10
  49.0 40.2 %all_to_all.20.second.convs.panels.up = bf16[64,56,128]{2,1,0:T(8,128)(2,1)S(1)} all-to-all(bf16[64,56,128]{2,1,0:T(8,128)(2,1)S(1)} %get-tuple-element.116), channel_id=1, replica_groups=mesh['req'=64,'head'=8] {'req'}, dimensions={0} | all-to-all | bytes 1835008 | tf_op jit(solution)/shard_map/all_to_all | solution.py:370
  89.2 1.7 %pack_third.1 = bf16[64,32,128]{2,1,0:T(8,128)(2,1)} custom-call(s32[8,128]{1,0:T(8,128)S(1)} %get-tuple-element.115.codes, bf16[64,32,128]{2,1,0:T(8,128)(2,1)S(1)} %all-to-all-done.first, bf16[64,56,128]{2,1,0:T(8,128)(2,1)S(1)} %all_to_all.20.second.convs.panels.up), custom_call_target="tpu_custom_call" | custom-call | bytes 1048576 | tf_op jit(solution)/shard_map/pack_third/pallas_call | solution.py:481
  91.0 13.2 %all-to-all-start.2 = ((bf16[64,32,128]{2,1,0:T(8,128)(2,1)}), bf16[64,32,128]{2,1,0:T(8,128)(2,1)S(1)}, u32[]{:S(2)}, u32[]{:S(2)}) async-start(bf16[64,32,128]{2,1,0:T(8,128)(2,1)} %pack_third.1), calls=%async_computation.2 | async-start | bytes 1048576 | tf_op jit(solution)/shard_map/all_to_all | solution.py:370
  104.2 0.0 copy-start.2
  104.2 8.1 %early_rows.1 = (f32[256,2304]{1,0:T(8,128)}, f32[2048,128]{1,0:T(8,128)S(1)}) custom-call(bf16[256,2048]{1,0:T(8,128)(2,1)} %x.3, bf16[256,2,128]{2,1,0:T(2,128)(2,1)} %bitcast.19, f32[4,2048]{1,0:T(4,128)} %taps.3, f32[4,2,128]{2,1,0:T(2,128)S(1)} %bitcast.28, bf16[64,56,128]{2,1,0:T(8,128)(2,1)S(1)} %all_to_all.20.second.convs.panels.up, ...), custom_call_target="tpu_custom_call" | custom-call | flops 536870912 | bytes 8388608 | tf_op jit(solution)/shard_map/early_rows/pallas_call | solution.py:493
  112.3 1.0 copy-done.1
  113.3 13.1 %all-to-all-done.2.state = bf16[64,32,128]{2,1,0:T(8,128)(2,1)S(1)} async-done(((bf16[64,32,128]{2,1,0:T(8,128)(2,1)}), bf16[64,32,128]{2,1,0:T(8,128)(2,1)S(1)}, u32[]{:S(2)}, u32[]{:S(2)}) %all-to-all-start.2) | async-done | bytes 524320 | tf_op jit(solution)/shard_map/all_to_all | solution.py:370
  126.4 5.1 %state.1 = (bf16[256,2048]{1,0:T(8,128)(2,1)}, bf16[8,128,128]{2,1,0:T(8,128)(2,1)}) custom-call(bf16[64,32,128]{2,1,0:T(8,128)(2,1)S(1)} %all-to-all-done.2.state, f32[256,2304]{1,0:T(8,128)} %get-tuple-element.129.part_far, f32[256,2048]{1,0:T(8,128)} %get-tuple-element.130.gate_far, f32[1,2048]{1,0:T(1,128)S(1)} %bitcast.15, ...), custom_call_target="tpu_custom_call" | custom-call | flops 268435456 | bytes 8388608 | tf_op jit(solution)/shard_map/state/pallas_call | solution.py:518
  131.5 16.4 %all-to-all-start.3 = ((bf16[8,128,128]{2,1,0:T(8,128)(2,1)}), bf16[8,128,128]{2,1,0:T(8,128)(2,1)S(1)}, u32[]{:S(2)}, u32[]{:S(2)}) async-start(bf16[8,128,128]{2,1,0:T(8,128)(2,1)} %get-tuple-element.134), calls=%async_computation.3 | async-start | bytes 524288 | tf_op jit(solution)/shard_map/all_to_all | solution.py:370
  147.9 2.3 %update.1 = bf16[1,2048,128]{2,1,0:T(8,128)(2,1)} custom-call(bf16[64,32,128]{2,1,0:T(8,128)(2,1)} %copy-done, f32[2048,128]{1,0:T(8,128)} %copy-done.1, f32[2048,128]{1,0:T(8,128)S(1)} %copy-done.3), custom_call_target="tpu_custom_call" | custom-call | flops 1048576 | bytes 3145728 | tf_op jit(solution)/shard_map/update/pallas_call | solution.py:532
  150.2 4.2 %all-to-all-done.3.parts = bf16[8,128,128]{2,1,0:T(8,128)(2,1)S(1)} async-done(((bf16[8,128,128]{2,1,0:T(8,128)(2,1)}), bf16[8,128,128]{2,1,0:T(8,128)(2,1)S(1)}, u32[]{:S(2)}, u32[]{:S(2)}) %all-to-all-start.3) | async-done | bytes 262176 | tf_op jit(solution)/shard_map/all_to_all | solution.py:370
  154.4 1.1 up.3
  (17 shorter events, 0.1 us)
Async XLA Ops:
  2.6 21.5 %copy-start.4 = (bf16[256,1,2,128]{3,2,1,0:T(2,128)(2,1)S(1)}, bf16[256,1,2,128]{3,2,1,0:T(2,128)(2,1)}, u32[]{:S(2)}) copy-start(bf16[256,1,2,128]{3,2,1,0:T(2,128)(2,1)} %param.21) | copy-start | bytes 393220
  2.6 21.5 %copy-start.8 = (f32[4,2048]{1,0:T(4,128)S(1)}, f32[4,2048]{1,0:T(4,128)}, u32[]{:S(2)}) copy-start(f32[4,2048]{1,0:T(4,128)} %taps.3) | copy-start | bytes 98308
  2.6 21.5 %copy-start.11 = (bf16[256,32]{0,1:T(8,128)(2,1)S(1)}, bf16[256,32]{0,1:T(8,128)(2,1)}, u32[]{:S(2)}) copy-start(bf16[256,32]{0,1:T(8,128)(2,1)} %param.22) | copy-start | bytes 49156
  2.6 21.5 %copy-start.12 = (f32[4,1,2,128]{3,2,1,0:T(2,128)S(1)}, f32[4,1,2,128]{3,2,1,0:T(2,128)}, u32[]{:S(2)}) copy-start(f32[4,1,2,128]{3,2,1,0:T(2,128)} %param.24) | copy-start | bytes 12292
  2.7 21.5 %copy-start.13 = (f32[32]{0:T(128)S(1)}, f32[32]{0:T(128)}, u32[]{:S(2)}) copy-start(f32[32]{0:T(128)} %param.27) | copy-start | bytes 388
  2.7 21.5 %copy-start.14 = (f32[32]{0:T(128)S(1)}, f32[32]{0:T(128)}, u32[]{:S(2)}) copy-start(f32[32]{0:T(128)} %param.25) | copy-start | bytes 388
  2.7 21.5 %copy-start.15 = (f32[32]{0:T(128)S(1)}, f32[32]{0:T(128)}, u32[]{:S(2)}) copy-start(f32[32]{0:T(128)} %param.26) | copy-start | bytes 388
  4.8 41.2 %all-to-all-start = ((bf16[64,32,128]{2,1,0:T(8,128)(2,1)}), bf16[64,32,128]{2,1,0:T(8,128)(2,1)S(1)}, u32[]{:S(2)}, u32[]{:S(2)}) async-start(bf16[64,32,128]{2,1,0:T(8,128)(2,1)} %pack_first.1), calls=%async_computation | async-start | bytes 1048576 | tf_op jit(solution)/shard_map/all_to_all | solution.py:370
  35.7 13.3 %copy-start.5 = (f32[256,128]{1,0:T(8,128)}, f32[256,128]{1,0:T(8,128)S(1)}, u32[]{:S(2)}) copy-start(f32[256,128]{1,0:T(8,128)S(1)} %get-tuple-element.120.decay) | copy-start | bytes 393220
  35.7 13.3 %copy-start.6 = (f32[256,128]{1,0:T(8,128)}, f32[256,128]{1,0:T(8,128)S(1)}, u32[]{:S(2)}) copy-start(f32[256,128]{1,0:T(8,128)S(1)} %get-tuple-element.122.step) | copy-start | bytes 393220
  35.8 13.3 %copy-start.7 = (bf16[256,128]{1,0:T(8,128)(2,1)}, bf16[256,128]{1,0:T(8,128)(2,1)S(1)}, u32[]{:S(2)}) copy-start(bf16[256,128]{1,0:T(8,128)(2,1)S(1)} %get-tuple-element.119.c_main) | copy-start | bytes 196612
  35.8 13.3 %copy-start.9 = (f32[32,256]{1,0:T(8,128)}, f32[32,256]{1,0:T(8,128)S(1)}, u32[]{:S(2)}) copy-start(f32[32,256]{1,0:T(8,128)S(1)} %get-tuple-element.121.decay_t) | copy-start | bytes 98308
  35.8 13.3 %copy-start.10 = (f32[32,256]{1,0:T(8,128)}, f32[32,256]{1,0:T(8,128)S(1)}, u32[]{:S(2)}) copy-start(f32[32,256]{1,0:T(8,128)S(1)} %get-tuple-element.123.step_t) | copy-start | bytes 98308
  91.0 35.4 %all-to-all-start.2 = ((bf16[64,32,128]{2,1,0:T(8,128)(2,1)}), bf16[64,32,128]{2,1,0:T(8,128)(2,1)S(1)}, u32[]{:S(2)}, u32[]{:S(2)}) async-start(bf16[64,32,128]{2,1,0:T(8,128)(2,1)} %pack_third.1), calls=%async_computation.2 | async-start | bytes 1048576 | tf_op jit(solution)/shard_map/all_to_all | solution.py:370
  104.2 22.2 %copy-start.2 = (f32[2048]{0:T(1024)S(1)}, f32[2048]{0:T(1024)}, u32[]{:S(2)}) copy-start(f32[2048]{0:T(1024)} %param.28) | copy-start | bytes 24580
  112.3 1.0 copy-start.1
  126.4 5.1 %copy-start = (bf16[64,32,128]{2,1,0:T(8,128)(2,1)}, bf16[64,32,128]{2,1,0:T(8,128)(2,1)S(1)}, u32[]{:S(2)}) copy-start(bf16[64,32,128]{2,1,0:T(8,128)(2,1)S(1)} %all-to-all-done.2.state) | copy-start | bytes 1572868
  126.4 21.5 %copy-start.3 = (f32[2048,128]{1,0:T(8,128)S(1)}, f32[2048,128]{1,0:T(8,128)}, u32[]{:S(2)}) copy-start(f32[2048,128]{1,0:T(8,128)} %get-tuple-element.136.kept) | copy-start | bytes 3145732
  131.5 22.9 %all-to-all-start.3 = ((bf16[8,128,128]{2,1,0:T(8,128)(2,1)}), bf16[8,128,128]{2,1,0:T(8,128)(2,1)S(1)}, u32[]{:S(2)}, u32[]{:S(2)}) async-start(bf16[8,128,128]{2,1,0:T(8,128)(2,1)} %get-tuple-element.134), calls=%async_computation.3 | async-start | bytes 524288 | tf_op jit(solution)/shard_map/all_to_all | solution.py:370

commit v6 on v5

--- a/solution.py
+++ b/solution.py
@@ -55,7 +55,10 @@
         out[chunk, 24:32, :] = tile.astype(BF16)
 
 
-def pack_second(me, first, states, out, codes, words, sems):
+def pack_second(me, first, states, out, codes, words, both, sems):
+    fetches = [pltpu.make_async_copy(states.at[slot], both.at[slot], sems.at[1 + slot]) for slot in range(2)]
+    for fetch in fetches:
+        fetch.start()
     lines = lax.broadcasted_iota(jnp.int32, (8, 128), 0)
     tall = lax.broadcasted_iota(jnp.int32, (64, 8, 128), 1)
     picked = jnp.sum(jnp.where(tall == 2, first[:, 24:32, :].astype(F32), 0.0), axis=1)
@@ -65,23 +68,18 @@
     to_scalars.start()
     to_scalars.wait()
     mine = lax.fori_loop(0, 64, lambda j, m: jnp.where(codes[1, j] == me[0], codes[2, j], m), 0, unroll=8)
-    own = pltpu.make_async_copy(states.at[mine], out.at[:, 0:32, :], sems.at[1])
-    own.start()
-
-    def panels(j, carry):
+    for fetch in fetches:
+        fetch.wait()
+
+    def body(j, carry):
+        out[j, 0:24, :] = both[mine, j, 0:24, :]
         out[j, 32:56, :] = first[codes[0, j], 0:24, :]
-        return carry
-
-    lax.fori_loop(0, 64, panels, 0, unroll=8)
-    own.wait()
-
-    def lines_of(j, carry):
         tile = first[codes[1, j], 24:32, :].astype(F32)
         line = jnp.where(codes[2, j] == 0, tile[0:1], tile[1:2])
-        out[j, 24:32, :] = jnp.where(lines == 6, line, out[j, 24:32, :].astype(F32)).astype(BF16)
+        out[j, 24:32, :] = jnp.where(lines == 6, line, both[mine, j, 24:32, :].astype(F32)).astype(BF16)
         return carry
 
-    lax.fori_loop(0, 64, lines_of, 0, unroll=8)
+    lax.fori_loop(0, 64, body, 0, unroll=8)
 
 
 def pack_third(codes, first, second, out):
@@ -472,7 +470,9 @@
         out_shape=[packed((64, 56, 128), BF16), packed((8, 128), jnp.int32)],
         in_specs=[smem(), vmem(), pl.BlockSpec(memory_space=pl.ANY)],
         out_specs=[vmem(), smem()],
-        scratch_shapes=[pltpu.VMEM((8, 128), jnp.int32), pltpu.SemaphoreType.DMA((2,))],
+        scratch_shapes=[
+            pltpu.VMEM((8, 128), jnp.int32), pltpu.VMEM((2, 64, 32, 128), BF16), pltpu.SemaphoreType.DMA((3,)),
+        ],
         compiler_params=params(52),
         cost_estimate=cost(0, 3 << 20),
         name="pack_second",
@@ -518,8 +518,7 @@
     normed, low = pl.pallas_call(
         state_kernel,
         out_shape=[packed((256, 2048), BF16), packed((8, 128, 128), BF16)],
-        grid=(1,),
-        in_specs=[whole(64, 32, 128), far, far, whole(1, 2048), whole(64, 56, 128)],
+        in_specs=[vmem(), far, far, vmem(), vmem()],
         out_specs=[far, far],
         scratch_shapes=[pltpu.VMEM((256, 2048), F32)] * 3
         + [pltpu.VMEM((128, 128), BF16), pltpu.VMEM((256, 128), F32), pltpu.VMEM((256, 2048), BF16), pltpu.SemaphoreType.DMA((2, 9))],

time: 156 us -> 155 us (level)
  no operation moved by 1% of the time
where the time goes in v6:
time: 155 us; the launch traced here: 154 us
  starting transfers between devices  48.1 us (31%)
  blocking collectives  40.2 us (26%)
  Pallas kernels  34.3 us (22%)
  waiting for transfers between devices  27.3 us (18%)
  between operations  2.83 us (2%)
    all_to_all x3, starting transfers between devices, exchange(): return lax.all_to_all(value, axis, split_axis=0, concat_axis=0, tiled=True)  48.1 us
    all_to_all x1, blocking collectives, exchange(): return lax.all_to_all(value, axis, split_axis=0, concat_axis=0, tiled=True)  40.2 us
    all_to_all x3, waiting for transfers between devices, exchange(): return lax.all_to_all(value, axis, split_axis=0, concat_axis=0, tiled=True)  27.3 us
    pallas_call x1, Pallas kernels, scan(): pl.pallas_call(scan_first_kernel if first else scan_kernel, out_shape=sca...  11.5 us
    pallas_call x1, Pallas kernels, per_device(): pl.pallas_call(early_rows, out_shape=[packed((256, 2304), F32), packed((2...  8.11 us
    pallas_call x1, Pallas kernels, per_device(): pl.pallas_call(state_kernel, out_shape=[packed((256, 2048), BF16), packed...  5.07 us
  transfers between devices with their start and end apart: 3, of which 3 were waited for; matrix products, arithmetic and copies ran while one was open for 0% of the time, Pallas kernels for 14%

profile of v6, /device:TPU:1, one launch (start us, length us, event | category | flops | bytes accessed | tf_op | source)
XLA Modules:
  0.0 153.8 jit_solution(17143093253418226701)
XLA Ops:
  2.6 0.0 copy-start.4
  2.6 0.0 copy-start.8
  2.6 0.0 copy-start.11
  2.6 0.0 copy-start.12
  2.7 0.0 copy-start.13
  2.7 0.0 copy-start.14
  2.7 0.0 copy-start.15
  2.7 2.2 %pack_first.1 = bf16[64,32,128]{2,1,0:T(8,128)(2,1)} custom-call(s32[1]{0:T(128)S(6)} %copy.61.tenant, s32[64]{0:T(128)} %table.1, s32[1]{0:T(128)S(6)} %copy.62.owner, s32[1]{0:T(128)S(6)} %copy.63.slot, bf16[64,2048]{1,0:T(8,128)(2,1)} %bitcast.22, bf16[1,64,1024]{2,1,0:T(8,128)(2,1)} %up.2, bf16[3,2,2048]{2,1,0:T(2,128)(2,1)} %bitcast.23, ...), custom_call_target="tpu_custom_call" | custom-call | bytes 2097152 | tf_op jit(solution)/shard_map/pack_first/pallas_call | solution.py:420
  4.8 19.3 %all-to-all-start = ((bf16[64,32,128]{2,1,0:T(8,128)(2,1)}), bf16[64,32,128]{2,1,0:T(8,128)(2,1)S(1)}, u32[]{:S(2)}, u32[]{:S(2)}) async-start(bf16[64,32,128]{2,1,0:T(8,128)(2,1)} %pack_first.1), calls=%async_computation | async-start | bytes 1048576 | tf_op jit(solution)/shard_map/all_to_all | solution.py:368
  24.1 0.0 copy-done.4
  24.1 0.0 copy-done.8
  24.2 0.0 copy-done.11
  24.2 0.0 copy-done.12
  24.2 0.0 copy-done.13
  24.2 0.0 copy-done.14
  24.2 0.0 copy-done.15
  24.2 11.5 %scan_late.1 = (f32[256,2048]{1,0:T(8,128)S(1)}, f32[256,2048]{1,0:T(8,128)}, f32[2048,128]{1,0:T(8,128)}, f32[2048,128]{1,0:T(8,128)}, bf16[256,128]{1,0:T(8,12...) custom-call(s32[1]{0:T(128)} %bitcast.11.flag, ...), custom_call_target="tpu_custom_call", output_to_operand_aliasing={{0}: (9, {}), {1}: (10, {}), {2}: (11, {}), {3}: (12, {}), ... | custom-call | flops 2147483648 | bytes 10485760 | tf_op jit(solution)/shard_map/scan_late/pallas_call | solution.py:441
  35.8 10.2 %all-to-all-done.first = bf16[64,32,128]{2,1,0:T(8,128)(2,1)S(1)} async-done(((bf16[64,32,128]{2,1,0:T(8,128)(2,1)}), bf16[64,32,128]{2,1,0:T(8,128)(2,1)S(1)}, u32[]{:S(2)}, u32[]{:S(2)}) %all-to-all-start) | async-done | bytes 524320 | tf_op jit(solution)/shard_map/all_to_all | solution.py:368
  46.0 2.3 %pack_second.1 = (bf16[64,56,128]{2,1,0:T(8,128)(2,1)S(1)}, s32[8,128]{1,0:T(8,128)S(1)}) custom-call(s32[1]{0:T(128)} %bitcast.10.me, bf16[64,32,128]{2,1,0:T(8,128)(2,1)S(1)} %all-to-all-done.first, bf16[2,64,32,128]{3,2,1,0:T(8,128)(2,1)} %bitcast.17), custom_call_target="tpu_custom_call" | custom-call | bytes 3145728 | tf_op jit(solution)/shard_map/pack_second/pallas_call | solution.py:468
  48.3 40.2 %all_to_all.20.second.convs.panels.up = bf16[64,56,128]{2,1,0:T(8,128)(2,1)S(1)} all-to-all(bf16[64,56,128]{2,1,0:T(8,128)(2,1)S(1)} %get-tuple-element.116), channel_id=1, replica_groups=mesh['req'=64,'head'=8] {'req'}, dimensions={0} | all-to-all | bytes 1835008 | tf_op jit(solution)/shard_map/all_to_all | solution.py:368
  88.6 1.7 %pack_third.1 = bf16[64,32,128]{2,1,0:T(8,128)(2,1)} custom-call(s32[8,128]{1,0:T(8,128)S(1)} %get-tuple-element.115.codes, bf16[64,32,128]{2,1,0:T(8,128)(2,1)S(1)} %all-to-all-done.first, bf16[64,56,128]{2,1,0:T(8,128)(2,1)S(1)} %all_to_all.20.second.convs.panels.up), custom_call_target="tpu_custom_call" | custom-call | bytes 1048576 | tf_op jit(solution)/shard_map/pack_third/pallas_call | solution.py:481
  90.3 12.4 %all-to-all-start.2 = ((bf16[64,32,128]{2,1,0:T(8,128)(2,1)}), bf16[64,32,128]{2,1,0:T(8,128)(2,1)S(1)}, u32[]{:S(2)}, u32[]{:S(2)}) async-start(bf16[64,32,128]{2,1,0:T(8,128)(2,1)} %pack_third.1), calls=%async_computation.2 | async-start | bytes 1048576 | tf_op jit(solution)/shard_map/all_to_all | solution.py:368
  102.7 0.0 copy-start.2
  102.7 8.1 %early_rows.1 = (f32[256,2304]{1,0:T(8,128)}, f32[2048,128]{1,0:T(8,128)S(1)}) custom-call(bf16[256,2048]{1,0:T(8,128)(2,1)} %x.3, bf16[256,2,128]{2,1,0:T(2,128)(2,1)} %bitcast.19, f32[4,2048]{1,0:T(4,128)} %taps.3, f32[4,2,128]{2,1,0:T(2,128)S(1)} %bitcast.28, bf16[64,56,128]{2,1,0:T(8,128)(2,1)S(1)} %all_to_all.20.second.convs.panels.up, ...), custom_call_target="tpu_custom_call" | custom-call | flops 536870912 | bytes 8388608 | tf_op jit(solution)/shard_map/early_rows/pallas_call | solution.py:493
  110.8 1.0 copy-done.1
  111.8 12.9 %all-to-all-done.2.state = bf16[64,32,128]{2,1,0:T(8,128)(2,1)S(1)} async-done(((bf16[64,32,128]{2,1,0:T(8,128)(2,1)}), bf16[64,32,128]{2,1,0:T(8,128)(2,1)S(1)}, u32[]{:S(2)}, u32[]{:S(2)}) %all-to-all-start.2) | async-done | bytes 524320 | tf_op jit(solution)/shard_map/all_to_all | solution.py:368
  124.7 5.1 %state.1 = (bf16[256,2048]{1,0:T(8,128)(2,1)}, bf16[8,128,128]{2,1,0:T(8,128)(2,1)}) custom-call(bf16[64,32,128]{2,1,0:T(8,128)(2,1)S(1)} %all-to-all-done.2.state, f32[256,2304]{1,0:T(8,128)} %get-tuple-element.129.part_far, f32[256,2048]{1,0:T(8,128)} %get-tuple-element.130.gate_far, f32[1,2048]{1,0:T(1,128)S(1)} %bitcast.15, ...), custom_call_target="tpu_custom_call" | custom-call | flops 268435456 | bytes 8388608 | tf_op jit(solution)/shard_map/state/pallas_call | solution.py:518
  129.8 16.4 %all-to-all-start.3 = ((bf16[8,128,128]{2,1,0:T(8,128)(2,1)}), bf16[8,128,128]{2,1,0:T(8,128)(2,1)S(1)}, u32[]{:S(2)}, u32[]{:S(2)}) async-start(bf16[8,128,128]{2,1,0:T(8,128)(2,1)} %get-tuple-element.134), calls=%async_computation.3 | async-start | bytes 524288 | tf_op jit(solution)/shard_map/all_to_all | solution.py:368
  146.2 0.0 copy-done.3
  146.2 2.3 %update.1 = bf16[1,2048,128]{2,1,0:T(8,128)(2,1)} custom-call(bf16[64,32,128]{2,1,0:T(8,128)(2,1)} %copy-done, f32[2048,128]{1,0:T(8,128)} %copy-done.1, f32[2048,128]{1,0:T(8,128)S(1)} %copy-done.3), custom_call_target="tpu_custom_call" | custom-call | flops 1048576 | bytes 3145728 | tf_op jit(solution)/shard_map/update/pallas_call | solution.py:531
  148.5 4.2 %all-to-all-done.3.parts = bf16[8,128,128]{2,1,0:T(8,128)(2,1)S(1)} async-done(((bf16[8,128,128]{2,1,0:T(8,128)(2,1)}), bf16[8,128,128]{2,1,0:T(8,128)(2,1)S(1)}, u32[]{:S(2)}, u32[]{:S(2)}) %all-to-all-start.3) | async-done | bytes 262176 | tf_op jit(solution)/shard_map/all_to_all | solution.py:368
  152.7 1.1 up.3
  (17 shorter events, 0.1 us)
Async XLA Ops:
  2.6 21.5 %copy-start.4 = (bf16[256,1,2,128]{3,2,1,0:T(2,128)(2,1)S(1)}, bf16[256,1,2,128]{3,2,1,0:T(2,128)(2,1)}, u32[]{:S(2)}) copy-start(bf16[256,1,2,128]{3,2,1,0:T(2,128)(2,1)} %param.21) | copy-start | bytes 393220
  2.6 21.5 %copy-start.8 = (f32[4,2048]{1,0:T(4,128)S(1)}, f32[4,2048]{1,0:T(4,128)}, u32[]{:S(2)}) copy-start(f32[4,2048]{1,0:T(4,128)} %taps.3) | copy-start | bytes 98308
  2.6 21.5 %copy-start.11 = (bf16[256,32]{0,1:T(8,128)(2,1)S(1)}, bf16[256,32]{0,1:T(8,128)(2,1)}, u32[]{:S(2)}) copy-start(bf16[256,32]{0,1:T(8,128)(2,1)} %param.22) | copy-start | bytes 49156
  2.6 21.5 %copy-start.12 = (f32[4,1,2,128]{3,2,1,0:T(2,128)S(1)}, f32[4,1,2,128]{3,2,1,0:T(2,128)}, u32[]{:S(2)}) copy-start(f32[4,1,2,128]{3,2,1,0:T(2,128)} %param.24) | copy-start | bytes 12292
  2.7 21.5 %copy-start.13 = (f32[32]{0:T(128)S(1)}, f32[32]{0:T(128)}, u32[]{:S(2)}) copy-start(f32[32]{0:T(128)} %param.27) | copy-start | bytes 388
  2.7 21.5 %copy-start.14 = (f32[32]{0:T(128)S(1)}, f32[32]{0:T(128)}, u32[]{:S(2)}) copy-start(f32[32]{0:T(128)} %param.25) | copy-start | bytes 388
  2.7 21.5 %copy-start.15 = (f32[32]{0:T(128)S(1)}, f32[32]{0:T(128)}, u32[]{:S(2)}) copy-start(f32[32]{0:T(128)} %param.26) | copy-start | bytes 388
  4.8 41.2 %all-to-all-start = ((bf16[64,32,128]{2,1,0:T(8,128)(2,1)}), bf16[64,32,128]{2,1,0:T(8,128)(2,1)S(1)}, u32[]{:S(2)}, u32[]{:S(2)}) async-start(bf16[64,32,128]{2,1,0:T(8,128)(2,1)} %pack_first.1), calls=%async_computation | async-start | bytes 1048576 | tf_op jit(solution)/shard_map/all_to_all | solution.py:368
  35.7 12.5 %copy-start.5 = (f32[256,128]{1,0:T(8,128)}, f32[256,128]{1,0:T(8,128)S(1)}, u32[]{:S(2)}) copy-start(f32[256,128]{1,0:T(8,128)S(1)} %get-tuple-element.120.decay) | copy-start | bytes 393220
  35.7 12.5 %copy-start.6 = (f32[256,128]{1,0:T(8,128)}, f32[256,128]{1,0:T(8,128)S(1)}, u32[]{:S(2)}) copy-start(f32[256,128]{1,0:T(8,128)S(1)} %get-tuple-element.122.step) | copy-start | bytes 393220
  35.8 12.5 %copy-start.7 = (bf16[256,128]{1,0:T(8,128)(2,1)}, bf16[256,128]{1,0:T(8,128)(2,1)S(1)}, u32[]{:S(2)}) copy-start(bf16[256,128]{1,0:T(8,128)(2,1)S(1)} %get-tuple-element.119.c_main) | copy-start | bytes 196612
  35.8 12.5 %copy-start.9 = (f32[32,256]{1,0:T(8,128)}, f32[32,256]{1,0:T(8,128)S(1)}, u32[]{:S(2)}) copy-start(f32[32,256]{1,0:T(8,128)S(1)} %get-tuple-element.121.decay_t) | copy-start | bytes 98308
  35.8 12.5 %copy-start.10 = (f32[32,256]{1,0:T(8,128)}, f32[32,256]{1,0:T(8,128)S(1)}, u32[]{:S(2)}) copy-start(f32[32,256]{1,0:T(8,128)S(1)} %get-tuple-element.123.step_t) | copy-start | bytes 98308
  90.3 34.4 %all-to-all-start.2 = ((bf16[64,32,128]{2,1,0:T(8,128)(2,1)}), bf16[64,32,128]{2,1,0:T(8,128)(2,1)S(1)}, u32[]{:S(2)}, u32[]{:S(2)}) async-start(bf16[64,32,128]{2,1,0:T(8,128)(2,1)} %pack_third.1), calls=%async_computation.2 | async-start | bytes 1048576 | tf_op jit(solution)/shard_map/all_to_all | solution.py:368
  102.7 22.0 %copy-start.2 = (f32[2048]{0:T(1024)S(1)}, f32[2048]{0:T(1024)}, u32[]{:S(2)}) copy-start(f32[2048]{0:T(1024)} %param.28) | copy-start | bytes 24580
  110.8 1.0 copy-start.1
  124.7 5.1 %copy-start = (bf16[64,32,128]{2,1,0:T(8,128)(2,1)}, bf16[64,32,128]{2,1,0:T(8,128)(2,1)S(1)}, u32[]{:S(2)}) copy-start(bf16[64,32,128]{2,1,0:T(8,128)(2,1)S(1)} %all-to-all-done.2.state) | copy-start | bytes 1572868
  124.7 21.5 %copy-start.3 = (f32[2048,128]{1,0:T(8,128)S(1)}, f32[2048,128]{1,0:T(8,128)}, u32[]{:S(2)}) copy-start(f32[2048,128]{1,0:T(8,128)} %get-tuple-element.136.kept) | copy-start | bytes 3145732
  129.8 22.9 %all-to-all-start.3 = ((bf16[8,128,128]{2,1,0:T(8,128)(2,1)}), bf16[8,128,128]{2,1,0:T(8,128)(2,1)S(1)}, u32[]{:S(2)}, u32[]{:S(2)}) async-start(bf16[8,128,128]{2,1,0:T(8,128)(2,1)} %get-tuple-element.134), calls=%async_computation.3 | async-start | bytes 524288 | tf_op jit(solution)/shard_map/all_to_all | solution.py:368

commit v7 on v6

--- a/solution.py
+++ b/solution.py
@@ -73,7 +73,7 @@
 
     def body(j, carry):
         out[j, 0:24, :] = both[mine, j, 0:24, :]
-        out[j, 32:56, :] = first[codes[0, j], 0:24, :]
+        out[j, 32:48, :] = first[codes[0, j], 0:16, :]
         tile = first[codes[1, j], 24:32, :].astype(F32)
         line = jnp.where(codes[2, j] == 0, tile[0:1], tile[1:2])
         out[j, 24:32, :] = jnp.where(lines == 6, line, both[mine, j, 24:32, :].astype(F32)).astype(BF16)
@@ -88,6 +88,7 @@
     def body(j, carry):
         owner = codes[1, j]
         out[j, 0:24, :] = second[owner, 0:24, :]
+        out[j, 32:40, :] = first[codes[0, j], 16:24, :]
         rest = first[owner, 24:32, :].astype(F32)
         rest = jnp.where(codes[2, j] == 0, pltpu.roll(rest, 2, 0), rest)
         out[j, 24:32, :] = jnp.where(lines >= 6, rest, second[owner, 24:32, :].astype(F32)).astype(BF16)
@@ -317,7 +318,7 @@
     square = jnp.zeros((256, 128), F32)
     for block in range(8):
         at = slice(block * 256, block * 256 + 256)
-        old = state[block * 8 : block * 8 + 8].reshape(256, 128)
+        old = state[block * 8 : block * 8 + 8, 0:32, :].reshape(256, 128)
         inter = lax.dot_general(c_value, old, (((1,), (1,)), ((), ())), preferred_element_type=F32)
         copies[2 * block].wait()
         copies[2 * block + 1].wait()
@@ -347,7 +348,7 @@
 
 
 def update_kernel(state, fresh, kept, updated):
-    updated[0] = (fresh[...] + kept[...] * state[...].reshape(2048, 128).astype(F32)).astype(BF16)
+    updated[0] = (fresh[...] + kept[...] * state[:, 0:32, :].reshape(2048, 128).astype(F32)).astype(BF16)
 
 
 def up_kernel(parts, up, out):
@@ -357,7 +358,7 @@
     reduced = total.astype(BF16)
     halves = [reduced[:, 0:64], reduced[:, 64:128]]
     for col in range(8):
-        panel = up[col * 8 : col * 8 + 8, 48:56, :].astype(F32).reshape(64, 128).astype(BF16)
+        panel = up[col * 8 : col * 8 + 8, 32:40, :].astype(F32).reshape(64, 128).astype(BF16)
         at = slice(col * 128, col * 128 + 128)
         for half in range(2):
             value = jnp.dot(halves[half], panel, preferred_element_type=F32) * ADAPTER_SCALE
@@ -467,20 +468,20 @@
 
     sent2, codes = pl.pallas_call(
         pack_second,
-        out_shape=[packed((64, 56, 128), BF16), packed((8, 128), jnp.int32)],
+        out_shape=[packed((64, 48, 128), BF16), packed((8, 128), jnp.int32)],
         in_specs=[smem(), vmem(), pl.BlockSpec(memory_space=pl.ANY)],
         out_specs=[vmem(), smem()],
         scratch_shapes=[
             pltpu.VMEM((8, 128), jnp.int32), pltpu.VMEM((2, 64, 32, 128), BF16), pltpu.SemaphoreType.DMA((3,)),
         ],
-        compiler_params=params(52),
+        compiler_params=params(50),
         cost_estimate=cost(0, 3 << 20),
         name="pack_second",
     )(me, got1, states)
     got2 = exchange(sent2, "req")
     sent3 = pl.pallas_call(
         pack_third,
-        out_shape=packed((64, 32, 128), BF16),
+        out_shape=packed((64, 40, 128), BF16),
         in_specs=[smem(), vmem(), vmem()],
         out_specs=vmem(),
         compiler_params=params(52),
@@ -543,10 +544,10 @@
         out_shape=packed((256, 1024), BF16),
         in_specs=[vmem()] * 2,
         out_specs=vmem(),
-        compiler_params=params(),
+        compiler_params=params(52),
         cost_estimate=cost(1 << 26, 1 << 20),
         name="up",
-    )(parts, got2)
+    )(parts, got3)
     return normed, term, updated.reshape(1, 32, 64, 128)
 
 

time: 155 us -> 152 us (0.981)
  blocking collectives: 40.2 us -> 33.9 us
  waiting for transfers between devices: 27.3 us -> 29.7 us
    all_to_all x1, blocking collectives: 40.2 us -> 33.9 us  [exchange(): return lax.all_to_all(value, axis, split_axis=0, concat_axis=0, tiled=True)]
    all_to_all x3, waiting for transfers between devices: 27.3 us -> 29.7 us  [exchange(): return lax.all_to_all(value, axis, split_axis=0, concat_axis=0, tiled=True)]
  transfers between devices with their start and end apart: 3 -> 3, of which waited for: 3 -> 3; matrix products, arithmetic and copies ran while one was open for 0% -> 0% of each run, Pallas kernels for 14% -> 15%
where the time goes in v7:
time: 152 us
  starting transfers between devices  48.9 us (32%)
  Pallas kernels  35.1 us (23%)
  blocking collectives  33.9 us (22%)
  waiting for transfers between devices  29.7 us (20%)
  between operations  2.79 us (2%)
    all_to_all x3, starting transfers between devices, exchange(): return lax.all_to_all(value, axis, split_axis=0, concat_axis=0, tiled=True)  48.9 us
    all_to_all x1, blocking collectives, exchange(): return lax.all_to_all(value, axis, split_axis=0, concat_axis=0, tiled=True)  33.9 us
    all_to_all x3, waiting for transfers between devices, exchange(): return lax.all_to_all(value, axis, split_axis=0, concat_axis=0, tiled=True)  29.7 us
    pallas_call x1, Pallas kernels, scan(): pl.pallas_call(scan_first_kernel if first else scan_kernel, out_shape=sca...  12 us
    pallas_call x1, Pallas kernels, per_device(): pl.pallas_call(early_rows, out_shape=[packed((256, 2304), F32), packed((2...  8.1 us
    pallas_call x1, Pallas kernels, per_device(): pl.pallas_call(state_kernel, out_shape=[packed((256, 2048), BF16), packed...  5.05 us
  transfers between devices with their start and end apart: 3, of which 3 were waited for; matrix products, arithmetic and copies ran while one was open for 0% of the time, Pallas kernels for 15%

profile of v7, /device:TPU:1, one launch (start us, length us, event | category | flops | bytes accessed | tf_op | source)
XLA Modules:
  0.0 151.5 jit_solution(7362212253726099996)
XLA Ops:
  2.6 0.0 copy-start.5
  2.6 0.0 copy-start.6
  2.6 0.0 copy-start.7
  2.6 0.0 copy-start.9
  2.7 0.0 copy-start.10
  2.7 0.0 copy-start.11
  2.7 0.0 copy-start.12
  2.7 0.0 copy-start.13
  2.7 2.1 %pack_first.1 = bf16[64,32,128]{2,1,0:T(8,128)(2,1)} custom-call(s32[1]{0:T(128)S(6)} %copy.61.tenant, s32[64]{0:T(128)} %table.1, s32[1]{0:T(128)S(6)} %copy.62.owner, s32[1]{0:T(128)S(6)} %copy.63.slot, bf16[64,2048]{1,0:T(8,128)(2,1)} %bitcast.22, bf16[1,64,1024]{2,1,0:T(8,128)(2,1)} %up.2, bf16[3,2,2048]{2,1,0:T(2,128)(2,1)} %bitcast.23, ...), custom_call_target="tpu_custom_call" | custom-call | bytes 2097152 | tf_op jit(solution)/shard_map/pack_first/pallas_call | solution.py:421
  4.8 19.3 %all-to-all-start = ((bf16[64,32,128]{2,1,0:T(8,128)(2,1)}), bf16[64,32,128]{2,1,0:T(8,128)(2,1)S(1)}, u32[]{:S(2)}, u32[]{:S(2)}) async-start(bf16[64,32,128]{2,1,0:T(8,128)(2,1)} %pack_first.1), calls=%async_computation | async-start | bytes 1048576 | tf_op jit(solution)/shard_map/all_to_all | solution.py:369
  24.1 0.0 copy-done.5
  24.1 0.0 copy-done.6
  24.2 0.0 copy-done.7
  24.2 0.0 copy-done.9
  24.2 0.0 copy-done.10
  24.2 0.0 copy-start.2
  24.2 12.0 %scan_late.1 = (f32[256,2048]{1,0:T(8,128)}, f32[256,2048]{1,0:T(8,128)}, f32[2048,128]{1,0:T(8,128)}, f32[2048,128]{1,0:T(8,128)}, bf16[256,128]{1,0:T(8,128)(2...) custom-call(s32[1]{0:T(128)} %bitcast.11.flag, ...), custom_call_target="tpu_custom_call", output_to_operand_aliasing={{0}: (9, {}), {1}: (10, {}), {2}: (11, {}), {3}: (12, {}), ... | custom-call | flops 2147483648 | bytes 10485760 | tf_op jit(solution)/shard_map/scan_late/pallas_call | solution.py:442
  36.3 9.7 %all-to-all-done.first = bf16[64,32,128]{2,1,0:T(8,128)(2,1)S(1)} async-done(((bf16[64,32,128]{2,1,0:T(8,128)(2,1)}), bf16[64,32,128]{2,1,0:T(8,128)(2,1)S(1)}, u32[]{:S(2)}, u32[]{:S(2)}) %all-to-all-start) | async-done | bytes 524320 | tf_op jit(solution)/shard_map/all_to_all | solution.py:369
  46.0 2.1 %pack_second.1 = (bf16[64,48,128]{2,1,0:T(8,128)(2,1)S(1)}, s32[8,128]{1,0:T(8,128)S(1)}) custom-call(s32[1]{0:T(128)} %bitcast.10.me, bf16[64,32,128]{2,1,0:T(8,128)(2,1)S(1)} %all-to-all-done.first, bf16[2,64,32,128]{3,2,1,0:T(8,128)(2,1)S(1)} %bitcast.16), custom_call_target="tpu_custom_call" | custom-call | bytes 3145728 | tf_op jit(solution)/shard_map/pack_second/pallas_call | solution.py:469
  48.1 33.9 %all_to_all.20.second.convs.panels = bf16[64,48,128]{2,1,0:T(8,128)(2,1)S(1)} all-to-all(bf16[64,48,128]{2,1,0:T(8,128)(2,1)S(1)} %get-tuple-element.116), channel_id=1, replica_groups=mesh['req'=64,'head'=8] {'req'}, dimensions={0} | all-to-all | bytes 1572864 | tf_op jit(solution)/shard_map/all_to_all | solution.py:369
  82.0 1.9 %pack_third.1 = bf16[64,40,128]{2,1,0:T(8,128)(2,1)} custom-call(s32[8,128]{1,0:T(8,128)S(1)} %get-tuple-element.115.codes, bf16[64,32,128]{2,1,0:T(8,128)(2,1)S(1)} %all-to-all-done.first, bf16[64,48,128]{2,1,0:T(8,128)(2,1)S(1)} %all_to_all.20.second.convs.panels), custom_call_target="tpu_custom_call" | custom-call | bytes 1048576 | tf_op jit(solution)/shard_map/pack_third/pallas_call | solution.py:482
  83.9 11.0 %all-to-all-start.2 = ((bf16[64,40,128]{2,1,0:T(8,128)(2,1)}), bf16[64,40,128]{2,1,0:T(8,128)(2,1)S(1)}, u32[]{:S(2)}, u32[]{:S(2)}) async-start(bf16[64,40,128]{2,1,0:T(8,128)(2,1)} %pack_third.1), calls=%async_computation.2 | async-start | bytes 1310720 | tf_op jit(solution)/shard_map/all_to_all | solution.py:369
  94.9 0.0 copy-start.4
  95.0 8.1 %early_rows.1 = (f32[256,2304]{1,0:T(8,128)}, f32[2048,128]{1,0:T(8,128)S(1)}) custom-call(bf16[256,2048]{1,0:T(8,128)(2,1)S(1)} %copy-done.5, bf16[256,2,128]{2,1,0:T(2,128)(2,1)S(1)} %bitcast.20, f32[4,2048]{1,0:T(4,128)S(1)} %copy-done.7, f32[4,2,128]{2,1,0:T(2,128)S(1)} %bitcast.28, bf16[64,48,128]{2,1,0:T(8,128)(2,1)S(1)} %all_to_all.20.second.convs.panels, ...), custom_call_target="tpu_custom_call" | custom-call | flops 536870912 | bytes 8388608 | tf_op jit(solution)/shard_map/early_rows/pallas_call | solution.py:494
  103.1 1.0 copy-done.3
  104.1 16.1 %all-to-all-done.2.state.up = bf16[64,40,128]{2,1,0:T(8,128)(2,1)S(1)} async-done(((bf16[64,40,128]{2,1,0:T(8,128)(2,1)}), bf16[64,40,128]{2,1,0:T(8,128)(2,1)S(1)}, u32[]{:S(2)}, u32[]{:S(2)}) %all-to-all-start.2) | async-done | bytes 655392 | tf_op jit(solution)/shard_map/all_to_all | solution.py:369
  120.2 0.0 copy-done.4
  120.2 5.1 %state.1 = (bf16[256,2048]{1,0:T(8,128)(2,1)}, bf16[8,128,128]{2,1,0:T(8,128)(2,1)}) custom-call(bf16[64,40,128]{2,1,0:T(8,128)(2,1)S(1)} %all-to-all-done.2.state.up, f32[256,2304]{1,0:T(8,128)} %get-tuple-element.129.part_far, f32[256,2048]{1,0:T(8,128)} %get-tuple-element.130.gate_far, f32[1,2048]{1,0:T(1,128)S(1)} %bitcast.17, ...), custom_call_target="tpu_custom_call" | custom-call | flops 268435456 | bytes 8388608 | tf_op jit(solution)/shard_map/state/pallas_call | solution.py:519
  125.2 18.6 %all-to-all-start.3 = ((bf16[8,128,128]{2,1,0:T(8,128)(2,1)}), bf16[8,128,128]{2,1,0:T(8,128)(2,1)S(1)}, u32[]{:S(2)}, u32[]{:S(2)}) async-start(bf16[8,128,128]{2,1,0:T(8,128)(2,1)} %get-tuple-element.134), calls=%async_computation.3 | async-start | bytes 524288 | tf_op jit(solution)/shard_map/all_to_all | solution.py:369
  143.9 2.7 %update.1 = bf16[1,2048,128]{2,1,0:T(8,128)(2,1)} custom-call(bf16[64,40,128]{2,1,0:T(8,128)(2,1)} %copy-done, f32[2048,128]{1,0:T(8,128)} %copy-done.3, f32[2048,128]{1,0:T(8,128)} %get-tuple-element.136.kept), custom_call_target="tpu_custom_call" | custom-call | flops 1048576 | bytes 3145728 | tf_op jit(solution)/shard_map/update/pallas_call | solution.py:532
  146.5 3.9 %all-to-all-done.3.parts = bf16[8,128,128]{2,1,0:T(8,128)(2,1)S(1)} async-done(((bf16[8,128,128]{2,1,0:T(8,128)(2,1)}), bf16[8,128,128]{2,1,0:T(8,128)(2,1)S(1)}, u32[]{:S(2)}, u32[]{:S(2)}) %all-to-all-start.3) | async-done | bytes 262176 | tf_op jit(solution)/shard_map/all_to_all | solution.py:369
  150.4 1.1 up.3
  (13 shorter events, 0.0 us)
Async XLA Ops:
  2.6 21.5 %copy-start.5 = (bf16[256,2048]{1,0:T(8,128)(2,1)S(1)}, bf16[256,2048]{1,0:T(8,128)(2,1)}, u32[]{:S(2)}) copy-start(bf16[256,2048]{1,0:T(8,128)(2,1)} %x.3) | copy-start | bytes 3145732
  2.6 21.5 %copy-start.6 = (bf16[256,1,2,128]{3,2,1,0:T(2,128)(2,1)S(1)}, bf16[256,1,2,128]{3,2,1,0:T(2,128)(2,1)}, u32[]{:S(2)}) copy-start(bf16[256,1,2,128]{3,2,1,0:T(2,128)(2,1)} %param.21) | copy-start | bytes 393220
  2.6 21.5 %copy-start.7 = (f32[4,2048]{1,0:T(4,128)S(1)}, f32[4,2048]{1,0:T(4,128)}, u32[]{:S(2)}) copy-start(f32[4,2048]{1,0:T(4,128)} %taps.3) | copy-start | bytes 98308
  2.6 21.5 %copy-start.9 = (bf16[256,32]{0,1:T(8,128)(2,1)S(1)}, bf16[256,32]{0,1:T(8,128)(2,1)}, u32[]{:S(2)}) copy-start(bf16[256,32]{0,1:T(8,128)(2,1)} %param.22) | copy-start | bytes 49156
  2.7 21.5 %copy-start.10 = (f32[4,1,2,128]{3,2,1,0:T(2,128)S(1)}, f32[4,1,2,128]{3,2,1,0:T(2,128)}, u32[]{:S(2)}) copy-start(f32[4,1,2,128]{3,2,1,0:T(2,128)} %param.24) | copy-start | bytes 12292
  2.7 21.5 %copy-start.11 = (f32[32]{0:T(128)S(1)}, f32[32]{0:T(128)}, u32[]{:S(2)}) copy-start(f32[32]{0:T(128)} %param.27) | copy-start | bytes 388
  2.7 21.5 %copy-start.12 = (f32[32]{0:T(128)S(1)}, f32[32]{0:T(128)}, u32[]{:S(2)}) copy-start(f32[32]{0:T(128)} %param.25) | copy-start | bytes 388
  2.7 21.5 %copy-start.13 = (f32[32]{0:T(128)S(1)}, f32[32]{0:T(128)}, u32[]{:S(2)}) copy-start(f32[32]{0:T(128)} %param.26) | copy-start | bytes 388
  4.8 41.2 %all-to-all-start = ((bf16[64,32,128]{2,1,0:T(8,128)(2,1)}), bf16[64,32,128]{2,1,0:T(8,128)(2,1)S(1)}, u32[]{:S(2)}, u32[]{:S(2)}) async-start(bf16[64,32,128]{2,1,0:T(8,128)(2,1)} %pack_first.1), calls=%async_computation | async-start | bytes 1048576 | tf_op jit(solution)/shard_map/all_to_all | solution.py:369
  24.2 21.8 %copy-start.2 = (bf16[2,32,64,128]{3,2,1,0:T(8,128)(2,1)S(1)}, bf16[2,32,64,128]{3,2,1,0:T(8,128)(2,1)}, u32[]{:S(2)}) copy-start(bf16[2,32,64,128]{3,2,1,0:T(8,128)(2,1)} %param.35) | copy-start | bytes 3145732
  36.3 47.7 %copy-start.8 = (f32[32,256]{1,0:T(8,128)}, f32[32,256]{1,0:T(8,128)S(1)}, u32[]{:S(2)}) copy-start(f32[32,256]{1,0:T(8,128)S(1)} %get-tuple-element.123.step_t) | copy-start | bytes 98308
  83.9 36.2 %all-to-all-start.2 = ((bf16[64,40,128]{2,1,0:T(8,128)(2,1)}), bf16[64,40,128]{2,1,0:T(8,128)(2,1)S(1)}, u32[]{:S(2)}, u32[]{:S(2)}) async-start(bf16[64,40,128]{2,1,0:T(8,128)(2,1)} %pack_third.1), calls=%async_computation.2 | async-start | bytes 1310720 | tf_op jit(solution)/shard_map/all_to_all | solution.py:369
  94.9 25.2 %copy-start.4 = (f32[2048]{0:T(1024)S(1)}, f32[2048]{0:T(1024)}, u32[]{:S(2)}) copy-start(f32[2048]{0:T(1024)} %param.28) | copy-start | bytes 24580
  103.0 1.0 copy-start.3
  120.1 5.1 %copy-start = (bf16[64,40,128]{2,1,0:T(8,128)(2,1)}, bf16[64,40,128]{2,1,0:T(8,128)(2,1)S(1)}, u32[]{:S(2)}) copy-start(bf16[64,40,128]{2,1,0:T(8,128)(2,1)S(1)} %all-to-all-done.2.state.up) | copy-start | bytes 1966084
  125.2 25.2 %copy-start.1 = (bf16[64,40,128]{2,1,0:T(8,128)(2,1)S(1)}, bf16[64,40,128]{2,1,0:T(8,128)(2,1)}, u32[]{:S(2)}) copy-start(bf16[64,40,128]{2,1,0:T(8,128)(2,1)} %copy-done) | copy-start | bytes 1966084
  125.2 25.1 %all-to-all-start.3 = ((bf16[8,128,128]{2,1,0:T(8,128)(2,1)}), bf16[8,128,128]{2,1,0:T(8,128)(2,1)S(1)}, u32[]{:S(2)}, u32[]{:S(2)}) async-start(bf16[8,128,128]{2,1,0:T(8,128)(2,1)} %get-tuple-element.134), calls=%async_computation.3 | async-start | bytes 524288 | tf_op jit(solution)/shard_map/all_to_all | solution.py:369
